TPU v7x, 128 devices: a whole 4x4x4 slice. The times are simulated.
128 devices in a mesh: expert: 16 (over y, z_lo, core), shard: 8 (over z_hi, x).
Axes of the slice: x: 4, y: 4, z: 4 (z_hi: 2, z_lo: 2; z = z_hi * 2 + z_lo), core: 2. Of those that a mesh axis runs over, the one named last changes fastest.
Arguments:
- tokens: bfloat16 [16384, 2048], P(('expert', 'shard')), may hold values from -6 to 6
- expert_ids: int32 [16384, 4], P(('expert', 'shard')), may hold values from 0 to 15, all different within a row; in each aligned block of 128 rows (0 to 127, 128 to 255, ...) at most 48 rows name the same one
- route_weights: float32 [16384, 4], P(('expert', 'shard')), may hold values from 0.1 to 1
- partner: int32 [16], replicated, may hold values from 0 to 15, as said below
- w_in: bfloat16 [16, 2, 2048, 768], P('expert', None, 'shard'), may hold values from -0.125 to 0.125
- w_down: bfloat16 [16, 768, 2048], P('expert', None, 'shard'), may hold values from -0.21875 to 0.21875
- m_in: float32 [16, 2, 2048, 768], P('expert', None, 'shard'), may hold values from -6 to 6
- v_in: float32 [16, 2, 2048, 768], P('expert', None, 'shard'), may hold values from 0.01 to 1
- m_down: float32 [16, 768, 2048], P('expert', None, 'shard'), may hold values from -6 to 6
- v_down: float32 [16, 768, 2048], P('expert', None, 'shard'), may hold values from 0.01 to 1
- cotangent: bfloat16 [16384, 2048], P(('expert', 'shard')), may hold values from -6 to 6
Outputs:
- mixed: bfloat16 [16384, 2048], P(('expert', 'shard'))
- token_grad: bfloat16 [16384, 2048], P(('expert', 'shard'))
- new_w_in: bfloat16 [16, 2, 2048, 768], P('expert', None, 'shard')
- new_w_down: bfloat16 [16, 768, 2048], P('expert', None, 'shard')
- new_m_in: float32 [16, 2, 2048, 768], P('expert', None, 'shard')
- new_v_in: float32 [16, 2, 2048, 768], P('expert', None, 'shard')
- new_m_down: float32 [16, 768, 2048], P('expert', None, 'shard')
- new_v_down: float32 [16, 768, 2048], P('expert', None, 'shard')
Inputs may be any that keep to these rules, and one draw needn't show every extreme that they name: `expert_ids`: within the rows of one device no expert is named more than 48 times, a bound that some block reaches. partner[g] is g or (g + 8) mod 16, and partner[partner[g]] = g; partner[0] is 8.
All inputs are finite; a program needn't handle non-finite values.
Results may differ from a plain program's by a relative error of at most 0.024.
Values may be sent and summed in bfloat16 or wider, within the bound.
A program may use at most 128 MiB of HBM per device.

v0:
```python
import jax
import jax.numpy as jnp
from jax import lax
from jax.sharding import PartitionSpec as P

beta_first = 0.9
beta_second = 0.999
learn_rate = 0.01
adam_eps = 1e-08
bias_first = 0.9999734386011124
bias_second = 0.09520785288629038


def shifted(block, axis, distance):
    devices = range(lax.axis_size(axis))
    route = [((i - distance) % len(devices), i) for i in devices]
    return lax.ppermute(block, axis, route)


def silu_parts(gate_pre):
    sigmoid_value = jax.nn.sigmoid(gate_pre)
    silu_value = gate_pre * sigmoid_value
    slope = sigmoid_value * (1.0 + gate_pre * (1.0 - sigmoid_value))
    return (silu_value, slope)


def adam_update(weight, first, second, grad):
    first_new = beta_first * first + (1.0 - beta_first) * grad
    second_new = beta_second * second + (1.0 - beta_second) * grad * grad
    update = learn_rate * (first_new / bias_first) / (jnp.sqrt(second_new / bias_second) + adam_eps)
    return ((weight.astype(jnp.float32) - update).astype(jnp.bfloat16), first_new, second_new)


def route_table(expert_ids, dest_rows, groups, capacity):
    entry_count = expert_ids.shape[0] * expert_ids.shape[1]
    flat_ids = expert_ids.reshape(entry_count)
    onehot = (flat_ids[:, None] == jnp.arange(groups, dtype=jnp.int32)[None, :]).astype(jnp.int32)
    before = jnp.cumsum(onehot, axis=0) - onehot
    slot_index = jnp.sum(before * onehot, axis=1)
    position = dest_rows.reshape(entry_count) * capacity + slot_index
    entry_index = jnp.arange(entry_count, dtype=jnp.int32)
    filler = jnp.full((groups * capacity,), -1, jnp.int32).at[position].set(entry_index)
    return (position, filler)


def fill_rows(source_rows, filler, groups, capacity):
    picked = jnp.take(source_rows, jnp.maximum(filler, 0), axis=0)
    kept = jnp.where((filler >= 0)[:, None], picked, jnp.zeros_like(picked))
    return kept.reshape(groups, capacity, source_rows.shape[1])


def contract_rows(left, right):
    return lax.dot_general(
        left, right, (((0,), (0,)), ((), ())), preferred_element_type=jnp.float32
    )


def contract_cols(left, right):
    return lax.dot_general(
        left, right, (((1,), (1,)), ((), ())), preferred_element_type=jnp.float32
    )


def body(
    tokens, expert_ids, route_weights, partner, w_in, w_down, m_in, v_in, m_down, v_down, cotangent
):
    groups = lax.axis_size("expert")
    halfway = groups // 2
    tok_rows = tokens.shape[0]
    width = tokens.shape[1]
    top_count = expert_ids.shape[1]
    capacity = 3 * tok_rows * top_count // (2 * groups)
    row_index = lax.axis_index("expert")
    expert_range = jnp.arange(groups, dtype=jnp.int32)
    own_partner = jnp.sum(jnp.where(expert_range == row_index, partner, 0))
    take_other = own_partner != row_index
    in_full, down_full = (
        lax.all_gather(w_in, "shard", axis=2, tiled=True),
        lax.all_gather(w_down, "shard", axis=2, tiled=True),
    )
    gate_weight = in_full[0, 0]
    up_weight = in_full[0, 1]
    down_weight = down_full[0]
    hidden_width = gate_weight.shape[1]
    position, filler = route_table(expert_ids, expert_ids, groups, capacity)
    token_fill = jnp.where(filler >= 0, filler // top_count, -1)
    send_rows = fill_rows(tokens, token_fill, groups, capacity)
    arrived = lax.all_to_all(send_rows, "expert", split_axis=0, concat_axis=0, tiled=True)
    rows_x = arrived.reshape(groups * capacity, width)
    own_moments = (m_in, v_in, m_down, v_down)
    gate_pre = jnp.dot(rows_x, gate_weight, preferred_element_type=jnp.float32)
    up_pre = jnp.dot(rows_x, up_weight, preferred_element_type=jnp.float32)
    silu_value, slope = silu_parts(gate_pre)
    hidden = (silu_value * up_pre).astype(jnp.bfloat16)
    expert_out = jnp.dot(hidden, down_weight, preferred_element_type=jnp.float32).astype(
        jnp.bfloat16
    )
    returned = lax.all_to_all(
        expert_out.reshape(groups, capacity, width),
        "expert",
        split_axis=0,
        concat_axis=0,
        tiled=True,
    )
    per_entry = jnp.take(returned.reshape(groups * capacity, width), position, axis=0).reshape(
        tok_rows, top_count, width
    )
    mixed = jnp.sum(route_weights[:, :, None] * per_entry.astype(jnp.float32), axis=1).astype(
        jnp.bfloat16
    )
    scaled = (route_weights[:, :, None] * cotangent[:, None, :].astype(jnp.float32)).astype(
        jnp.bfloat16
    )
    send_grads = fill_rows(scaled.reshape(tok_rows * top_count, width), filler, groups, capacity)
    dout_rows = lax.all_to_all(
        send_grads, "expert", split_axis=0, concat_axis=0, tiled=True
    ).reshape(groups * capacity, width)
    grad_hidden = contract_cols(dout_rows, down_weight)
    grad_gate = (grad_hidden * up_pre * slope).astype(jnp.bfloat16)
    grad_up = (grad_hidden * silu_value).astype(jnp.bfloat16)
    entry_grads = (
        contract_cols(grad_gate, gate_weight) + contract_cols(grad_up, up_weight)
    ).astype(jnp.bfloat16)
    back_rows = lax.all_to_all(
        entry_grads.reshape(groups, capacity, width),
        "expert",
        split_axis=0,
        concat_axis=0,
        tiled=True,
    )
    per_back = jnp.take(back_rows.reshape(groups * capacity, width), position, axis=0).reshape(
        tok_rows, top_count, width
    )
    token_grad = jnp.sum(per_back.astype(jnp.float32), axis=1).astype(jnp.bfloat16)
    grad_both = jnp.concatenate([grad_gate, grad_up], axis=1)
    share_rows = width // lax.axis_size("shard")
    shares = lax.psum_scatter(
        jnp.concatenate(
            [contract_rows(rows_x, grad_both), contract_rows(dout_rows, hidden)], axis=1
        ).astype(jnp.bfloat16),
        "shard",
        scatter_dimension=0,
        tiled=True,
    ).astype(jnp.float32)
    grad_in = jnp.transpose(
        shares[:, : 2 * hidden_width].reshape(share_rows, 2, hidden_width), (1, 0, 2)
    )[None]
    grad_down = jnp.transpose(shares[:, 2 * hidden_width :])[None]
    new_in, first_in, second_in = adam_update(w_in, own_moments[0], own_moments[1], grad_in)
    new_down, first_down, second_down = adam_update(
        w_down, own_moments[2], own_moments[3], grad_down
    )
    moved_weights = shifted((new_in, new_down), "expert", halfway)
    moved_states = (
        shifted(first_in.astype(jnp.bfloat16), "expert", halfway).astype(first_in.dtype),
        shifted(second_in.astype(jnp.bfloat16), "expert", halfway).astype(second_in.dtype),
        shifted(first_down.astype(jnp.bfloat16), "expert", halfway).astype(first_down.dtype),
        shifted(second_down.astype(jnp.bfloat16), "expert", halfway).astype(second_down.dtype),
    )
    placed_weights = tuple(
        (
            jnp.where(take_other, moved, owned)
            for moved, owned in zip(moved_weights, (new_in, new_down))
        )
    )
    placed_moments = tuple(
        (
            jnp.where(take_other, moved, owned)
            for moved, owned in zip(moved_states, (first_in, second_in, first_down, second_down))
        )
    )
    return (
        mixed,
        token_grad,
        placed_weights[0],
        placed_weights[1],
        placed_moments[0],
        placed_moments[1],
        placed_moments[2],
        placed_moments[3],
    )


def solution(mesh):
    placed = (
        P(("expert", "shard"), None),
        P(("expert", "shard"), None),
        P(("expert", "shard"), None),
        P(),
        P("expert", None, "shard", None),
        P("expert", None, "shard"),
        P("expert", None, "shard", None),
        P("expert", None, "shard", None),
        P("expert", None, "shard"),
        P("expert", None, "shard"),
        P(("expert", "shard"), None),
    )
    return jax.shard_map(
        body,
        mesh=mesh,
        in_specs=placed,
        out_specs=(
            P(("expert", "shard"), None),
            P(("expert", "shard"), None),
            P("expert", None, "shard", None),
            P("expert", None, "shard"),
            P("expert", None, "shard", None),
            P("expert", None, "shard", None),
            P("expert", None, "shard"),
            P("expert", None, "shard"),
        ),
        check_vma=False,
    )
```

profile of v0, /device:TPU:1, one launch (start us, length us, event | category | flops | bytes accessed | tf_op | source)
XLA Modules:
  0.0 548.0 jit_solution(6786216978534705951)
XLA Ops:
  11.4 2.4 scatter_custom_fusion
  14.1 4.3 gather_fusion
  18.4 3.3 select_select_fusion.1
  21.7 7.5 %all-to-all-start = ((bf16[16,48,2048]{2,1,0:T(8,128)(2,1)}), bf16[16,48,2048]{2,1,0:T(8,128)(2,1)}, u32[]{:S(2)}, u32[]{:S(2)}) async-start(bf16[16,48,2048]{2,1,0:T(8,128)(2,1)} %select_select_fusion.1), calls=%async_computation | async-start | bytes 6291456 | tf_op jit(solution)/shard_map/all_to_all | solution.py:88
  30.0 3.0 mul.162
  33.0 5.3 mul.163
  38.6 2.5 multiply_convert_fusion
  41.1 4.3 gather_fusion.1
  45.4 3.3 select_select_fusion
  48.8 20.4 %all-to-all-done = bf16[16,48,2048]{2,1,0:T(8,128)(2,1)} async-done(((bf16[16,48,2048]{2,1,0:T(8,128)(2,1)}), bf16[16,48,2048]{2,1,0:T(8,128)(2,1)}, u32[]{:S(2)}, u32[]{:S(2)}) %all-to-all-start) | async-done | bytes 3145760 | tf_op jit(solution)/shard_map/all_to_all | solution.py:88
  69.2 8.0 %all-to-all-start.2 = ((bf16[16,48,2048]{2,1,0:T(8,128)(2,1)}), bf16[16,48,2048]{2,1,0:T(8,128)(2,1)S(1)}, u32[]{:S(2)}, u32[]{:S(2)}) async-start(bf16[16,48,2048]{2,1,0:T(8,128)(2,1)} %select_select_fusion), calls=%async_computation.2 | async-start | bytes 6291456 | tf_op jit(solution)/shard_map/all_to_all | solution.py:115
  77.5 81.1 %all-gather.3.cloned.1.call-done = bf16[1,2,2048,768]{3,2,1,0:T(8,128)(2,1)} async-done(((bf16[1,2,256,768]{3,2,1,0:T(8,128)(2,1)}), bf16[1,2,2048,768]{3,2,1,0:T(8,128)(2,1)}) %all-gather.3.cloned.1.call-update) | async-done | bytes 6291472 | tf_op jit(solution)/shard_map/all_gather | solution.py:78
  158.6 7.0 %fusion.4 = f32[768,768]{0,1:T(8,128)} fusion(bf16[768,2048]{1,0:T(8,128)(2,1)} %bitcast.4, bf16[1,2,2048,768]{3,2,1,0:T(8,128)(2,1)} %all-gather.3.cloned.1.call-done), kind=kOutput, calls=%fused_computation.20 | convolution fusion | flops 2415919104 | bytes 8650752 | tf_op jit(solution)/shard_map/dot_general | solution.py:91
  165.6 6.0 %fusion.5 = f32[768,768]{0,1:T(8,128)} fusion(bf16[768,2048]{1,0:T(8,128)(2,1)} %bitcast.4, bf16[1,2,2048,768]{3,2,1,0:T(8,128)(2,1)S(1)} %copy-done.15), kind=kOutput, calls=%fused_computation.21 | convolution fusion | flops 2415919104 | bytes 8650752 | tf_op jit(solution)/shard_map/dot_general | solution.py:92
  171.7 54.2 %all-gather.5.cloned.1.call-done = bf16[1,768,2048]{2,1,0:T(8,128)(2,1)} async-done(((bf16[1,768,256]{2,1,0:T(8,128)(2,1)}), bf16[1,768,2048]{2,1,0:T(8,128)(2,1)}) %all-gather.5.cloned.1.call-update) | async-done | bytes 3145744 | tf_op jit(solution)/shard_map/all_gather | solution.py:79
  225.9 6.7 %multiply_convert_fusion.1 = (bf16[768,768]{0,1:T(8,128)(2,1)S(1)}, bf16[768,768]{0,1:T(8,128)(2,1)S(1)}, bf16[768,768]{0,1:T(8,128)(2,1)S(1)}) fusion(f32[768,768]{0,1:T(8,128)} %fusion.4, f32[768,768]{0,1:T(8,128)} %fusion.5, bf16[768,2048]{1,0:T(8,128)(2,1)S(1)} %bitcast.130, bf16[1,768,2048]{2,1,0:T(8,128)(2,1)} %all-gather.5.cloned.1.call-done), kind=kOutput, calls=%fused_computation.26 | convolution fusion | flops 2424766464 | bytes 14548992 | tf_op jit(solution)/shard_map/dot_general | solution.py:59
  232.6 3.3 convolution_convert_fusion.1
  236.0 8.3 %convolution_convert_fusion = bf16[2048,1536]{0,1:T(8,128)(2,1)S(1)} fusion(bf16[768,2048]{1,0:T(8,128)(2,1)} %bitcast.4, bf16[768,768]{0,1:T(8,128)(2,1)S(1)} %get-tuple-element.11, bf16[768,768]{0,1:T(8,128)(2,1)S(1)} %get-tuple-element.12), kind=kOutput, calls=%fused_computation.6 | convolution fusion | flops 4839702528 | bytes 11796480 | tf_op jit(solution)/shard_map/dot_general | solution.py:53
  244.3 11.5 %pad_maximum_fusion = bf16[2048,2304]{0,1:T(8,128)(2,1)} fusion(bf16[2048,768]{0,1:T(8,128)(2,1)S(1)} %convolution_convert_fusion.1, bf16[2048,1536]{0,1:T(8,128)(2,1)S(1)} %convolution_convert_fusion), kind=kLoop, calls=%fused_computation.5 | loop fusion | flops 18874368 | bytes 18874368 | tf_op jit(solution)/shard_map/concatenate | solution.py:138
  255.8 5.1 fusion.3
  260.9 4.1 add_convert_fusion
  265.0 6.2 %all-to-all-start.3 = ((bf16[16,48,2048]{2,1,0:T(8,128)(2,1)}), bf16[16,48,2048]{2,1,0:T(8,128)(2,1)S(1)}, u32[]{:S(2)}, u32[]{:S(2)}) async-start(bf16[16,48,2048]{2,1,0:T(8,128)(2,1)} %bitcast.132), calls=%async_computation.3 | async-start | bytes 6291456 | tf_op jit(solution)/shard_map/all_to_all | solution.py:124
  271.3 6.5 %convolution_convert_fusion.2 = bf16[768,2048]{1,0:T(8,128)(2,1)} fusion(bf16[768,768]{0,1:T(8,128)(2,1)} %copy-done.18, bf16[1,768,2048]{2,1,0:T(8,128)(2,1)} %all-gather.5.cloned.1.call-done), kind=kOutput, calls=%fused_computation.11 | convolution fusion | flops 2417491968 | bytes 7471104 | tf_op jit(solution)/shard_map/dot_general | solution.py:95
  277.8 35.3 %all-to-all-done.3 = bf16[16,48,2048]{2,1,0:T(8,128)(2,1)S(1)} async-done(((bf16[16,48,2048]{2,1,0:T(8,128)(2,1)}), bf16[16,48,2048]{2,1,0:T(8,128)(2,1)S(1)}, u32[]{:S(2)}, u32[]{:S(2)}) %all-to-all-start.3) | async-done | bytes 3145760 | tf_op jit(solution)/shard_map/all_to_all | solution.py:124
  313.1 6.0 %all-to-all-start.1 = ((bf16[16,48,2048]{2,1,0:T(8,128)(2,1)}), bf16[16,48,2048]{2,1,0:T(8,128)(2,1)}, u32[]{:S(2)}, u32[]{:S(2)}) async-start(bf16[16,48,2048]{2,1,0:T(8,128)(2,1)} %bitcast.129), calls=%async_computation.1 | async-start | bytes 6291456 | tf_op jit(solution)/shard_map/all_to_all | solution.py:98
  320.4 3.3 gather_fusion.3
  323.7 39.6 %all-to-all-done.1 = bf16[16,48,2048]{2,1,0:T(8,128)(2,1)} async-done(((bf16[16,48,2048]{2,1,0:T(8,128)(2,1)}), bf16[16,48,2048]{2,1,0:T(8,128)(2,1)}, u32[]{:S(2)}, u32[]{:S(2)}) %all-to-all-start.1) | async-done | bytes 3145760 | tf_op jit(solution)/shard_map/all_to_all | solution.py:98
  363.3 7.5 %gather_fusion.2 = bf16[512,2048]{1,0:T(8,128)(2,1)} fusion(bf16[768,2048]{1,0:T(8,128)(2,1)} %bitcast.9, s32[1024]{0:T(1024)S(1)} %pad_clamp_fusion.1), kind=kCustom, calls=%fused_computation.clone | custom fusion | bytes 4196352 | tf_op jit(solution)/shard_map/jit(_take)/gather | solution.py:105
  370.8 78.3 %reduce-scatter.2.cloned.1.call-done = bf16[256,2304]{0,1:T(8,128)(2,1)} async-done(((bf16[2048,2304]{0,1:T(8,128)(2,1)}), bf16[256,2304]{0,1:T(8,128)(2,1)}) %reduce-scatter.2.cloned.1.call-update) | async-done | bytes 1179664 | tf_op jit(solution)/shard_map/reduce_scatter | solution.py:137
  449.2 2.4 slice.35
  451.6 1.9 copy.27
  453.5 2.7 fusion.28
  456.1 2.7 collective-permute-start.3
  460.9 3.1 broadcast_select_fusion
  464.0 5.2 reshape.151
  469.3 15.1 %collective-permute-done.5 = bf16[1,768,256]{2,1,0:T(8,128)(2,1)} collective-permute-done((bf16[1,768,256]{2,1,0:T(8,128)(2,1)S(1)}, bf16[1,768,256]{2,1,0:T(8,128)(2,1)}, u32[]{:S(2)}, u32[]{:S(2)}) %collective-permute-start.5) | collective-permute-done | bytes 393248 | tf_op jit(solution)/shard_map/ppermute | solution.py:17
  484.3 3.2 convert_select_fusion.2
  487.5 2.7 collective-permute-start.1
  490.5 4.0 convert_select_fusion
  494.5 2.9 collective-permute-start
  497.4 4.0 multiply_reduce_fusion
  501.4 4.1 reshape.149
  505.5 5.0 reduce_sum.44
  511.5 2.6 convert_select_fusion.3
  514.2 8.8 %collective-permute-done = bf16[1,2,256,768]{3,2,1,0:T(8,128)(2,1)} collective-permute-done((bf16[1,2,256,768]{3,2,1,0:T(8,128)(2,1)S(1)}, bf16[1,2,256,768]{3,2,1,0:T(8,128)(2,1)}, u32[]{:S(2)}, u32[]{:S(2)}) %collective-permute-start) | collective-permute-done | bytes 786464 | tf_op jit(solution)/shard_map/ppermute | solution.py:17
  523.0 2.2 broadcast_select_fusion.1
  525.1 14.6 %collective-permute-done.2 = bf16[1,2,256,768]{3,2,1,0:T(8,128)(2,1)S(1)} collective-permute-done((bf16[1,2,256,768]{3,2,1,0:T(8,128)(2,1)}, bf16[1,2,256,768]{3,2,1,0:T(8,128)(2,1)S(1)}, u32[]{:S(2)}, u32[]{:S(2)}) %collective-permute-start.2) | collective-permute-done | bytes 786464 | tf_op jit(solution)/shard_map/ppermute | solution.py:17
  539.7 1.5 convert_select_fusion.1
  (89 shorter events, 9.9 us)
Async XLA Ops:
  7.2 6.9 %copy-start = (bf16[128,2048]{1,0:T(8,128)(2,1)S(1)}, bf16[128,2048]{1,0:T(8,128)(2,1)}, u32[]{:S(2)}) copy-start(bf16[128,2048]{1,0:T(8,128)(2,1)} %param.13) | copy-start | bytes 1572868
  7.2 151.4 %all-gather.3.cloned.1.call-start = ((), (), s32[]{:S(2)}) async-start(), calls=%async_computation.5 | async-start | bytes 7077888 | tf_op jit(solution)/shard_map/all_gather | solution.py:78
  21.7 8.3 %copy-start.13 = (bf16[128,2048]{1,0:T(8,128)(2,1)S(1)}, bf16[128,2048]{1,0:T(8,128)(2,1)}, u32[]{:S(2)}) copy-start(bf16[128,2048]{1,0:T(8,128)(2,1)} %param.23) | copy-start | bytes 1572868
  21.7 47.5 %all-to-all-start = ((bf16[16,48,2048]{2,1,0:T(8,128)(2,1)}), bf16[16,48,2048]{2,1,0:T(8,128)(2,1)}, u32[]{:S(2)}, u32[]{:S(2)}) async-start(bf16[16,48,2048]{2,1,0:T(8,128)(2,1)} %select_select_fusion.1), calls=%async_computation | async-start | bytes 6291456 | tf_op jit(solution)/shard_map/all_to_all | solution.py:88
  29.2 196.6 %all-gather.5.cloned.1.call-start = ((), (), s32[]{:S(2)}) async-start(), calls=%async_computation.6 | async-start | bytes 3538944 | tf_op jit(solution)/shard_map/all_gather | solution.py:79
  33.0 5.3 copy-start.14
  69.2 102.5 %all-to-all-start.2 = ((bf16[16,48,2048]{2,1,0:T(8,128)(2,1)}), bf16[16,48,2048]{2,1,0:T(8,128)(2,1)S(1)}, u32[]{:S(2)}, u32[]{:S(2)}) async-start(bf16[16,48,2048]{2,1,0:T(8,128)(2,1)} %select_select_fusion), calls=%async_computation.2 | async-start | bytes 6291456 | tf_op jit(solution)/shard_map/all_to_all | solution.py:115
  77.1 372.0 %reduce-scatter.2.cloned.1.call-start = ((), (), s32[]{:S(2)}) async-start(), calls=%async_computation.7 | async-start | bytes 10616832 | tf_op jit(solution)/shard_map/reduce_scatter | solution.py:137
  158.6 7.0 %copy-start.15 = (bf16[1,2,2048,768]{3,2,1,0:T(8,128)(2,1)S(1)}, bf16[1,2,2048,768]{3,2,1,0:T(8,128)(2,1)}, u32[]{:S(2)}) copy-start(bf16[1,2,2048,768]{3,2,1,0:T(8,128)(2,1)} %all-gather.3.cloned.1.call-done) | copy-start | bytes 18874372
  232.5 3.4 copy-start.18
  232.6 3.4 copy-start.17
  232.6 3.4 copy-start.19
  255.8 5.1 slice-start
  255.8 5.1 slice-start.1
  255.8 5.1 copy-start.20
  265.0 48.0 %all-to-all-start.3 = ((bf16[16,48,2048]{2,1,0:T(8,128)(2,1)}), bf16[16,48,2048]{2,1,0:T(8,128)(2,1)S(1)}, u32[]{:S(2)}, u32[]{:S(2)}) async-start(bf16[16,48,2048]{2,1,0:T(8,128)(2,1)} %bitcast.132), calls=%async_computation.3 | async-start | bytes 6291456 | tf_op jit(solution)/shard_map/all_to_all | solution.py:124
  313.1 6.0 %copy-start.16 = (s32[16]{0:T(128)S(1)}, s32[16]{0:T(128)}, u32[]{:S(2)}) copy-start(s32[16]{0:T(128)} %param.16) | copy-start | bytes 196
  313.1 50.2 %all-to-all-start.1 = ((bf16[16,48,2048]{2,1,0:T(8,128)(2,1)}), bf16[16,48,2048]{2,1,0:T(8,128)(2,1)}, u32[]{:S(2)}, u32[]{:S(2)}) async-start(bf16[16,48,2048]{2,1,0:T(8,128)(2,1)} %bitcast.129), calls=%async_computation.1 | async-start | bytes 6291456 | tf_op jit(solution)/shard_map/all_to_all | solution.py:98
  453.4 5.4 copy-start.6
  453.4 7.0 %copy-start.11 = (f32[1,768,256]{2,1,0:T(8,128)S(1)}, f32[1,768,256]{2,1,0:T(8,128)}, u32[]{:S(2)}) copy-start(f32[1,768,256]{2,1,0:T(8,128)} %param.22) | copy-start | bytes 2359300
  456.1 4.8 copy-start.4
  456.1 4.8 copy-start.5
  456.1 34.3 %collective-permute-start.3 = (bf16[1,2,256,768]{3,2,1,0:T(8,128)(2,1)}, bf16[1,2,256,768]{3,2,1,0:T(8,128)(2,1)}, u32[]{:S(2)}, u32[]{:S(2)}) collective-permute-start(bf16[1,2,256,768]{3,2,1,0:T(8,128)(2,1)} %fusion.28), channel_id=1, source_target_pairs={{64,0},{72,8},{80,16},{88,24},{96,32},{104,40},{112,48},{120,56},{... | collective-permute-start | bytes 2359304 | tf_op jit(solution)/shard_map/ppermute | solution.py:17
  459.1 1.4 copy-start.3
  460.6 23.7 %collective-permute-start.5 = (bf16[1,768,256]{2,1,0:T(8,128)(2,1)S(1)}, bf16[1,768,256]{2,1,0:T(8,128)(2,1)}, u32[]{:S(2)}, u32[]{:S(2)}) collective-permute-start(bf16[1,768,256]{2,1,0:T(8,128)(2,1)S(1)} %fusion.26), channel_id=1, source_target_pairs={{64,0},{72,8},{80,16},{88,24},{96,32},{104,40},{112,48},{120,56},{... | collective-permute-start | bytes 1179656 | tf_op jit(solution)/shard_map/ppermute | solution.py:17
  464.0 20.3 %copy-start.12 = (bf16[1,768,256]{2,1,0:T(8,128)(2,1)S(1)}, bf16[1,768,256]{2,1,0:T(8,128)(2,1)}, u32[]{:S(2)}) copy-start(bf16[1,768,256]{2,1,0:T(8,128)(2,1)} %param.18) | copy-start | bytes 1179652
  469.2 21.2 %copy-start.7 = (f32[1,2,256,768]{3,2,1,0:T(8,128)S(1)}, f32[1,2,256,768]{3,2,1,0:T(8,128)}, u32[]{:S(2)}) copy-start(f32[1,2,256,768]{3,2,1,0:T(8,128)} %param.20) | copy-start | bytes 4718596
  469.3 21.2 %copy-start.8 = (f32[1,2,256,768]{3,2,1,0:T(8,128)S(1)}, f32[1,2,256,768]{3,2,1,0:T(8,128)}, u32[]{:S(2)}) copy-start(f32[1,2,256,768]{3,2,1,0:T(8,128)} %param.19) | copy-start | bytes 4718596
  469.3 21.2 %copy-start.10 = (bf16[1,2,256,768]{3,2,1,0:T(8,128)(2,1)S(1)}, bf16[1,2,256,768]{3,2,1,0:T(8,128)(2,1)}, u32[]{:S(2)}) copy-start(bf16[1,2,256,768]{3,2,1,0:T(8,128)(2,1)} %param.17) | copy-start | bytes 2359300
  487.5 23.3 %collective-permute-start.1 = (bf16[1,768,256]{2,1,0:T(8,128)(2,1)S(1)}, bf16[1,768,256]{2,1,0:T(8,128)(2,1)S(1)}, u32[]{:S(2)}, u32[]{:S(2)}) collective-permute-start(bf16[1,768,256]{2,1,0:T(8,128)(2,1)S(1)} %get-tuple-element.15), channel_id=1, source_target_pairs={{64,0},{72,8},{80,16},{88,24},{96,32},{104,40},{112,48},{120,56},{... | collective-permute-start | bytes 1179656 | tf_op jit(solution)/shard_map/ppermute | solution.py:17
  490.2 21.3 %collective-permute-start.4 = (bf16[1,768,256]{2,1,0:T(8,128)(2,1)}, bf16[1,768,256]{2,1,0:T(8,128)(2,1)}, u32[]{:S(2)}, u32[]{:S(2)}) collective-permute-start(bf16[1,768,256]{2,1,0:T(8,128)(2,1)} %get-tuple-element.16), channel_id=1, source_target_pairs={{64,0},{72,8},{80,16},{88,24},{96,32},{104,40},{112,48},{120,56},{... | collective-permute-start | bytes 1179656 | tf_op jit(solution)/shard_map/ppermute | solution.py:17
  490.5 6.9 %copy-start.2 = (f32[128,4,2048]{2,1,0:T(4,128)S(1)}, f32[128,4,2048]{2,1,0:T(4,128)}, u32[]{:S(2)}) copy-start(f32[128,4,2048]{2,1,0:T(4,128)} %reshape.151) | copy-start | bytes 12582916
  494.5 28.5 %collective-permute-start = (bf16[1,2,256,768]{3,2,1,0:T(8,128)(2,1)S(1)}, bf16[1,2,256,768]{3,2,1,0:T(8,128)(2,1)}, u32[]{:S(2)}, u32[]{:S(2)}) collective-permute-start(bf16[1,2,256,768]{3,2,1,0:T(8,128)(2,1)S(1)} %get-tuple-element.18), channel_id=1, source_target_pairs={{64,0},{72,8},{80,16},{88,24},{96,32},{104,40},{112,48},{120,56},{... | collective-permute-start | bytes 2359304 | tf_op jit(solution)/shard_map/ppermute | solution.py:17
  510.5 29.2 %collective-permute-start.2 = (bf16[1,2,256,768]{3,2,1,0:T(8,128)(2,1)}, bf16[1,2,256,768]{3,2,1,0:T(8,128)(2,1)S(1)}, u32[]{:S(2)}, u32[]{:S(2)}) collective-permute-start(bf16[1,2,256,768]{3,2,1,0:T(8,128)(2,1)} %get-tuple-element.19), channel_id=1, source_target_pairs={{64,0},{72,8},{80,16},{88,24},{96,32},{104,40},{112,48},{120,56},{... | collective-permute-start | bytes 2359304 | tf_op jit(solution)/shard_map/ppermute | solution.py:17
  511.5 28.2 %copy-start.9 = (f32[1,2,256,768]{3,2,1,0:T(8,128)S(1)}, f32[1,2,256,768]{3,2,1,0:T(8,128)}, u32[]{:S(2)}) copy-start(f32[1,2,256,768]{3,2,1,0:T(8,128)} %param.19) | copy-start | bytes 4718596
  523.0 18.3 %copy-start.1 = (bf16[128,2048]{1,0:T(8,128)(2,1)S(1)}, bf16[128,2048]{1,0:T(8,128)(2,1)}, u32[]{:S(2)}) copy-start(bf16[128,2048]{1,0:T(8,128)(2,1)} %param.13) | copy-start | bytes 1572868
Sparse Core Ops, SparseCore 0:
  10.3 148.3 all-gather.2
  160.8 65.0 all-gather.4
  255.9 193.1 reduce-scatter.1
where the time goes:
time: 555 us; the launch traced here: 548 us
  waiting for transfers between devices  349 us (63%)
  other arithmetic  52.6 us (9%)
  local copies, waits for them, and re-layouts  47.2 us (9%)
  matrix products  47.1 us (8%)
  starting transfers between devices  37.2 us (7%)
  between operations  15 us (3%)
    all_gather x1, waiting for transfers between devices, body(): lax.all_gather(w_in, 'shard', axis=2, tiled=True)  81.1 us
    reduce_scatter x1, waiting for transfers between devices, body(): lax.psum_scatter(jnp.concatenate([contract_rows(rows_x, grad_both), contr...  78.3 us
    all_gather x1, waiting for transfers between devices, body(): lax.all_gather(w_down, 'shard', axis=2, tiled=True)  54.2 us
    all_to_all x1, waiting for transfers between devices, body(): lax.all_to_all(expert_out.reshape(groups, capacity, width), 'expert', spl...  39.6 us
    ppermute x6, waiting for transfers between devices, shifted(): return lax.ppermute(block, axis, route)  38.4 us
    all_to_all x1, waiting for transfers between devices, body(): lax.all_to_all(entry_grads.reshape(groups, capacity, width), 'expert', sp...  35.3 us
    all_to_all x1, waiting for transfers between devices, body(): lax.all_to_all(send_rows, 'expert', split_axis=0, concat_axis=0, tiled=True)  20.4 us
    dot_general x3, matrix products, contract_cols(): lax.dot_general(left, right, (((1,), (1,)), ((), ())), preferred_element_...  15.9 us
  transfers between devices with their start and end apart: 13, of which 9 were waited for; matrix products, arithmetic and copies ran while one was open for 20% of the time, Pallas kernels for 0%

commit v1 on v0

--- a/solution.py
+++ b/solution.py
@@ -74,6 +74,18 @@
     expert_range = jnp.arange(groups, dtype=jnp.int32)
     own_partner = jnp.sum(jnp.where(expert_range == row_index, partner, 0))
     take_other = own_partner != row_index
+    moved_weights = shifted((w_in, w_down), "expert", halfway)
+    w_in, w_down = (
+        jnp.where(take_other, moved, owned) for moved, owned in zip(moved_weights, (w_in, w_down))
+    )
+    moved_states = tuple(
+        shifted(state.astype(jnp.bfloat16), "expert", halfway).astype(state.dtype)
+        for state in (m_in, v_in, m_down, v_down)
+    )
+    m_in, v_in, m_down, v_down = (
+        jnp.where(take_other, moved, owned)
+        for moved, owned in zip(moved_states, (m_in, v_in, m_down, v_down))
+    )
     in_full, down_full = (
         lax.all_gather(w_in, "shard", axis=2, tiled=True),
         lax.all_gather(w_down, "shard", axis=2, tiled=True),
@@ -82,7 +94,7 @@
     up_weight = in_full[0, 1]
     down_weight = down_full[0]
     hidden_width = gate_weight.shape[1]
-    position, filler = route_table(expert_ids, expert_ids, groups, capacity)
+    position, filler = route_table(expert_ids, partner[expert_ids], groups, capacity)
     token_fill = jnp.where(filler >= 0, filler // top_count, -1)
     send_rows = fill_rows(tokens, token_fill, groups, capacity)
     arrived = lax.all_to_all(send_rows, "expert", split_axis=0, concat_axis=0, tiled=True)
@@ -150,35 +162,7 @@
     new_down, first_down, second_down = adam_update(
         w_down, own_moments[2], own_moments[3], grad_down
     )
-    moved_weights = shifted((new_in, new_down), "expert", halfway)
-    moved_states = (
-        shifted(first_in.astype(jnp.bfloat16), "expert", halfway).astype(first_in.dtype),
-        shifted(second_in.astype(jnp.bfloat16), "expert", halfway).astype(second_in.dtype),
-        shifted(first_down.astype(jnp.bfloat16), "expert", halfway).astype(first_down.dtype),
-        shifted(second_down.astype(jnp.bfloat16), "expert", halfway).astype(second_down.dtype),
-    )
-    placed_weights = tuple(
-        (
-            jnp.where(take_other, moved, owned)
-            for moved, owned in zip(moved_weights, (new_in, new_down))
-        )
-    )
-    placed_moments = tuple(
-        (
-            jnp.where(take_other, moved, owned)
-            for moved, owned in zip(moved_states, (first_in, second_in, first_down, second_down))
-        )
-    )
-    return (
-        mixed,
-        token_grad,
-        placed_weights[0],
-        placed_weights[1],
-        placed_moments[0],
-        placed_moments[1],
-        placed_moments[2],
-        placed_moments[3],
-    )
+    return (mixed, token_grad, new_in, new_down, first_in, second_in, first_down, second_down)
 
 
 def solution(mesh):

time: 555 us -> 467 us (0.84)
  waiting for transfers between devices: 349 us -> 250 us
  other arithmetic: 52.6 us -> 63.4 us
  starting transfers between devices: 37.2 us -> 43.7 us
    all_gather x1, waiting for transfers between devices: 54.2 us -> 0.02 us  [body(): lax.all_gather(w_down, 'shard', axis=2, tiled=True)]
    all_gather x1, waiting for transfers between devices: 81.1 us -> 46.9 us  [body(): lax.all_gather(w_in, 'shard', axis=2, tiled=True)]
    all_to_all x1, waiting for transfers between devices: 0.01 us -> 32.1 us  [body(): lax.all_to_all(send_grads, 'expert', split_axis=0, concat_axis=0, tiled=T...]
    reduce_scatter x1, waiting for transfers between devices: 78.3 us -> 50.9 us  [body(): lax.psum_scatter(jnp.concatenate([contract_rows(rows_x, grad_both), contr...]
    ppermute x6, waiting for transfers between devices: 38.4 us -> 23.2 us  [shifted(): return lax.ppermute(block, axis, route)]
    select_n x6 -> x2, other arithmetic: 14.2 us -> 1.76 us  [body(): jnp.where(take_other, moved, owned)]
    all_to_all x1, waiting for transfers between devices: 20.4 us -> 32.5 us  [body(): lax.all_to_all(send_rows, 'expert', split_axis=0, concat_axis=0, tiled=True)]
    convert_element_type x2 -> x6, other arithmetic: 2.81 us -> 12.8 us  [the longest x2 7.62 us: adam_update(): (weight.astype(jnp.float32) - update).astype(jnp.bfloat16)]
  transfers between devices with their start and end apart: 13 -> 13, of which waited for: 9 -> 8; matrix products, arithmetic and copies ran while one was open for 20% -> 25% of each run, Pallas kernels for 0% -> 0%
where the time goes in v1:
time: 467 us; the launch traced here: 460 us
  waiting for transfers between devices  250 us (54%)
  other arithmetic  63.4 us (14%)
  local copies, waits for them, and re-layouts  45.1 us (10%)
  starting transfers between devices  43.7 us (9%)
  matrix products  43.3 us (9%)
  between operations  15.1 us (3%)
    reduce_scatter x1, waiting for transfers between devices, body(): lax.psum_scatter(jnp.concatenate([contract_rows(rows_x, grad_both), contr...  50.9 us
    all_gather x1, waiting for transfers between devices, body(): lax.all_gather(w_in, 'shard', axis=2, tiled=True)  46.9 us
    all_to_all x1, waiting for transfers between devices, body(): lax.all_to_all(entry_grads.reshape(groups, capacity, width), 'expert', sp...  33.8 us
    all_to_all x1, waiting for transfers between devices, body(): lax.all_to_all(send_rows, 'expert', split_axis=0, concat_axis=0, tiled=True)  32.5 us
    all_to_all x1, waiting for transfers between devices, body(): lax.all_to_all(send_grads, 'expert', split_axis=0, concat_axis=0, tiled=T...  32.1 us
    all_to_all x1, waiting for transfers between devices, body(): lax.all_to_all(expert_out.reshape(groups, capacity, width), 'expert', spl...  30.1 us
    ppermute x6, waiting for transfers between devices, shifted(): return lax.ppermute(block, axis, route)  23.2 us
    dot_general x3, matrix products, contract_cols(): lax.dot_general(left, right, (((1,), (1,)), ((), ())), preferred_element_...  16.2 us
  transfers between devices with their start and end apart: 13, of which 8 were waited for; matrix products, arithmetic and copies ran while one was open for 25% of the time, Pallas kernels for 0%

profile of v1, /device:TPU:1, one launch (start us, length us, event | category | flops | bytes accessed | tf_op | source)
XLA Modules:
  0.0 460.2 jit_solution(10623074164776586844)
XLA Ops:
  7.2 3.8 collective-permute-start.1
  11.1 1.3 fusion.23
  13.0 6.8 %collective-permute-done.1 = bf16[1,768,256]{2,1,0:T(8,128)(2,1)S(1)} collective-permute-done((bf16[1,768,256]{2,1,0:T(8,128)(2,1)}, bf16[1,768,256]{2,1,0:T(8,128)(2,1)S(1)}, u32[]{:S(2)}, u32[]{:S(2)}) %collective-permute-start.1) | collective-permute-done | bytes 393248 | tf_op jit(solution)/shard_map/ppermute | solution.py:17
  20.7 3.0 collective-permute-start
  23.7 16.4 %collective-permute-done = bf16[1,2,256,768]{3,2,1,0:T(8,128)(2,1)S(1)} collective-permute-done((bf16[1,2,256,768]{3,2,1,0:T(8,128)(2,1)}, bf16[1,2,256,768]{3,2,1,0:T(8,128)(2,1)S(1)}, u32[]{:S(2)}, u32[]{:S(2)}) %collective-permute-start) | collective-permute-done | bytes 786464 | tf_op jit(solution)/shard_map/ppermute | solution.py:17
  41.5 3.1 mul.160
  44.5 5.3 %mul.161 = f32[512,2048]{1,0:T(8,128)} reshape(f32[128,4,2048]{2,1,0:T(4,128)} %mul.160) | data formatting | bytes 8388608 | tf_op jit(solution)/shard_map/mul | solution.py:123
  50.8 10.2 %select_multiply_fusion = s32[128,4]{0,1:T(4,128)S(1)} fusion(s32[128,4]{0,1:T(4,128)S(1)} %copy-done.14, s32[]{:T(128)} %bitcast, s32[]{:T(128)} %bitcast.1, s32[]{:T(128)} %bitcast.2, s32[]{:T(128)} %bitcast.3, s32[]{:T(128)} %bitcast.4, s32[]{:T(128)} %bitcast.5, s32[]{:T(128)} %bitcast.6, s32[]{:T(128)} %bitcast.7, s32[]{:T(128)} %bitcast.8, s32[]{:T(128)} %bitcast.9, ...), kind=kLoop, calls=%fused_computation.69 | loop fusion | flops 17408 | bytes 4160 | tf_op jit(solution)/shard_map/mul | solution.py:40
  61.2 1.2 reduce-window.6
  62.8 2.4 scatter_custom_fusion
  65.5 2.5 multiply_convert_fusion
  67.9 4.3 gather_fusion.1
  72.2 3.4 select_select_fusion
  75.5 9.2 %all-to-all-start.2 = ((bf16[16,48,2048]{2,1,0:T(8,128)(2,1)}), bf16[16,48,2048]{2,1,0:T(8,128)(2,1)}, u32[]{:S(2)}, u32[]{:S(2)}) async-start(bf16[16,48,2048]{2,1,0:T(8,128)(2,1)} %select_select_fusion), calls=%async_computation.2 | async-start | bytes 6291456 | tf_op jit(solution)/shard_map/all_to_all | solution.py:127
  84.9 4.3 gather_fusion
  89.2 3.4 select_select_fusion.1
  92.6 32.1 %all-to-all-done.2 = bf16[16,48,2048]{2,1,0:T(8,128)(2,1)} async-done(((bf16[16,48,2048]{2,1,0:T(8,128)(2,1)}), bf16[16,48,2048]{2,1,0:T(8,128)(2,1)}, u32[]{:S(2)}, u32[]{:S(2)}) %all-to-all-start.2) | async-done | bytes 3145760 | tf_op jit(solution)/shard_map/all_to_all | solution.py:127
  124.7 8.0 %all-to-all-start = ((bf16[16,48,2048]{2,1,0:T(8,128)(2,1)}), bf16[16,48,2048]{2,1,0:T(8,128)(2,1)S(1)}, u32[]{:S(2)}, u32[]{:S(2)}) async-start(bf16[16,48,2048]{2,1,0:T(8,128)(2,1)} %select_select_fusion.1), calls=%async_computation | async-start | bytes 6291456 | tf_op jit(solution)/shard_map/all_to_all | solution.py:100
  133.4 7.0 %fusion = f32[768,768]{0,1:T(8,128)} fusion(bf16[768,2048]{1,0:T(8,128)(2,1)} %bitcast.27, bf16[1,768,2048]{2,1,0:T(8,128)(2,1)} %all-gather.5.cloned.1.call-done), kind=kOutput, calls=%fused_computation.14 | convolution fusion | flops 2415919104 | bytes 8650752 | tf_op jit(solution)/shard_map/dot_general | solution.py:59
  140.4 32.5 %all-to-all-done = bf16[16,48,2048]{2,1,0:T(8,128)(2,1)S(1)} async-done(((bf16[16,48,2048]{2,1,0:T(8,128)(2,1)}), bf16[16,48,2048]{2,1,0:T(8,128)(2,1)S(1)}, u32[]{:S(2)}, u32[]{:S(2)}) %all-to-all-start) | async-done | bytes 3145760 | tf_op jit(solution)/shard_map/all_to_all | solution.py:100
  172.9 46.9 %all-gather.3.cloned.1.call-done = bf16[1,2,2048,768]{3,2,1,0:T(8,128)(2,1)} async-done(((bf16[1,2,256,768]{3,2,1,0:T(8,128)(2,1)}), bf16[1,2,2048,768]{3,2,1,0:T(8,128)(2,1)}) %all-gather.3.cloned.1.call-update) | async-done | bytes 6291472 | tf_op jit(solution)/shard_map/all_gather | solution.py:90
  219.7 4.7 %fusion.5 = f32[768,768]{0,1:T(8,128)S(1)} fusion(bf16[768,2048]{1,0:T(8,128)(2,1)S(1)} %bitcast.106, bf16[1,2,2048,768]{3,2,1,0:T(8,128)(2,1)} %all-gather.3.cloned.1.call-done), kind=kOutput, calls=%fused_computation.21 | convolution fusion | flops 2415919104 | bytes 8650752 | tf_op jit(solution)/shard_map/dot_general | solution.py:104
  224.5 3.5 multiply_convert_fusion.2
  228.0 5.9 %convolution_convert_fusion.1 = bf16[2048,768]{0,1:T(8,128)(2,1)S(1)} fusion(bf16[768,768]{0,1:T(8,128)(2,1)S(1)} %get-tuple-element.19, bf16[768,2048]{1,0:T(8,128)(2,1)} %bitcast.27), kind=kOutput, calls=%fused_computation.10 | convolution fusion | flops 2417491968 | bytes 7471104 | tf_op jit(solution)/shard_map/dot_general | solution.py:53
  234.0 6.3 %convolution_convert_fusion = bf16[2048,1536]{0,1:T(8,128)(2,1)S(1)} fusion(bf16[768,2048]{1,0:T(8,128)(2,1)S(1)} %bitcast.108, bf16[768,768]{0,1:T(8,128)(2,1)S(1)} %get-tuple-element.18, bf16[768,768]{0,1:T(8,128)(2,1)S(1)} %get-tuple-element.17), kind=kOutput, calls=%fused_computation.6 | convolution fusion | flops 4839702528 | bytes 11796480 | tf_op jit(solution)/shard_map/dot_general | solution.py:53
  240.3 11.6 %pad_maximum_fusion = bf16[2048,2304]{0,1:T(8,128)(2,1)} fusion(bf16[2048,768]{0,1:T(8,128)(2,1)S(1)} %convolution_convert_fusion.1, bf16[2048,1536]{0,1:T(8,128)(2,1)S(1)} %convolution_convert_fusion), kind=kLoop, calls=%fused_computation.5 | loop fusion | flops 18874368 | bytes 18874368 | tf_op jit(solution)/shard_map/concatenate | solution.py:150
  252.0 5.1 %fusion.4 = f32[768,2048]{1,0:T(8,128)S(1)} fusion(bf16[768,768]{0,1:T(8,128)(2,1)} %copy-done.17, bf16[1,2,2048,768]{3,2,1,0:T(8,128)(2,1)} %all-gather.3.cloned.1.call-done), kind=kOutput, calls=%fused_computation.20 | convolution fusion | flops 2415919104 | bytes 10616832 | tf_op jit(solution)/shard_map/dot_general | solution.py:59
  257.0 4.1 add_convert_fusion
  261.2 5.8 %all-to-all-start.3 = ((bf16[16,48,2048]{2,1,0:T(8,128)(2,1)}), bf16[16,48,2048]{2,1,0:T(8,128)(2,1)S(1)}, u32[]{:S(2)}, u32[]{:S(2)}) async-start(bf16[16,48,2048]{2,1,0:T(8,128)(2,1)} %bitcast.109), calls=%async_computation.3 | async-start | bytes 6291456 | tf_op jit(solution)/shard_map/all_to_all | solution.py:136
  267.0 6.6 %convolution_convert_fusion.2 = bf16[768,2048]{1,0:T(8,128)(2,1)} fusion(bf16[768,768]{0,1:T(8,128)(2,1)} %copy-done.19, bf16[1,768,2048]{2,1,0:T(8,128)(2,1)} %all-gather.5.cloned.1.call-done), kind=kOutput, calls=%fused_computation.11 | convolution fusion | flops 2417491968 | bytes 7471104 | tf_op jit(solution)/shard_map/dot_general | solution.py:107
  273.6 33.8 %all-to-all-done.3 = bf16[16,48,2048]{2,1,0:T(8,128)(2,1)S(1)} async-done(((bf16[16,48,2048]{2,1,0:T(8,128)(2,1)}), bf16[16,48,2048]{2,1,0:T(8,128)(2,1)S(1)}, u32[]{:S(2)}, u32[]{:S(2)}) %all-to-all-start.3) | async-done | bytes 3145760 | tf_op jit(solution)/shard_map/all_to_all | solution.py:136
  307.4 7.3 %all-to-all-start.1 = ((bf16[16,48,2048]{2,1,0:T(8,128)(2,1)}), bf16[16,48,2048]{2,1,0:T(8,128)(2,1)}, u32[]{:S(2)}, u32[]{:S(2)}) async-start(bf16[16,48,2048]{2,1,0:T(8,128)(2,1)} %bitcast.105), calls=%async_computation.1 | async-start | bytes 6291456 | tf_op jit(solution)/shard_map/all_to_all | solution.py:110
  314.7 2.7 convert_element_type.94
  317.4 2.7 collective-permute-start.2
  322.1 2.7 collective-permute-start.4
  326.0 3.3 gather_fusion.3
  329.3 30.1 %all-to-all-done.1 = bf16[16,48,2048]{2,1,0:T(8,128)(2,1)} async-done(((bf16[16,48,2048]{2,1,0:T(8,128)(2,1)}), bf16[16,48,2048]{2,1,0:T(8,128)(2,1)}, u32[]{:S(2)}, u32[]{:S(2)}) %all-to-all-start.1) | async-done | bytes 3145760 | tf_op jit(solution)/shard_map/all_to_all | solution.py:110
  359.5 7.7 %gather_fusion.2 = bf16[512,2048]{1,0:T(8,128)(2,1)} fusion(bf16[768,2048]{1,0:T(8,128)(2,1)} %bitcast.25, s32[1024]{0:T(1024)S(1)} %pad_clamp_fusion.1), kind=kCustom, calls=%fused_computation.clone | custom fusion | bytes 4196352 | tf_op jit(solution)/shard_map/jit(_take)/gather | solution.py:117
  367.2 5.0 %broadcast_select_fusion = (bf16[512,2048]{1,0:T(8,128)(2,1)}, f32[512,2048]{1,0:T(8,128)}) fusion(bf16[512,2048]{1,0:T(8,128)(2,1)S(1)} %copy-done.2, pred[512]{0:T(512)(128)(4,1)S(1)} %get-tuple-element.15, bf16[512,2048]{1,0:T(8,128)(2,1)} %gather_fusion.2), kind=kLoop, calls=%fused_computation.32 | loop fusion | flops 3145728 | bytes 10486272 | tf_op jit(solution)/shard_map/jit(_take)/select_n | solution.py:143
  372.1 5.2 %reshape.153 = f32[128,4,2048]{2,1,0:T(4,128)} reshape(f32[512,2048]{1,0:T(8,128)} %get-tuple-element.27) | data formatting | bytes 8388608 | tf_op jit(solution)/shard_map/convert_element_type | solution.py:120
  377.3 3.0 reshape.151
  380.3 3.9 reduce_sum.45
  384.1 6.2 %multiply_reduce_fusion = bf16[128,2048]{1,0:T(8,128)(2,1)} fusion(f32[128,4,2048]{2,1,0:T(4,128)} %reshape.153, f32[128,4]{1,0:T(8,128)S(1)} %copy.21), kind=kLoop, calls=%fused_computation.9 | loop fusion | flops 1835008 | bytes 4720640 | tf_op jit(solution)/shard_map/reduce_sum | solution.py:120
  390.3 50.9 %reduce-scatter.2.cloned.1.call-done = bf16[256,2304]{0,1:T(8,128)(2,1)} async-done(((bf16[2048,2304]{0,1:T(8,128)(2,1)}), bf16[256,2304]{0,1:T(8,128)(2,1)}) %reduce-scatter.2.cloned.1.call-update) | async-done | bytes 1179664 | tf_op jit(solution)/shard_map/reduce_scatter | solution.py:149
  441.2 1.2 slice.52
  442.5 1.6 copy.28
  445.7 4.7 %subtract_convert_fusion = (bf16[1,2,256,768]{3,2,1,0:T(8,128)(2,1)}, f32[1,2,256,768]{3,2,1,0:T(8,128)}, f32[1,2,256,768]{3,2,1,0:T(8,128)}) fusion(bf16[1,2,256,768]{3,2,1,0:T(8,128)(2,1)S(1)} %copy-done.3, f32[256,2,768]{2,0,1:T(8,128)} %copy.28, f32[1,2,256,768]{3,2,1,0:T(8,128)S(1)} %copy-done.5, bf16[1,2,256,768]{3,2,1,0:T(8,128)(2,1)} %collective-permute-done.2, ...), kind=kLoop, calls=%fused_computation.37 | loop fusion | flops 7077888 | bytes 11010049 | tf_op jit(solution)/shard_map/convert_element_type | solution.py:31
  450.5 2.9 subtract_convert_fusion.1
  (93 shorter events, 9.5 us)
Async XLA Ops:
  7.2 77.7 %copy-start = (bf16[128,2048]{1,0:T(8,128)(2,1)S(1)}, bf16[128,2048]{1,0:T(8,128)(2,1)}, u32[]{:S(2)}) copy-start(bf16[128,2048]{1,0:T(8,128)(2,1)} %param.13) | copy-start | bytes 1572868
  7.2 126.2 %all-gather.5.cloned.1.call-start = ((), (), s32[]{:S(2)}) async-start(), calls=%async_computation.6 | async-start | bytes 3538944 | tf_op jit(solution)/shard_map/all_gather | solution.py:91
  7.2 12.6 %collective-permute-start.1 = (bf16[1,768,256]{2,1,0:T(8,128)(2,1)}, bf16[1,768,256]{2,1,0:T(8,128)(2,1)S(1)}, u32[]{:S(2)}, u32[]{:S(2)}) collective-permute-start(bf16[1,768,256]{2,1,0:T(8,128)(2,1)} %param.18), channel_id=1, source_target_pairs={{64,0},{72,8},{80,16},{88,24},{96,32},{104,40},{112,48},{120,56},{... | collective-permute-start | bytes 1179656 | tf_op jit(solution)/shard_map/ppermute | solution.py:17
  13.0 28.1 %copy-start.14 = (s32[128,4]{0,1:T(4,128)S(1)}, s32[128,4]{0,1:T(4,128)}, u32[]{:S(2)}) copy-start(s32[128,4]{0,1:T(4,128)} %param.14) | copy-start | bytes 6148
  13.0 28.4 %copy-start.12 = (bf16[128,2048]{1,0:T(8,128)(2,1)S(1)}, bf16[128,2048]{1,0:T(8,128)(2,1)}, u32[]{:S(2)}) copy-start(bf16[128,2048]{1,0:T(8,128)(2,1)} %param.23) | copy-start | bytes 1572868
  20.6 199.1 %all-gather.3.cloned.1.call-start = ((), (), s32[]{:S(2)}) async-start(), calls=%async_computation.5 | async-start | bytes 7077888 | tf_op jit(solution)/shard_map/all_gather | solution.py:90
  20.7 19.4 %collective-permute-start = (bf16[1,2,256,768]{3,2,1,0:T(8,128)(2,1)}, bf16[1,2,256,768]{3,2,1,0:T(8,128)(2,1)S(1)}, u32[]{:S(2)}, u32[]{:S(2)}) collective-permute-start(bf16[1,2,256,768]{3,2,1,0:T(8,128)(2,1)} %param.17), channel_id=1, source_target_pairs={{64,0},{72,8},{80,16},{88,24},{96,32},{104,40},{112,48},{120,56},{... | collective-permute-start | bytes 2359304 | tf_op jit(solution)/shard_map/ppermute | solution.py:17
  44.5 5.3 %copy-start.15 = (f32[128,4]{0,1:T(4,128)S(1)}, f32[128,4]{0,1:T(4,128)}, u32[]{:S(2)}) copy-start(f32[128,4]{0,1:T(4,128)} %param.15) | copy-start | bytes 6148
  44.5 5.6 %copy-start.13 = (s32[16]{0:T(128)S(1)}, s32[16]{0:T(128)}, u32[]{:S(2)}) copy-start(s32[16]{0:T(128)} %param.16) | copy-start | bytes 196
  75.5 49.2 %all-to-all-start.2 = ((bf16[16,48,2048]{2,1,0:T(8,128)(2,1)}), bf16[16,48,2048]{2,1,0:T(8,128)(2,1)}, u32[]{:S(2)}, u32[]{:S(2)}) async-start(bf16[16,48,2048]{2,1,0:T(8,128)(2,1)} %select_select_fusion), calls=%async_computation.2 | async-start | bytes 6291456 | tf_op jit(solution)/shard_map/all_to_all | solution.py:127
  124.7 48.1 %all-to-all-start = ((bf16[16,48,2048]{2,1,0:T(8,128)(2,1)}), bf16[16,48,2048]{2,1,0:T(8,128)(2,1)S(1)}, u32[]{:S(2)}, u32[]{:S(2)}) async-start(bf16[16,48,2048]{2,1,0:T(8,128)(2,1)} %select_select_fusion.1), calls=%async_computation | async-start | bytes 6291456 | tf_op jit(solution)/shard_map/all_to_all | solution.py:100
  132.8 308.4 %reduce-scatter.2.cloned.1.call-start = ((), (), s32[]{:S(2)}) async-start(), calls=%async_computation.7 | async-start | bytes 10616832 | tf_op jit(solution)/shard_map/reduce_scatter | solution.py:149
  219.7 4.7 %copy-start.16 = (bf16[1,2,2048,768]{3,2,1,0:T(8,128)(2,1)S(1)}, bf16[1,2,2048,768]{3,2,1,0:T(8,128)(2,1)}, u32[]{:S(2)}) copy-start(bf16[1,2,2048,768]{3,2,1,0:T(8,128)(2,1)} %all-gather.3.cloned.1.call-done) | copy-start | bytes 18874372
  219.7 4.7 %copy-start.18 = (f32[768,768]{0,1:T(8,128)S(1)}, f32[768,768]{0,1:T(8,128)}, u32[]{:S(2)}) copy-start(f32[768,768]{0,1:T(8,128)} %fusion) | copy-start | bytes 7077892
  228.0 6.0 %copy-start.19 = (bf16[768,768]{0,1:T(8,128)(2,1)}, bf16[768,768]{0,1:T(8,128)(2,1)S(1)}, u32[]{:S(2)}) copy-start(bf16[768,768]{0,1:T(8,128)(2,1)S(1)} %get-tuple-element.19) | copy-start | bytes 3538948
  228.0 6.0 %copy-start.17 = (bf16[768,768]{0,1:T(8,128)(2,1)}, bf16[768,768]{0,1:T(8,128)(2,1)S(1)}, u32[]{:S(2)}) copy-start(bf16[768,768]{0,1:T(8,128)(2,1)S(1)} %get-tuple-element.18) | copy-start | bytes 3538948
  228.0 6.0 %copy-start.20 = (bf16[768,768]{0,1:T(8,128)(2,1)}, bf16[768,768]{0,1:T(8,128)(2,1)S(1)}, u32[]{:S(2)}) copy-start(bf16[768,768]{0,1:T(8,128)(2,1)S(1)} %get-tuple-element.17) | copy-start | bytes 3538948
  251.9 5.1 %slice-start = ((s8[6291456]{0:T(1024)(128)(4,1)}), s8[2097152]{0:T(1024)(128)(4,1)S(1)}, s32[]{:S(2)}) async-start(s8[6291456]{0:T(1024)(128)(4,1)} %bitcast.112), calls=%async_computation.8 | async-start | bytes 4194304
  251.9 5.1 %slice-start.1 = ((s8[6291456]{0:T(1024)(128)(4,1)}), s8[4194304]{0:T(1024)(128)(4,1)S(1)}, s32[]{:S(2)}) async-start(s8[6291456]{0:T(1024)(128)(4,1)} %bitcast.112), calls=%async_computation.9 | async-start | bytes 8388608
  251.9 5.1 %copy-start.21 = (bf16[768,768]{0,1:T(8,128)(2,1)S(1)}, bf16[768,768]{0,1:T(8,128)(2,1)}, u32[]{:S(2)}) copy-start(bf16[768,768]{0,1:T(8,128)(2,1)} %copy-done.20) | copy-start | bytes 3538948
  261.2 46.3 %all-to-all-start.3 = ((bf16[16,48,2048]{2,1,0:T(8,128)(2,1)}), bf16[16,48,2048]{2,1,0:T(8,128)(2,1)S(1)}, u32[]{:S(2)}, u32[]{:S(2)}) async-start(bf16[16,48,2048]{2,1,0:T(8,128)(2,1)} %bitcast.109), calls=%async_computation.3 | async-start | bytes 6291456 | tf_op jit(solution)/shard_map/all_to_all | solution.py:136
  307.4 52.0 %all-to-all-start.1 = ((bf16[16,48,2048]{2,1,0:T(8,128)(2,1)}), bf16[16,48,2048]{2,1,0:T(8,128)(2,1)}, u32[]{:S(2)}, u32[]{:S(2)}) async-start(bf16[16,48,2048]{2,1,0:T(8,128)(2,1)} %bitcast.105), calls=%async_computation.1 | async-start | bytes 6291456 | tf_op jit(solution)/shard_map/all_to_all | solution.py:110
  314.7 5.4 %copy-start.6 = (f32[1,2,256,768]{3,2,1,0:T(8,128)S(1)}, f32[1,2,256,768]{3,2,1,0:T(8,128)}, u32[]{:S(2)}) copy-start(f32[1,2,256,768]{3,2,1,0:T(8,128)} %param.20) | copy-start | bytes 4718596
  314.7 6.6 %copy-start.8 = (f32[1,768,256]{2,1,0:T(8,128)S(1)}, f32[1,768,256]{2,1,0:T(8,128)}, u32[]{:S(2)}) copy-start(f32[1,768,256]{2,1,0:T(8,128)} %param.21) | copy-start | bytes 2359300
  314.7 10.2 %copy-start.10 = (f32[1,768,256]{2,1,0:T(8,128)S(1)}, f32[1,768,256]{2,1,0:T(8,128)}, u32[]{:S(2)}) copy-start(f32[1,768,256]{2,1,0:T(8,128)} %param.22) | copy-start | bytes 2359300
  317.4 126.9 %collective-permute-start.2 = (bf16[1,2,256,768]{3,2,1,0:T(8,128)(2,1)}, bf16[1,2,256,768]{3,2,1,0:T(8,128)(2,1)}, u32[]{:S(2)}, u32[]{:S(2)}) collective-permute-start(bf16[1,2,256,768]{3,2,1,0:T(8,128)(2,1)} %convert_element_type.94), channel_id=1, source_target_pairs={{64,0},{72,8},{80,16},{88,24},{96,32},{104,40},{112,48},{120,56},{... | collective-permute-start | bytes 2359304 | tf_op jit(solution)/shard_map/ppermute | solution.py:17
  321.1 123.2 %collective-permute-start.3 = (bf16[1,2,256,768]{3,2,1,0:T(8,128)(2,1)}, bf16[1,2,256,768]{3,2,1,0:T(8,128)(2,1)}, u32[]{:S(2)}, u32[]{:S(2)}) collective-permute-start(bf16[1,2,256,768]{3,2,1,0:T(8,128)(2,1)} %convert_element_type.97), channel_id=1, source_target_pairs={{64,0},{72,8},{80,16},{88,24},{96,32},{104,40},{112,48},{120,56},{... | collective-permute-start | bytes 2359304 | tf_op jit(solution)/shard_map/ppermute | solution.py:17
  322.1 128.3 %collective-permute-start.4 = (bf16[1,768,256]{2,1,0:T(8,128)(2,1)}, bf16[1,768,256]{2,1,0:T(8,128)(2,1)}, u32[]{:S(2)}, u32[]{:S(2)}) collective-permute-start(bf16[1,768,256]{2,1,0:T(8,128)(2,1)} %convert_element_type.101), channel_id=1, source_target_pairs={{64,0},{72,8},{80,16},{88,24},{96,32},{104,40},{112,48},{120,56},{... | collective-permute-start | bytes 1179656 | tf_op jit(solution)/shard_map/ppermute | solution.py:17
  325.7 124.8 %collective-permute-start.5 = (bf16[1,768,256]{2,1,0:T(8,128)(2,1)}, bf16[1,768,256]{2,1,0:T(8,128)(2,1)}, u32[]{:S(2)}, u32[]{:S(2)}) collective-permute-start(bf16[1,768,256]{2,1,0:T(8,128)(2,1)} %convert_element_type.103), channel_id=1, source_target_pairs={{64,0},{72,8},{80,16},{88,24},{96,32},{104,40},{112,48},{120,56},{... | collective-permute-start | bytes 1179656 | tf_op jit(solution)/shard_map/ppermute | solution.py:17
  359.5 7.7 %copy-start.2 = (bf16[512,2048]{1,0:T(8,128)(2,1)S(1)}, bf16[512,2048]{1,0:T(8,128)(2,1)}, u32[]{:S(2)}) copy-start(bf16[512,2048]{1,0:T(8,128)(2,1)} %gather_fusion.3) | copy-start | bytes 6291460
  442.5 1.6 copy-start.4
  444.1 1.1 copy-start.3
  444.1 1.7 copy-start.5
  444.3 6.2 %copy-start.7 = (bf16[1,768,256]{2,1,0:T(8,128)(2,1)S(1)}, bf16[1,768,256]{2,1,0:T(8,128)(2,1)}, u32[]{:S(2)}) copy-start(bf16[1,768,256]{2,1,0:T(8,128)(2,1)} %broadcast_select_fusion.2) | copy-start | bytes 1179652
  444.3 6.2 %copy-start.9 = (f32[1,768,256]{2,1,0:T(8,128)S(1)}, f32[1,768,256]{2,1,0:T(8,128)}, u32[]{:S(2)}) copy-start(f32[1,768,256]{2,1,0:T(8,128)} %param.21) | copy-start | bytes 2359300
  444.3 6.2 %copy-start.11 = (f32[1,768,256]{2,1,0:T(8,128)S(1)}, f32[1,768,256]{2,1,0:T(8,128)}, u32[]{:S(2)}) copy-start(f32[1,768,256]{2,1,0:T(8,128)} %param.22) | copy-start | bytes 2359300
  445.7 7.7 %copy-start.1 = (bf16[128,2048]{1,0:T(8,128)(2,1)S(1)}, bf16[128,2048]{1,0:T(8,128)(2,1)}, u32[]{:S(2)}) copy-start(bf16[128,2048]{1,0:T(8,128)(2,1)} %param.13) | copy-start | bytes 1572868
Sparse Core Ops, SparseCore 0:
  20.8 70.1 all-gather.4
  93.8 125.8 all-gather.2
  252.0 189.1 reduce-scatter.1

commit v2 on v1

--- a/solution.py
+++ b/solution.py
@@ -15,6 +15,32 @@
     devices = range(lax.axis_size(axis))
     route = [((i - distance) % len(devices), i) for i in devices]
     return lax.ppermute(block, axis, route)
+
+
+def gather_shards(block, axis, dim):
+    count = lax.axis_size(axis)
+    me = lax.axis_index(axis)
+    arrived = [block] + [
+        lax.ppermute(block, axis, [(i, (i + k) % count) for i in range(count)])
+        for k in range(1, count)
+    ]
+    order = (me - jnp.arange(count, dtype=jnp.int32)) % count
+    stacked = jnp.take(jnp.stack(arrived), order, axis=0)
+    return jnp.concatenate([stacked[j] for j in range(count)], axis=dim)
+
+
+def scatter_sum(partial, axis):
+    count = lax.axis_size(axis)
+    me = lax.axis_index(axis)
+    rows = partial.shape[0] // count
+    chunks = partial.reshape(count, rows, partial.shape[1])
+    total = jnp.take(chunks, me, axis=0).astype(jnp.float32)
+    for k in range(1, count):
+        piece = jnp.take(chunks, (me + k) % count, axis=0)
+        total = total + lax.ppermute(
+            piece, axis, [(i, (i + k) % count) for i in range(count)]
+        ).astype(jnp.float32)
+    return total
 
 
 def silu_parts(gate_pre):
@@ -86,10 +112,7 @@
         jnp.where(take_other, moved, owned)
         for moved, owned in zip(moved_states, (m_in, v_in, m_down, v_down))
     )
-    in_full, down_full = (
-        lax.all_gather(w_in, "shard", axis=2, tiled=True),
-        lax.all_gather(w_down, "shard", axis=2, tiled=True),
-    )
+    in_full, down_full = (gather_shards(w_in, "shard", 2), gather_shards(w_down, "shard", 2))
     gate_weight = in_full[0, 0]
     up_weight = in_full[0, 1]
     down_weight = down_full[0]
@@ -146,14 +169,12 @@
     token_grad = jnp.sum(per_back.astype(jnp.float32), axis=1).astype(jnp.bfloat16)
     grad_both = jnp.concatenate([grad_gate, grad_up], axis=1)
     share_rows = width // lax.axis_size("shard")
-    shares = lax.psum_scatter(
+    shares = scatter_sum(
         jnp.concatenate(
             [contract_rows(rows_x, grad_both), contract_rows(dout_rows, hidden)], axis=1
         ).astype(jnp.bfloat16),
         "shard",
-        scatter_dimension=0,
-        tiled=True,
-    ).astype(jnp.float32)
+    )
     grad_in = jnp.transpose(
         shares[:, : 2 * hidden_width].reshape(share_rows, 2, hidden_width), (1, 0, 2)
     )[None]

time: 467 us -> 630 us (1.35)
  local copies, waits for them, and re-layouts: 45.1 us -> 107 us
  starting transfers between devices: 43.7 us -> 91.1 us
  waiting for transfers between devices: 250 us -> 292 us
  between operations: 15.1 us -> 2.23 us
  other arithmetic: 63.4 us -> 75.2 us
  matrix products: 43.3 us -> 52.9 us
    ppermute x0 -> x21, waiting for transfers between devices: none -> 188 us  [the longest x7 103 us: scatter_sum(): lax.ppermute(piece, axis, [(i, (i + k) % count) for i in range(count)])]
    ppermute x6, waiting for transfers between devices: 23.2 us -> 88.6 us  [shifted(): return lax.ppermute(block, axis, route)]
    reduce_scatter x1 -> x0, waiting for transfers between devices: 50.9 us -> none  [body(): lax.psum_scatter(jnp.concatenate([contract_rows(rows_x, grad_both), contr...]
    all_gather x2 -> x0, waiting for transfers between devices: 46.9 us -> none  [the longest x1 46.9 us: body(): lax.all_gather(w_in, 'shard', axis=2, tiled=True)]
    unnamed x50 -> x78, local copies, waits for them, and re-layouts: 1.75 us -> 42.7 us
    ppermute x0 -> x21, starting transfers between devices: none -> 35.2 us  [the longest x14 24.5 us: gather_shards(): lax.ppermute(block, axis, [(i, (i + k) % count) for i in range(count)])]
    all_to_all x1, waiting for transfers between devices: 33.8 us -> 0.01 us  [body(): lax.all_to_all(entry_grads.reshape(groups, capacity, width), 'expert', sp...]
    all_to_all x1, waiting for transfers between devices: 32.5 us -> 0.01 us  [body(): lax.all_to_all(send_rows, 'expert', split_axis=0, concat_axis=0, tiled=True)]
  transfers between devices with their start and end apart: 13 -> 31, of which waited for: 8 -> 18; matrix products, arithmetic and copies ran while one was open for 25% -> 25% of each run, Pallas kernels for 0% -> 0%
where the time goes in v2:
time: 630 us; the launch traced here: 620 us
  waiting for transfers between devices  292 us (46%)
  local copies, waits for them, and re-layouts  107 us (17%)
  starting transfers between devices  91.1 us (14%)
  other arithmetic  75.2 us (12%)
  matrix products  52.9 us (8%)
    ppermute x7, waiting for transfers between devices, scatter_sum(): lax.ppermute(piece, axis, [(i, (i + k) % count) for i in range(count)])  103 us
    ppermute x6, waiting for transfers between devices, shifted(): return lax.ppermute(block, axis, route)  88.6 us
    ppermute x14, waiting for transfers between devices, gather_shards(): lax.ppermute(block, axis, [(i, (i + k) % count) for i in range(count)])  84.7 us
    unnamed x78, local copies, waits for them, and re-layouts  42.7 us
    ppermute x6, starting transfers between devices, shifted(): return lax.ppermute(block, axis, route)  26.5 us
    ppermute x14, starting transfers between devices, gather_shards(): lax.ppermute(block, axis, [(i, (i + k) % count) for i in range(count)])  24.5 us
    dot_general x3, matrix products, contract_cols(): lax.dot_general(left, right, (((1,), (1,)), ((), ())), preferred_element_...  20.7 us
    all_to_all x1, waiting for transfers between devices, body(): lax.all_to_all(send_grads, 'expert', split_axis=0, concat_axis=0, tiled=T...  15.1 us
  transfers between devices with their start and end apart: 31, of which 18 were waited for; matrix products, arithmetic and copies ran while one was open for 25% of the time, Pallas kernels for 0%

profile of v2, /device:TPU:1, one launch (start us, length us, event | category | flops | bytes accessed | tf_op | source)
XLA Modules:
  0.0 619.8 jit_solution(16810991209922505881)
XLA Ops:
  3.7 10.8 %select_multiply_fusion = s32[128,4]{0,1:T(4,128)S(1)} fusion(s32[128,4]{0,1:T(4,128)} %param.16, s32[]{:T(128)} %bitcast, s32[]{:T(128)} %bitcast.1, s32[]{:T(128)} %bitcast.2, s32[]{:T(128)} %bitcast.3, s32[]{:T(128)} %bitcast.4, s32[]{:T(128)} %bitcast.5, s32[]{:T(128)} %bitcast.6, s32[]{:T(128)} %bitcast.7, s32[]{:T(128)} %bitcast.8, s32[]{:T(128)} %bitcast.9, ...), kind=kLoop, calls=%fused_computation.162 | loop fusion | flops 17408 | bytes 4160 | tf_op jit(solution)/shard_map/mul | solution.py:66
  18.9 4.3 gather_fusion
  26.6 7.5 %all-to-all-start = ((bf16[16,48,2048]{2,1,0:T(8,128)(2,1)}), bf16[16,48,2048]{2,1,0:T(8,128)(2,1)}, u32[]{:S(2)}, u32[]{:S(2)}) async-start(bf16[16,48,2048]{2,1,0:T(8,128)(2,1)} %select_select_fusion.1), calls=%async_computation | async-start | bytes 6291456 | tf_op jit(solution)/shard_map/all_to_all | solution.py:123
  41.7 5.3 mul.161
  50.3 4.3 gather_fusion.3
  57.9 44.4 %collective-permute-done.8 = bf16[1,768,256]{1,2,0:T(8,128)(2,1)S(1)} collective-permute-done((bf16[1,768,256]{1,2,0:T(8,128)(2,1)S(1)}, bf16[1,768,256]{1,2,0:T(8,128)(2,1)S(1)}, u32[]{:S(2)}, u32[]{:S(2)}) %collective-permute-start.8) | collective-permute-done | bytes 393248 | tf_op jit(solution)/shard_map/ppermute | solution.py:17
  106.3 4.2 collective-permute-start.11
  118.9 10.9 %collective-permute-done.10 = bf16[1,768,256]{1,2,0:T(8,128)(2,1)S(1)} collective-permute-done((bf16[1,768,256]{1,2,0:T(8,128)(2,1)S(1)}, bf16[1,768,256]{1,2,0:T(8,128)(2,1)S(1)}, u32[]{:S(2)}, u32[]{:S(2)}) %collective-permute-start.10) | collective-permute-done | bytes 393248 | tf_op jit(solution)/shard_map/ppermute | solution.py:24
  129.8 3.5 collective-permute-done.11
  133.2 4.0 collective-permute-start.1
  137.2 5.7 collective-permute-done.12
  145.3 4.6 collective-permute-start.3
  159.7 5.4 collective-permute-done.1
  167.1 17.2 %collective-permute-done.2 = bf16[1,2,256,768]{3,2,1,0:T(8,128)(2,1)} collective-permute-done((bf16[1,2,256,768]{3,2,1,0:T(8,128)(2,1)}, bf16[1,2,256,768]{3,2,1,0:T(8,128)(2,1)}, u32[]{:S(2)}, u32[]{:S(2)}) %collective-permute-start.2) | collective-permute-done | bytes 786464 | tf_op jit(solution)/shard_map/ppermute | solution.py:24
  186.4 9.7 %collective-permute-done.3 = bf16[1,2,256,768]{3,2,1,0:T(8,128)(2,1)} collective-permute-done((bf16[1,2,256,768]{3,2,1,0:T(8,128)(2,1)}, bf16[1,2,256,768]{3,2,1,0:T(8,128)(2,1)}, u32[]{:S(2)}, u32[]{:S(2)}) %collective-permute-start.3) | collective-permute-done | bytes 786464 | tf_op jit(solution)/shard_map/ppermute | solution.py:24
  198.1 15.9 %collective-permute-done.4 = bf16[1,2,256,768]{3,2,1,0:T(8,128)(2,1)} collective-permute-done((bf16[1,2,256,768]{3,2,1,0:T(8,128)(2,1)}, bf16[1,2,256,768]{3,2,1,0:T(8,128)(2,1)}, u32[]{:S(2)}, u32[]{:S(2)}) %collective-permute-start.4) | collective-permute-done | bytes 786464 | tf_op jit(solution)/shard_map/ppermute | solution.py:24
  221.8 11.0 %collective-permute-done.7 = bf16[1,2,256,768]{3,2,1,0:T(8,128)(2,1)S(1)} collective-permute-done((bf16[1,2,256,768]{3,2,1,0:T(8,128)(2,1)}, bf16[1,2,256,768]{3,2,1,0:T(8,128)(2,1)S(1)}, u32[]{:S(2)}, u32[]{:S(2)}) %collective-permute-start.7) | collective-permute-done | bytes 786464 | tf_op jit(solution)/shard_map/ppermute | solution.py:24
  233.7 6.4 %gather_fusion.1 = bf16[8,2,256,768]{3,2,1,0:T(8,128)(2,1)} fusion(bf16[8,2,256,768]{3,2,1,0:T(8,128)(2,1)} %bitcast.29, s32[1024]{0:T(1024)S(1)} %pad_clamp_fusion.2), kind=kCustom, calls=%fused_computation.3 | custom fusion | bytes 12582944 | tf_op jit(solution)/shard_map/jit(_take)/gather | solution.py:28
  240.1 6.1 fusion.68
  254.6 5.6 all-to-all-start.2
  270.8 6.9 %fusion.4 = f32[768,768]{0,1:T(8,128)} fusion(bf16[768,2048]{1,0:T(8,128)(2,1)} %bitcast.20, bf16[1,2,2048,768]{3,2,1,0:T(8,128)(2,1)} %fusion.25), kind=kOutput, calls=%fused_computation.38 | convolution fusion | flops 2415919104 | bytes 8650752 | tf_op jit(solution)/shard_map/dot_general | solution.py:126
  277.7 6.9 %fusion.5 = f32[768,768]{0,1:T(8,128)} fusion(bf16[768,2048]{1,0:T(8,128)(2,1)} %bitcast.20, bf16[1,2,2048,768]{3,2,1,0:T(8,128)(2,1)} %fusion.25), kind=kOutput, calls=%fused_computation.39 | convolution fusion | flops 2415919104 | bytes 8650752 | tf_op jit(solution)/shard_map/dot_general | solution.py:127
  284.6 15.1 %all-to-all-done.2 = bf16[16,48,2048]{2,1,0:T(8,128)(2,1)S(1)} async-done(((bf16[16,48,2048]{2,1,0:T(8,128)(2,1)}), bf16[16,48,2048]{2,1,0:T(8,128)(2,1)S(1)}, u32[]{:S(2)}, u32[]{:S(2)}) %all-to-all-start.2) | async-done | bytes 3145760 | tf_op jit(solution)/shard_map/all_to_all | solution.py:150
  299.7 8.9 %multiply_convert_fusion.1 = (bf16[768,768]{0,1:T(8,128)(2,1)S(1)}, bf16[768,768]{0,1:T(8,128)(2,1)S(1)}, bf16[768,768]{0,1:T(8,128)(2,1)}) fusion(f32[768,768]{0,1:T(8,128)} %fusion.4, f32[768,768]{0,1:T(8,128)} %fusion.5, bf16[768,2048]{1,0:T(8,128)(2,1)S(1)} %bitcast.272, bf16[1,768,2048]{1,2,0:T(8,128)(2,1)} %copy-done.16), kind=kOutput, calls=%fused_computation.45 | convolution fusion | flops 2424766464 | bytes 14548992 | tf_op jit(solution)/shard_map/dot_general | solution.py:85
  308.6 5.6 fusion.3
  314.2 6.2 add_convert_fusion
  320.4 7.8 %all-to-all-start.3 = ((bf16[16,48,2048]{2,1,0:T(8,128)(2,1)}), bf16[16,48,2048]{2,1,0:T(8,128)(2,1)S(1)}, u32[]{:S(2)}, u32[]{:S(2)}) async-start(bf16[16,48,2048]{2,1,0:T(8,128)(2,1)} %bitcast.278), calls=%async_computation.3 | async-start | bytes 6291456 | tf_op jit(solution)/shard_map/all_to_all | solution.py:159
  328.2 4.7 copy.71
  332.8 9.1 %convolution_convert_fusion = bf16[8,256,1536]{2,1,0:T(8,128)(2,1)} fusion(bf16[8,256,768]{2,1,0:T(8,128)(2,1)} %bitcast.280, bf16[768,768]{0,1:T(8,128)(2,1)} %copy-done.21, bf16[768,768]{0,1:T(8,128)(2,1)} %copy-done.19), kind=kOutput, calls=%fused_computation.25 | convolution fusion | flops 4839702528 | bytes 11796480 | tf_op jit(solution)/shard_map/dot_general | solution.py:79
  341.9 4.7 copy.73
  346.6 5.0 convolution_convert_fusion.2
  358.1 4.3 select_bitcast_fusion.6
  365.4 67.6 %collective-permute-done.23 = bf16[256,2304]{1,0:T(8,128)(2,1)} collective-permute-done((bf16[256,2304]{1,0:T(8,128)(2,1)}, bf16[256,2304]{1,0:T(8,128)(2,1)}, u32[]{:S(2)}, u32[]{:S(2)}) %collective-permute-start.23) | collective-permute-done | bytes 1179680 | tf_op jit(solution)/shard_map/ppermute | solution.py:40
  433.0 4.1 collective-permute-start.17
  437.1 4.3 convolution_convert_fusion.1
  441.4 8.5 %all-to-all-start.1 = ((bf16[16,48,2048]{2,1,0:T(8,128)(2,1)}), bf16[16,48,2048]{2,1,0:T(8,128)(2,1)}, u32[]{:S(2)}, u32[]{:S(2)}) async-start(bf16[16,48,2048]{2,1,0:T(8,128)(2,1)} %bitcast.279), calls=%async_computation.1 | async-start | bytes 6291456 | tf_op jit(solution)/shard_map/all_to_all | solution.py:133
  465.9 20.4 %collective-permute-start.25 = (bf16[1,768,256]{1,2,0:T(8,128)(2,1)}, bf16[1,768,256]{1,2,0:T(8,128)(2,1)S(1)}, u32[]{:S(2)}, u32[]{:S(2)}) collective-permute-start(bf16[1,768,256]{1,2,0:T(8,128)(2,1)} %convert_element_type.130), channel_id=1, source_target_pairs={{64,0},{72,8},{80,16},{88,24},{96,32},{104,40},{112,48},{120,56},{... | collective-permute-start | bytes 1179656 | tf_op jit(solution)/shard_map/ppermute | solution.py:17
  488.2 33.7 %collective-permute-done.17 = bf16[256,2304]{1,0:T(8,128)(2,1)} collective-permute-done((bf16[256,2304]{1,0:T(8,128)(2,1)}, bf16[256,2304]{1,0:T(8,128)(2,1)}, u32[]{:S(2)}, u32[]{:S(2)}) %collective-permute-start.17) | collective-permute-done | bytes 1179680 | tf_op jit(solution)/shard_map/ppermute | solution.py:40
  521.8 4.9 convert_add_fusion
  528.1 35.8 %collective-permute-done.25 = bf16[1,768,256]{1,2,0:T(8,128)(2,1)S(1)} collective-permute-done((bf16[1,768,256]{1,2,0:T(8,128)(2,1)}, bf16[1,768,256]{1,2,0:T(8,128)(2,1)S(1)}, u32[]{:S(2)}, u32[]{:S(2)}) %collective-permute-start.25) | collective-permute-done | bytes 393248 | tf_op jit(solution)/shard_map/ppermute | solution.py:17
  563.9 8.4 %collective-permute-done.26 = bf16[1,768,256]{1,2,0:T(8,128)(2,1)S(1)} collective-permute-done((bf16[1,768,256]{1,2,0:T(8,128)(2,1)}, bf16[1,768,256]{1,2,0:T(8,128)(2,1)S(1)}, u32[]{:S(2)}, u32[]{:S(2)}) %collective-permute-start.26) | collective-permute-done | bytes 393248 | tf_op jit(solution)/shard_map/ppermute | solution.py:17
  580.5 4.9 subtract_convert_fusion
  585.4 3.5 gather_fusion.5
  588.9 7.7 %gather_fusion.4 = bf16[512,2048]{1,0:T(8,128)(2,1)} fusion(bf16[768,2048]{1,0:T(8,128)(2,1)} %bitcast.76, s32[1024]{0:T(1024)S(1)} %pad_clamp_fusion.1), kind=kCustom, calls=%fused_computation.clone | custom fusion | bytes 4196352 | tf_op jit(solution)/shard_map/jit(_take)/gather | solution.py:140
  596.6 4.7 broadcast_select_fusion
  601.3 5.2 reshape.328
  606.5 6.2 %multiply_reduce_fusion = bf16[128,2048]{1,0:T(8,128)(2,1)} fusion(f32[128,4,2048]{2,1,0:T(4,128)} %reshape.328, f32[128,4]{1,0:T(8,128)S(1)} %copy-done.11), kind=kLoop, calls=%fused_computation.27 | loop fusion | flops 1835008 | bytes 4720640 | tf_op jit(solution)/shard_map/reduce_sum | solution.py:143
  615.5 3.9 reduce_sum.45
  (168 shorter events, 122.1 us)
Async XLA Ops:
  0.6 18.3 %copy-start = (bf16[128,2048]{1,0:T(8,128)(2,1)S(1)}, bf16[128,2048]{1,0:T(8,128)(2,1)}, u32[]{:S(2)}) copy-start(bf16[128,2048]{1,0:T(8,128)(2,1)} %param.15) | copy-start | bytes 1572868
  14.6 8.6 %copy-start.12 = (s32[128,4]{1,0:T(8,128)}, s32[128,4]{1,0:T(8,128)S(1)}, u32[]{:S(2)}) copy-start(s32[128,4]{1,0:T(8,128)S(1)} %copy.49) | copy-start | bytes 6148
  26.6 10.4 %copy-start.14 = (bf16[1,768,256]{2,1,0:T(8,128)(2,1)S(1)}, bf16[1,768,256]{2,1,0:T(8,128)(2,1)}, u32[]{:S(2)}) copy-start(bf16[1,768,256]{2,1,0:T(8,128)(2,1)} %param.20) | copy-start | bytes 1179652
  26.6 10.8 %copy-start.15 = (s32[16]{0:T(128)S(1)}, s32[16]{0:T(128)}, u32[]{:S(2)}) copy-start(s32[16]{0:T(128)} %param.18) | copy-start | bytes 196
  26.6 12.1 %copy-start.13 = (bf16[128,2048]{1,0:T(8,128)(2,1)S(1)}, bf16[128,2048]{1,0:T(8,128)(2,1)}, u32[]{:S(2)}) copy-start(bf16[128,2048]{1,0:T(8,128)(2,1)} %param.25) | copy-start | bytes 1572868
  26.6 228.0 %all-to-all-start = ((bf16[16,48,2048]{2,1,0:T(8,128)(2,1)}), bf16[16,48,2048]{2,1,0:T(8,128)(2,1)}, u32[]{:S(2)}, u32[]{:S(2)}) async-start(bf16[16,48,2048]{2,1,0:T(8,128)(2,1)} %select_select_fusion.1), calls=%async_computation | async-start | bytes 6291456 | tf_op jit(solution)/shard_map/all_to_all | solution.py:123
  34.1 76.4 %collective-permute-start = (bf16[1,2,256,768]{3,2,1,0:T(8,128)(2,1)}, bf16[1,2,256,768]{3,2,1,0:T(8,128)(2,1)}, u32[]{:S(2)}, u32[]{:S(2)}) collective-permute-start(bf16[1,2,256,768]{3,2,1,0:T(8,128)(2,1)} %param.19), channel_id=1, source_target_pairs={{64,0},{72,8},{80,16},{88,24},{96,32},{104,40},{112,48},{120,56},{... | collective-permute-start | bytes 2359304 | tf_op jit(solution)/shard_map/ppermute | solution.py:17
  37.1 65.2 %collective-permute-start.8 = (bf16[1,768,256]{1,2,0:T(8,128)(2,1)S(1)}, bf16[1,768,256]{1,2,0:T(8,128)(2,1)S(1)}, u32[]{:S(2)}, u32[]{:S(2)}) collective-permute-start(bf16[1,768,256]{1,2,0:T(8,128)(2,1)S(1)} %copy.61), channel_id=1, source_target_pairs={{64,0},{72,8},{80,16},{88,24},{96,32},{104,40},{112,48},{120,56},{... | collective-permute-start | bytes 1179656 | tf_op jit(solution)/shard_map/ppermute | solution.py:17
  41.7 5.3 copy-start.18
  102.5 14.2 %collective-permute-start.9 = (bf16[1,768,256]{1,2,0:T(8,128)(2,1)S(1)}, bf16[1,768,256]{1,2,0:T(8,128)(2,1)S(1)}, u32[]{:S(2)}, u32[]{:S(2)}) collective-permute-start(bf16[1,768,256]{1,2,0:T(8,128)(2,1)S(1)} %get-tuple-element.46), channel_id=1, source_target_pairs={{0,1},{1,2},{2,3},{3,4},{4,5},{5,6},{6,7},{7,0},{8,9},{9,10},{10,1... | collective-permute-start | bytes 1179656 | tf_op jit(solution)/shard_map/ppermute | solution.py:24
  103.8 26.0 %collective-permute-start.10 = (bf16[1,768,256]{1,2,0:T(8,128)(2,1)S(1)}, bf16[1,768,256]{1,2,0:T(8,128)(2,1)S(1)}, u32[]{:S(2)}, u32[]{:S(2)}) collective-permute-start(bf16[1,768,256]{1,2,0:T(8,128)(2,1)S(1)} %get-tuple-element.46), channel_id=1, source_target_pairs={{0,2},{1,3},{2,4},{3,5},{4,6},{5,7},{6,0},{7,1},{8,10},{9,11},{10,... | collective-permute-start | bytes 1179656 | tf_op jit(solution)/shard_map/ppermute | solution.py:24
  106.3 26.9 %collective-permute-start.11 = (bf16[1,768,256]{1,2,0:T(8,128)(2,1)S(1)}, bf16[1,768,256]{1,2,0:T(8,128)(2,1)S(1)}, u32[]{:S(2)}, u32[]{:S(2)}) collective-permute-start(bf16[1,768,256]{1,2,0:T(8,128)(2,1)S(1)} %get-tuple-element.46), channel_id=1, source_target_pairs={{0,3},{1,4},{2,5},{3,6},{4,7},{5,0},{6,1},{7,2},{8,11},{9,12},{10,... | collective-permute-start | bytes 1179656 | tf_op jit(solution)/shard_map/ppermute | solution.py:24
  110.5 32.5 %collective-permute-start.12 = (bf16[1,768,256]{1,2,0:T(8,128)(2,1)S(1)}, bf16[1,768,256]{1,2,0:T(8,128)(2,1)S(1)}, u32[]{:S(2)}, u32[]{:S(2)}) collective-permute-start(bf16[1,768,256]{1,2,0:T(8,128)(2,1)S(1)} %get-tuple-element.46), channel_id=1, source_target_pairs={{0,4},{1,5},{2,6},{3,7},{4,0},{5,1},{6,2},{7,3},{8,12},{9,13},{10,... | collective-permute-start | bytes 1179656 | tf_op jit(solution)/shard_map/ppermute | solution.py:24
  110.5 34.8 %collective-permute-start.13 = (bf16[1,768,256]{1,2,0:T(8,128)(2,1)S(1)}, bf16[1,768,256]{1,2,0:T(8,128)(2,1)S(1)}, u32[]{:S(2)}, u32[]{:S(2)}) collective-permute-start(bf16[1,768,256]{1,2,0:T(8,128)(2,1)S(1)} %get-tuple-element.46), channel_id=1, source_target_pairs={{0,5},{1,6},{2,7},{3,0},{4,1},{5,2},{6,3},{7,4},{8,13},{9,14},{10,... | collective-permute-start | bytes 1179656 | tf_op jit(solution)/shard_map/ppermute | solution.py:24
  116.7 33.3 %collective-permute-start.14 = (bf16[1,768,256]{1,2,0:T(8,128)(2,1)S(1)}, bf16[1,768,256]{1,2,0:T(8,128)(2,1)S(1)}, u32[]{:S(2)}, u32[]{:S(2)}) collective-permute-start(bf16[1,768,256]{1,2,0:T(8,128)(2,1)S(1)} %get-tuple-element.46), channel_id=1, source_target_pairs={{0,6},{1,7},{2,0},{3,1},{4,2},{5,3},{6,4},{7,5},{8,14},{9,15},{10,... | collective-permute-start | bytes 1179656 | tf_op jit(solution)/shard_map/ppermute | solution.py:24
  129.7 20.9 %collective-permute-start.15 = (bf16[1,768,256]{1,2,0:T(8,128)(2,1)S(1)}, bf16[1,768,256]{1,2,0:T(8,128)(2,1)S(1)}, u32[]{:S(2)}, u32[]{:S(2)}) collective-permute-start(bf16[1,768,256]{1,2,0:T(8,128)(2,1)S(1)} %get-tuple-element.46), channel_id=1, source_target_pairs={{0,7},{1,0},{2,1},{3,2},{4,3},{5,4},{6,5},{7,6},{8,15},{9,8},{10,9... | collective-permute-start | bytes 1179656 | tf_op jit(solution)/shard_map/ppermute | solution.py:24
  133.2 31.8 %collective-permute-start.1 = (bf16[1,2,256,768]{3,2,1,0:T(8,128)(2,1)}, bf16[1,2,256,768]{3,2,1,0:T(8,128)(2,1)}, u32[]{:S(2)}, u32[]{:S(2)}) collective-permute-start(bf16[1,2,256,768]{3,2,1,0:T(8,128)(2,1)} %get-tuple-element.48), channel_id=1, source_target_pairs={{0,1},{1,2},{2,3},{3,4},{4,5},{5,6},{6,7},{7,0},{8,9},{9,10},{10,1... | collective-permute-start | bytes 2359304 | tf_op jit(solution)/shard_map/ppermute | solution.py:24
  143.0 41.3 %collective-permute-start.2 = (bf16[1,2,256,768]{3,2,1,0:T(8,128)(2,1)}, bf16[1,2,256,768]{3,2,1,0:T(8,128)(2,1)}, u32[]{:S(2)}, u32[]{:S(2)}) collective-permute-start(bf16[1,2,256,768]{3,2,1,0:T(8,128)(2,1)} %get-tuple-element.48), channel_id=1, source_target_pairs={{0,2},{1,3},{2,4},{3,5},{4,6},{5,7},{6,0},{7,1},{8,10},{9,11},{10,... | collective-permute-start | bytes 2359304 | tf_op jit(solution)/shard_map/ppermute | solution.py:24
  145.3 50.7 %collective-permute-start.3 = (bf16[1,2,256,768]{3,2,1,0:T(8,128)(2,1)}, bf16[1,2,256,768]{3,2,1,0:T(8,128)(2,1)}, u32[]{:S(2)}, u32[]{:S(2)}) collective-permute-start(bf16[1,2,256,768]{3,2,1,0:T(8,128)(2,1)} %get-tuple-element.48), channel_id=1, source_target_pairs={{0,3},{1,4},{2,5},{3,6},{4,7},{5,0},{6,1},{7,2},{8,11},{9,12},{10,... | collective-permute-start | bytes 2359304 | tf_op jit(solution)/shard_map/ppermute | solution.py:24
  150.0 64.1 %collective-permute-start.4 = (bf16[1,2,256,768]{3,2,1,0:T(8,128)(2,1)}, bf16[1,2,256,768]{3,2,1,0:T(8,128)(2,1)}, u32[]{:S(2)}, u32[]{:S(2)}) collective-permute-start(bf16[1,2,256,768]{3,2,1,0:T(8,128)(2,1)} %get-tuple-element.48), channel_id=1, source_target_pairs={{0,4},{1,5},{2,6},{3,7},{4,0},{5,1},{6,2},{7,3},{8,12},{9,13},{10,... | collective-permute-start | bytes 2359304 | tf_op jit(solution)/shard_map/ppermute | solution.py:24
  150.6 65.5 %collective-permute-start.5 = (bf16[1,2,256,768]{3,2,1,0:T(8,128)(2,1)}, bf16[1,2,256,768]{3,2,1,0:T(8,128)(2,1)}, u32[]{:S(2)}, u32[]{:S(2)}) collective-permute-start(bf16[1,2,256,768]{3,2,1,0:T(8,128)(2,1)} %get-tuple-element.48), channel_id=1, source_target_pairs={{0,5},{1,6},{2,7},{3,0},{4,1},{5,2},{6,3},{7,4},{8,13},{9,14},{10,... | collective-permute-start | bytes 2359304 | tf_op jit(solution)/shard_map/ppermute | solution.py:24
  165.1 55.7 %collective-permute-start.6 = (bf16[1,2,256,768]{3,2,1,0:T(8,128)(2,1)}, bf16[1,2,256,768]{3,2,1,0:T(8,128)(2,1)S(1)}, u32[]{:S(2)}, u32[]{:S(2)}) collective-permute-start(bf16[1,2,256,768]{3,2,1,0:T(8,128)(2,1)} %get-tuple-element.48), channel_id=1, source_target_pairs={{0,6},{1,7},{2,0},{3,1},{4,2},{5,3},{6,4},{7,5},{8,14},{9,15},{10,... | collective-permute-start | bytes 2359304 | tf_op jit(solution)/shard_map/ppermute | solution.py:24
  184.3 48.5 %collective-permute-start.7 = (bf16[1,2,256,768]{3,2,1,0:T(8,128)(2,1)}, bf16[1,2,256,768]{3,2,1,0:T(8,128)(2,1)S(1)}, u32[]{:S(2)}, u32[]{:S(2)}) collective-permute-start(bf16[1,2,256,768]{3,2,1,0:T(8,128)(2,1)} %get-tuple-element.48), channel_id=1, source_target_pairs={{0,7},{1,0},{2,1},{3,2},{4,3},{5,4},{6,5},{7,6},{8,15},{9,8},{10,9... | collective-permute-start | bytes 2359304 | tf_op jit(solution)/shard_map/ppermute | solution.py:24
  254.6 45.1 %all-to-all-start.2 = ((bf16[16,48,2048]{2,1,0:T(8,128)(2,1)}), bf16[16,48,2048]{2,1,0:T(8,128)(2,1)S(1)}, u32[]{:S(2)}, u32[]{:S(2)}) async-start(bf16[16,48,2048]{2,1,0:T(8,128)(2,1)} %select_select_fusion), calls=%async_computation.2 | async-start | bytes 6291456 | tf_op jit(solution)/shard_map/all_to_all | solution.py:150
  299.7 8.9 %copy-start.4 = (bf16[16,48,2048]{2,1,0:T(8,128)(2,1)}, bf16[16,48,2048]{2,1,0:T(8,128)(2,1)S(1)}, u32[]{:S(2)}) copy-start(bf16[16,48,2048]{2,1,0:T(8,128)(2,1)S(1)} %all-to-all-done.2) | copy-start | bytes 9437188
  308.6 5.6 copy-start.19
  308.6 5.6 copy-start.21
  320.4 121.0 %all-to-all-start.3 = ((bf16[16,48,2048]{2,1,0:T(8,128)(2,1)}), bf16[16,48,2048]{2,1,0:T(8,128)(2,1)S(1)}, u32[]{:S(2)}, u32[]{:S(2)}) async-start(bf16[16,48,2048]{2,1,0:T(8,128)(2,1)} %bitcast.278), calls=%async_computation.3 | async-start | bytes 6291456 | tf_op jit(solution)/shard_map/all_to_all | solution.py:159
  346.6 5.0 copy-start.2
  354.5 78.5 %collective-permute-start.23 = (bf16[256,2304]{1,0:T(8,128)(2,1)}, bf16[256,2304]{1,0:T(8,128)(2,1)}, u32[]{:S(2)}, u32[]{:S(2)}) collective-permute-start(bf16[256,2304]{1,0:T(8,128)(2,1)} %get-tuple-element.55), channel_id=1, source_target_pairs={{0,7},{1,0},{2,1},{3,2},{4,3},{5,4},{6,5},{7,6},{8,15},{9,8},{10,9... | collective-permute-start | bytes 3538952 | tf_op jit(solution)/shard_map/ppermute | solution.py:40
  354.5 78.5 %collective-permute-start.22 = (bf16[256,2304]{1,0:T(8,128)(2,1)}, bf16[256,2304]{1,0:T(8,128)(2,1)}, u32[]{:S(2)}, u32[]{:S(2)}) collective-permute-start(bf16[256,2304]{1,0:T(8,128)(2,1)} %get-tuple-element.54), channel_id=1, source_target_pairs={{0,6},{1,7},{2,0},{3,1},{4,2},{5,3},{6,4},{7,5},{8,14},{9,15},{10,... | collective-permute-start | bytes 3538952 | tf_op jit(solution)/shard_map/ppermute | solution.py:40
  357.0 80.2 %copy-start.17 = (bf16[1,768,2048]{1,2,0:T(8,128)(2,1)S(1)}, bf16[1,768,2048]{1,2,0:T(8,128)(2,1)}, u32[]{:S(2)}) copy-start(bf16[1,768,2048]{1,2,0:T(8,128)(2,1)} %copy-done.16) | copy-start | bytes 9437188
  357.0 80.2 %copy-start.20 = (bf16[768,768]{0,1:T(8,128)(2,1)S(1)}, bf16[768,768]{0,1:T(8,128)(2,1)}, u32[]{:S(2)}) copy-start(bf16[768,768]{0,1:T(8,128)(2,1)} %get-tuple-element.58) | copy-start | bytes 3538948
  357.0 105.9 %collective-permute-start.21 = (bf16[256,2304]{1,0:T(8,128)(2,1)}, bf16[256,2304]{1,0:T(8,128)(2,1)}, u32[]{:S(2)}, u32[]{:S(2)}) collective-permute-start(bf16[256,2304]{1,0:T(8,128)(2,1)} %get-tuple-element.53), channel_id=1, source_target_pairs={{0,5},{1,6},{2,7},{3,0},{4,1},{5,2},{6,3},{7,4},{8,13},{9,14},{10,... | collective-permute-start | bytes 3538952 | tf_op jit(solution)/shard_map/ppermute | solution.py:40
  362.3 103.5 %collective-permute-start.20 = (bf16[256,2304]{1,0:T(8,128)(2,1)}, bf16[256,2304]{1,0:T(8,128)(2,1)}, u32[]{:S(2)}, u32[]{:S(2)}) collective-permute-start(bf16[256,2304]{1,0:T(8,128)(2,1)} %get-tuple-element.52), channel_id=1, source_target_pairs={{0,4},{1,5},{2,6},{3,7},{4,0},{5,1},{6,2},{7,3},{8,12},{9,13},{10,... | collective-permute-start | bytes 3538952 | tf_op jit(solution)/shard_map/ppermute | solution.py:40
  363.0 102.9 %collective-permute-start.19 = (bf16[256,2304]{1,0:T(8,128)(2,1)}, bf16[256,2304]{1,0:T(8,128)(2,1)}, u32[]{:S(2)}, u32[]{:S(2)}) collective-permute-start(bf16[256,2304]{1,0:T(8,128)(2,1)} %get-tuple-element.51), channel_id=1, source_target_pairs={{0,3},{1,4},{2,5},{3,6},{4,7},{5,0},{6,1},{7,2},{8,11},{9,12},{10,... | collective-permute-start | bytes 3538952 | tf_op jit(solution)/shard_map/ppermute | solution.py:40
  433.0 55.1 %collective-permute-start.18 = (bf16[256,2304]{1,0:T(8,128)(2,1)}, bf16[256,2304]{1,0:T(8,128)(2,1)}, u32[]{:S(2)}, u32[]{:S(2)}) collective-permute-start(bf16[256,2304]{1,0:T(8,128)(2,1)} %get-tuple-element.50), channel_id=1, source_target_pairs={{0,2},{1,3},{2,4},{3,5},{4,6},{5,7},{6,0},{7,1},{8,10},{9,11},{10,... | collective-permute-start | bytes 3538952 | tf_op jit(solution)/shard_map/ppermute | solution.py:40
  433.0 88.8 %collective-permute-start.17 = (bf16[256,2304]{1,0:T(8,128)(2,1)}, bf16[256,2304]{1,0:T(8,128)(2,1)}, u32[]{:S(2)}, u32[]{:S(2)}) collective-permute-start(bf16[256,2304]{1,0:T(8,128)(2,1)} %get-tuple-element.49), channel_id=1, source_target_pairs={{0,1},{1,2},{2,3},{3,4},{4,5},{5,6},{6,7},{7,0},{8,9},{9,10},{10,1... | collective-permute-start | bytes 3538952 | tf_op jit(solution)/shard_map/ppermute | solution.py:40
  441.4 147.4 %all-to-all-start.1 = ((bf16[16,48,2048]{2,1,0:T(8,128)(2,1)}), bf16[16,48,2048]{2,1,0:T(8,128)(2,1)}, u32[]{:S(2)}, u32[]{:S(2)}) async-start(bf16[16,48,2048]{2,1,0:T(8,128)(2,1)} %bitcast.279), calls=%async_computation.1 | async-start | bytes 6291456 | tf_op jit(solution)/shard_map/all_to_all | solution.py:133
  462.8 117.7 %collective-permute-start.16 = (bf16[1,2,256,768]{3,2,1,0:T(8,128)(2,1)}, bf16[1,2,256,768]{3,2,1,0:T(8,128)(2,1)}, u32[]{:S(2)}, u32[]{:S(2)}) collective-permute-start(bf16[1,2,256,768]{3,2,1,0:T(8,128)(2,1)} %convert_element_type.116), channel_id=1, source_target_pairs={{64,0},{72,8},{80,16},{88,24},{96,32},{104,40},{112,48},{120,56},{... | collective-permute-start | bytes 2359304 | tf_op jit(solution)/shard_map/ppermute | solution.py:17
  465.8 114.7 %collective-permute-start.24 = (bf16[1,2,256,768]{3,2,1,0:T(8,128)(2,1)}, bf16[1,2,256,768]{3,2,1,0:T(8,128)(2,1)}, u32[]{:S(2)}, u32[]{:S(2)}) collective-permute-start(bf16[1,2,256,768]{3,2,1,0:T(8,128)(2,1)} %convert_element_type.126), channel_id=1, source_target_pairs={{64,0},{72,8},{80,16},{88,24},{96,32},{104,40},{112,48},{120,56},{... | collective-permute-start | bytes 2359304 | tf_op jit(solution)/shard_map/ppermute | solution.py:17
  465.9 98.0 %collective-permute-start.25 = (bf16[1,768,256]{1,2,0:T(8,128)(2,1)}, bf16[1,768,256]{1,2,0:T(8,128)(2,1)S(1)}, u32[]{:S(2)}, u32[]{:S(2)}) collective-permute-start(bf16[1,768,256]{1,2,0:T(8,128)(2,1)} %convert_element_type.130), channel_id=1, source_target_pairs={{64,0},{72,8},{80,16},{88,24},{96,32},{104,40},{112,48},{120,56},{... | collective-permute-start | bytes 1179656 | tf_op jit(solution)/shard_map/ppermute | solution.py:17
  488.2 84.2 %collective-permute-start.26 = (bf16[1,768,256]{1,2,0:T(8,128)(2,1)}, bf16[1,768,256]{1,2,0:T(8,128)(2,1)S(1)}, u32[]{:S(2)}, u32[]{:S(2)}) collective-permute-start(bf16[1,768,256]{1,2,0:T(8,128)(2,1)} %convert_element_type.132), channel_id=1, source_target_pairs={{64,0},{72,8},{80,16},{88,24},{96,32},{104,40},{112,48},{120,56},{... | collective-permute-start | bytes 1179656 | tf_op jit(solution)/shard_map/ppermute | solution.py:17
  526.7 45.6 %copy-start.6 = (f32[1,768,256]{1,2,0:T(8,128)S(1)}, f32[1,768,256]{1,2,0:T(8,128)}, u32[]{:S(2)}) copy-start(f32[1,768,256]{1,2,0:T(8,128)} %copy.76) | copy-start | bytes 2359300
  526.8 45.6 %copy-start.7 = (f32[1,768,256]{1,2,0:T(8,128)S(1)}, f32[1,768,256]{1,2,0:T(8,128)}, u32[]{:S(2)}) copy-start(f32[1,768,256]{1,2,0:T(8,128)} %copy.78) | copy-start | bytes 2359300
  588.9 7.7 %copy-start.5 = (bf16[512,2048]{1,0:T(8,128)(2,1)S(1)}, bf16[512,2048]{1,0:T(8,128)(2,1)}, u32[]{:S(2)}) copy-start(bf16[512,2048]{1,0:T(8,128)(2,1)} %gather_fusion.5) | copy-start | bytes 6291460
  601.3 5.2 copy-start.11
  612.7 6.7 %copy-start.1 = (bf16[128,2048]{1,0:T(8,128)(2,1)S(1)}, bf16[128,2048]{1,0:T(8,128)(2,1)}, u32[]{:S(2)}) copy-start(bf16[128,2048]{1,0:T(8,128)(2,1)} %param.15) | copy-start | bytes 1572868
  (5 other events, 9.3 us)

commit v3 on v1

--- a/solution.py
+++ b/solution.py
@@ -1,7 +1,10 @@
 import jax
 import jax.numpy as jnp
 from jax import lax
+from jax.experimental import pallas as pl
+from jax.experimental.pallas import tpu as pltpu
 from jax.sharding import PartitionSpec as P
+import functools
 
 beta_first = 0.9
 beta_second = 0.999
@@ -15,6 +18,64 @@
     devices = range(lax.axis_size(axis))
     route = [((i - distance) % len(devices), i) for i in devices]
     return lax.ppermute(block, axis, route)
+
+
+def exchange_kernel(count, spread, width, *refs):
+    sources, targets = refs[:width], refs[width : 2 * width]
+    send_sems, recv_sems, local_sems = refs[2 * width :]
+    me = lax.axis_index("shard")
+    row = lax.axis_index("expert")
+    mesh_ids = pl.DeviceIdType.MESH
+    barrier = pltpu.get_barrier_semaphore()
+    for k in range(1, count):
+        pl.semaphore_signal(
+            barrier, inc=1, device_id=(row, lax.rem(me + k, count)), device_id_type=mesh_ids
+        )
+    pl.semaphore_wait(barrier, count - 1)
+    copies = []
+    for a in range(width):
+        own = sources[a] if spread else sources[a].at[me]
+        local = pltpu.make_async_copy(own, targets[a].at[me], local_sems.at[a])
+        local.start()
+        copies.append(local)
+        for k in range(1, count):
+            peer = lax.rem(me + k, count)
+            remote = pltpu.make_async_remote_copy(
+                src_ref=sources[a] if spread else sources[a].at[peer],
+                dst_ref=targets[a].at[me],
+                send_sem=send_sems.at[a, k - 1],
+                recv_sem=recv_sems.at[a, k - 1],
+                device_id=(row, peer),
+                device_id_type=mesh_ids,
+            )
+            remote.start()
+            copies.append(remote)
+    for copy in copies:
+        copy.wait()
+
+
+def exchange(blocks, spread, ident):
+    count = lax.axis_size("shard")
+    width = len(blocks)
+    shapes = tuple(
+        jax.ShapeDtypeStruct((count,) + b.shape if spread else b.shape, b.dtype) for b in blocks
+    )
+    moved = sum(b.size * b.dtype.itemsize for b in blocks)
+    return pl.pallas_call(
+        functools.partial(exchange_kernel, count, spread, width),
+        out_shape=shapes,
+        in_specs=[pl.BlockSpec(memory_space=pl.ANY)] * width,
+        out_specs=tuple(pl.BlockSpec(memory_space=pl.ANY) for _ in blocks),
+        scratch_shapes=[
+            pltpu.SemaphoreType.DMA((width, count - 1)),
+            pltpu.SemaphoreType.DMA((width, count - 1)),
+            pltpu.SemaphoreType.DMA((width,)),
+        ],
+        compiler_params=pltpu.CompilerParams(collective_id=ident, has_side_effects=True),
+        cost_estimate=pl.CostEstimate(
+            flops=0, transcendentals=0, bytes_accessed=2 * moved * (count if spread else 1)
+        ),
+    )(*blocks)
 
 
 def silu_parts(gate_pre):
@@ -86,13 +147,10 @@
         jnp.where(take_other, moved, owned)
         for moved, owned in zip(moved_states, (m_in, v_in, m_down, v_down))
     )
-    in_full, down_full = (
-        lax.all_gather(w_in, "shard", axis=2, tiled=True),
-        lax.all_gather(w_down, "shard", axis=2, tiled=True),
-    )
-    gate_weight = in_full[0, 0]
-    up_weight = in_full[0, 1]
-    down_weight = down_full[0]
+    gate_parts, up_parts, down_parts = exchange((w_in[0, 0], w_in[0, 1], w_down[0]), True, 0)
+    gate_weight = gate_parts.reshape(-1, gate_parts.shape[-1])
+    up_weight = up_parts.reshape(-1, up_parts.shape[-1])
+    down_weight = jnp.transpose(down_parts, (1, 0, 2)).reshape(down_parts.shape[1], -1)
     hidden_width = gate_weight.shape[1]
     position, filler = route_table(expert_ids, partner[expert_ids], groups, capacity)
     token_fill = jnp.where(filler >= 0, filler // top_count, -1)
@@ -146,14 +204,14 @@
     token_grad = jnp.sum(per_back.astype(jnp.float32), axis=1).astype(jnp.bfloat16)
     grad_both = jnp.concatenate([grad_gate, grad_up], axis=1)
     share_rows = width // lax.axis_size("shard")
-    shares = lax.psum_scatter(
-        jnp.concatenate(
-            [contract_rows(rows_x, grad_both), contract_rows(dout_rows, hidden)], axis=1
-        ).astype(jnp.bfloat16),
-        "shard",
-        scatter_dimension=0,
-        tiled=True,
-    ).astype(jnp.float32)
+    partial = jnp.concatenate(
+        [contract_rows(rows_x, grad_both), contract_rows(dout_rows, hidden)], axis=1
+    ).astype(jnp.bfloat16)
+    shard_count = lax.axis_size("shard")
+    (arrived_parts,) = exchange(
+        (partial.reshape(shard_count, share_rows, partial.shape[1]),), False, 1
+    )
+    shares = jnp.sum(arrived_parts.astype(jnp.float32), axis=0)
     grad_in = jnp.transpose(
         shares[:, : 2 * hidden_width].reshape(share_rows, 2, hidden_width), (1, 0, 2)
     )[None]

time: 467 us -> 638 us (1.37)
  Pallas kernels: 0 us -> 299 us
  waiting for transfers between devices: 250 us -> 112 us
  local copies, waits for them, and re-layouts: 45.1 us -> 72 us
  between operations: 15.1 us -> 1.81 us
    pallas_call x0 -> x2, Pallas kernels: none -> 299 us  [exchange(): pl.pallas_call(functools.partial(exchange_kernel, count, spread, width),...]
    reduce_scatter x1 -> x0, waiting for transfers between devices: 50.9 us -> none  [body(): lax.psum_scatter(jnp.concatenate([contract_rows(rows_x, grad_both), contr...]
    all_gather x2 -> x0, waiting for transfers between devices: 46.9 us -> none  [the longest x1 46.9 us: body(): lax.all_gather(w_in, 'shard', axis=2, tiled=True)]
    ppermute x6, waiting for transfers between devices: 23.2 us -> 64.1 us  [shifted(): return lax.ppermute(block, axis, route)]
    all_to_all x1, waiting for transfers between devices: 32.5 us -> 0.01 us  [body(): lax.all_to_all(send_rows, 'expert', split_axis=0, concat_axis=0, tiled=True)]
    all_to_all x1, waiting for transfers between devices: 30.1 us -> 0.01 us  [body(): lax.all_to_all(expert_out.reshape(groups, capacity, width), 'expert', spl...]
    all_to_all x1, waiting for transfers between devices: 33.8 us -> 16.2 us  [body(): lax.all_to_all(entry_grads.reshape(groups, capacity, width), 'expert', sp...]
    dot_general x0 -> x2, local copies, waits for them, and re-layouts: none -> 9.37 us  [contract_rows(): lax.dot_general(left, right, (((0,), (0,)), ((), ())), preferred_element_...]
  transfers between devices with their start and end apart: 13 -> 10, of which waited for: 8 -> 3; matrix products, arithmetic and copies ran while one was open for 25% -> 14% of each run, Pallas kernels for 0% -> 47%
where the time goes in v3:
time: 638 us; the launch traced here: 630 us
  Pallas kernels  299 us (47%)
  waiting for transfers between devices  112 us (18%)
  local copies, waits for them, and re-layouts  72 us (11%)
  other arithmetic  61.6 us (10%)
  matrix products  45 us (7%)
  starting transfers between devices  38.3 us (6%)
    pallas_call x2, Pallas kernels, exchange(): pl.pallas_call(functools.partial(exchange_kernel, count, spread, width),...  299 us
    ppermute x6, waiting for transfers between devices, shifted(): return lax.ppermute(block, axis, route)  64.1 us
    all_to_all x1, waiting for transfers between devices, body(): lax.all_to_all(send_grads, 'expert', split_axis=0, concat_axis=0, tiled=T...  31.8 us
    all_to_all x1, waiting for transfers between devices, body(): lax.all_to_all(entry_grads.reshape(groups, capacity, width), 'expert', sp...  16.2 us
    dot_general x2, matrix products, contract_rows(): lax.dot_general(left, right, (((0,), (0,)), ((), ())), preferred_element_...  14.1 us
    dot_general x3, matrix products, contract_cols(): lax.dot_general(left, right, (((1,), (1,)), ((), ())), preferred_element_...  14 us
  transfers between devices with their start and end apart: 10, of which 3 were waited for; matrix products, arithmetic and copies ran while one was open for 14% of the time, Pallas kernels for 47%

profile of v3, /device:TPU:1, one launch (start us, length us, event | category | flops | bytes accessed | tf_op | source)
XLA Modules:
  0.0 629.7 jit_solution(8570237438119971711)
XLA Ops:
  1.7 2.0 fusion.22
  3.7 11.0 %select_multiply_fusion = s32[128,4]{0,1:T(4,128)S(1)} fusion(s32[128,4]{0,1:T(4,128)} %param.14, s32[]{:T(128)} %bitcast, s32[]{:T(128)} %bitcast.1, s32[]{:T(128)} %bitcast.2, s32[]{:T(128)} %bitcast.3, s32[]{:T(128)} %bitcast.4, s32[]{:T(128)} %bitcast.5, s32[]{:T(128)} %bitcast.6, s32[]{:T(128)} %bitcast.7, s32[]{:T(128)} %bitcast.8, s32[]{:T(128)} %bitcast.9, ...), kind=kLoop, calls=%fused_computation.66 | loop fusion | flops 17408 | bytes 4160 | tf_op jit(solution)/shard_map/mul | solution.py:101
  16.4 2.4 scatter_custom_fusion
  18.9 4.2 mul.160
  23.1 5.3 mul.161
  29.2 2.5 multiply_convert_fusion
  31.7 4.2 gather_fusion.1
  36.0 3.3 select_select_fusion
  39.3 7.3 %all-to-all-start.2 = ((bf16[16,48,2048]{2,1,0:T(8,128)(2,1)}), bf16[16,48,2048]{2,1,0:T(8,128)(2,1)}, u32[]{:S(2)}, u32[]{:S(2)}) async-start(bf16[16,48,2048]{2,1,0:T(8,128)(2,1)} %select_select_fusion), calls=%async_computation.2 | async-start | bytes 6291456 | tf_op jit(solution)/shard_map/all_to_all | solution.py:185
  46.8 4.3 gather_fusion
  51.1 3.3 select_select_fusion.1
  54.4 31.8 %all-to-all-done.2 = bf16[16,48,2048]{2,1,0:T(8,128)(2,1)} async-done(((bf16[16,48,2048]{2,1,0:T(8,128)(2,1)}), bf16[16,48,2048]{2,1,0:T(8,128)(2,1)}, u32[]{:S(2)}, u32[]{:S(2)}) %all-to-all-start.2) | async-done | bytes 3145760 | tf_op jit(solution)/shard_map/all_to_all | solution.py:185
  86.2 8.2 %all-to-all-start = ((bf16[16,48,2048]{2,1,0:T(8,128)(2,1)}), bf16[16,48,2048]{2,1,0:T(8,128)(2,1)S(1)}, u32[]{:S(2)}, u32[]{:S(2)}) async-start(bf16[16,48,2048]{2,1,0:T(8,128)(2,1)} %select_select_fusion.1), calls=%async_computation | async-start | bytes 6291456 | tf_op jit(solution)/shard_map/all_to_all | solution.py:158
  94.4 2.9 collective-permute-start
  98.7 64.1 %collective-permute-done.1 = bf16[1,768,256]{2,1,0:T(8,128)(2,1)} collective-permute-done((bf16[1,768,256]{2,1,0:T(8,128)(2,1)S(1)}, bf16[1,768,256]{2,1,0:T(8,128)(2,1)}, u32[]{:S(2)}, u32[]{:S(2)}) %collective-permute-start.1) | collective-permute-done | bytes 393248 | tf_op jit(solution)/shard_map/ppermute | solution.py:20
  167.6 138.8 %shard_map.170 = (bf16[8,256,768]{2,1,0:T(8,128)(2,1)}, bf16[8,256,768]{2,1,0:T(8,128)(2,1)}, bf16[8,768,256]{2,1,0:T(8,128)(2,1)}) custom-call(bf16[256,768]{1,0:T(8,128)(2,1)} %get-tuple-element.27.refs_0_, bf16[256,768]{1,0:T(8,128)(2,1)} %get-tuple-element.26.refs_1_, bf16[768,256]{1,0:T(8,128)(2,1)} %fusion.8.refs_2_), custom_call_target="tpu_custom_call" | custom-call | bytes 18874368 | tf_op jit(solution)/shard_map/pallas_call | solution.py:64
  306.4 4.8 copy.57
  311.3 6.9 %fusion.24 = f32[768,768]{0,1:T(8,128)} fusion(bf16[768,2048]{1,0:T(8,128)(2,1)} %bitcast.31, bf16[768,2048]{0,1:T(8,128)(2,1)} %bitcast.120), kind=kOutput, calls=%fused_computation.81 | convolution fusion | flops 2415919104 | bytes 8650752 | tf_op jit(solution)/shard_map/dot_general | solution.py:120
  318.2 5.7 fusion.23
  323.9 4.5 multiply_convert_fusion.1
  328.5 2.7 fusion.25
  331.2 4.5 add_convert_fusion
  335.7 5.3 all-to-all-start.3
  341.0 2.5 convert_element_type.95
  343.6 2.9 collective-permute-start.2
  348.3 2.9 collective-permute-start.4
  353.0 4.7 copy.59
  357.8 6.6 %convolution_convert_fusion.1 = bf16[768,2048]{1,0:T(8,128)(2,1)} fusion(bf16[768,768]{0,1:T(8,128)(2,1)} %get-tuple-element.25, bf16[768,2048]{0,1:T(8,128)(2,1)} %bitcast.121), kind=kOutput, calls=%fused_computation.11 | convolution fusion | flops 2417491968 | bytes 7471104 | tf_op jit(solution)/shard_map/dot_general | solution.py:165
  364.4 16.2 %all-to-all-done.3 = bf16[16,48,2048]{2,1,0:T(8,128)(2,1)S(1)} async-done(((bf16[16,48,2048]{2,1,0:T(8,128)(2,1)}), bf16[16,48,2048]{2,1,0:T(8,128)(2,1)S(1)}, u32[]{:S(2)}, u32[]{:S(2)}) %all-to-all-start.3) | async-done | bytes 3145760 | tf_op jit(solution)/shard_map/all_to_all | solution.py:194
  380.5 8.5 %all-to-all-start.1 = ((bf16[16,48,2048]{2,1,0:T(8,128)(2,1)}), bf16[16,48,2048]{2,1,0:T(8,128)(2,1)}, u32[]{:S(2)}, u32[]{:S(2)}) async-start(bf16[16,48,2048]{2,1,0:T(8,128)(2,1)} %bitcast.119), calls=%async_computation.1 | async-start | bytes 6291456 | tf_op jit(solution)/shard_map/all_to_all | solution.py:168
  389.0 9.1 %convolution_convert_fusion = bf16[8,256,1536]{2,1,0:T(8,128)(2,1)} fusion(bf16[8,256,768]{2,1,0:T(8,128)(2,1)} %bitcast.123, bf16[768,768]{0,1:T(8,128)(2,1)} %copy-done.23, bf16[768,768]{0,1:T(8,128)(2,1)} %copy-done.21), kind=kOutput, calls=%fused_computation.8 | convolution fusion | flops 4839702528 | bytes 11796480 | tf_op jit(solution)/shard_map/dot_general | solution.py:114
  398.1 4.6 copy.61
  402.7 5.0 convolution_convert_fusion.2
  407.7 3.9 pad_maximum_fusion.refs_0_
  411.7 160.2 %shard_map.171 = bf16[8,256,2304]{2,1,0:T(8,128)(2,1)} custom-call(bf16[8,256,2304]{2,1,0:T(8,128)(2,1)} %pad_maximum_fusion.refs_0_), custom_call_target="tpu_custom_call" | custom-call | bytes 18874368 | tf_op jit(solution)/shard_map/pallas_call | solution.py:64
  571.9 5.2 convert_reduce_fusion
  579.4 3.0 copy.63
  582.4 3.0 copy.64
  585.4 2.3 copy.70
  587.7 3.4 subtract_convert_fusion.1
  591.3 4.2 subtract_convert_fusion
  595.6 3.3 gather_fusion.3
  598.8 7.9 %gather_fusion.2 = bf16[512,2048]{1,0:T(8,128)(2,1)} fusion(bf16[768,2048]{1,0:T(8,128)(2,1)} %bitcast.29, s32[1024]{0:T(1024)S(1)} %pad_clamp_fusion.1), kind=kCustom, calls=%fused_computation.clone | custom fusion | bytes 4196352 | tf_op jit(solution)/shard_map/jit(_take)/gather | solution.py:175
  606.7 4.6 broadcast_select_fusion
  611.4 5.3 reshape.170
  616.6 6.2 multiply_reduce_fusion
  622.8 2.8 reshape.168
  625.6 3.9 reduce_sum.54
  (92 shorter events, 15.6 us)
Async XLA Ops:
  0.6 46.2 %copy-start = (bf16[128,2048]{1,0:T(8,128)(2,1)S(1)}, bf16[128,2048]{1,0:T(8,128)(2,1)}, u32[]{:S(2)}) copy-start(bf16[128,2048]{1,0:T(8,128)(2,1)} %param.13) | copy-start | bytes 1572868
  14.8 8.4 %copy-start.16 = (s32[128,4]{1,0:T(8,128)}, s32[128,4]{1,0:T(8,128)S(1)}, u32[]{:S(2)}) copy-start(s32[128,4]{1,0:T(8,128)S(1)} %copy.52) | copy-start | bytes 6148
  23.1 5.3 copy-start.18
  28.5 0.6 copy-start.14
  39.3 46.9 %all-to-all-start.2 = ((bf16[16,48,2048]{2,1,0:T(8,128)(2,1)}), bf16[16,48,2048]{2,1,0:T(8,128)(2,1)}, u32[]{:S(2)}, u32[]{:S(2)}) async-start(bf16[16,48,2048]{2,1,0:T(8,128)(2,1)} %select_select_fusion), calls=%async_computation.2 | async-start | bytes 6291456 | tf_op jit(solution)/shard_map/all_to_all | solution.py:185
  54.4 42.9 %copy-start.13 = (bf16[1,768,256]{2,1,0:T(8,128)(2,1)S(1)}, bf16[1,768,256]{2,1,0:T(8,128)(2,1)}, u32[]{:S(2)}) copy-start(bf16[1,768,256]{2,1,0:T(8,128)(2,1)} %param.18) | copy-start | bytes 1179652
  54.4 43.0 %copy-start.17 = (s32[16]{0:T(128)S(1)}, s32[16]{0:T(128)}, u32[]{:S(2)}) copy-start(s32[16]{0:T(128)} %param.16) | copy-start | bytes 196
  86.2 232.0 %all-to-all-start = ((bf16[16,48,2048]{2,1,0:T(8,128)(2,1)}), bf16[16,48,2048]{2,1,0:T(8,128)(2,1)S(1)}, u32[]{:S(2)}, u32[]{:S(2)}) async-start(bf16[16,48,2048]{2,1,0:T(8,128)(2,1)} %select_select_fusion.1), calls=%async_computation | async-start | bytes 6291456 | tf_op jit(solution)/shard_map/all_to_all | solution.py:158
  94.4 70.2 %collective-permute-start = (bf16[1,2,256,768]{3,2,1,0:T(8,128)(2,1)}, bf16[1,2,256,768]{3,2,1,0:T(8,128)(2,1)}, u32[]{:S(2)}, u32[]{:S(2)}) collective-permute-start(bf16[1,2,256,768]{3,2,1,0:T(8,128)(2,1)} %param.17), channel_id=1, source_target_pairs={{64,0},{72,8},{80,16},{88,24},{96,32},{104,40},{112,48},{120,56},{... | collective-permute-start | bytes 2359304 | tf_op jit(solution)/shard_map/ppermute | solution.py:20
  97.3 65.5 %collective-permute-start.1 = (bf16[1,768,256]{2,1,0:T(8,128)(2,1)S(1)}, bf16[1,768,256]{2,1,0:T(8,128)(2,1)}, u32[]{:S(2)}, u32[]{:S(2)}) collective-permute-start(bf16[1,768,256]{2,1,0:T(8,128)(2,1)S(1)} %copy-done.13), channel_id=1, source_target_pairs={{64,0},{72,8},{80,16},{88,24},{96,32},{104,40},{112,48},{120,56},{... | collective-permute-start | bytes 1179656 | tf_op jit(solution)/shard_map/ppermute | solution.py:20
  165.8 0.9 copy-start.4
  318.2 5.8 copy-start.2
  318.2 5.8 copy-start.20
  318.2 5.8 copy-start.22
  328.5 2.7 copy-start.21
  328.5 2.7 copy-start.23
  328.5 2.7 copy-start.19
  335.7 44.8 %all-to-all-start.3 = ((bf16[16,48,2048]{2,1,0:T(8,128)(2,1)}), bf16[16,48,2048]{2,1,0:T(8,128)(2,1)S(1)}, u32[]{:S(2)}, u32[]{:S(2)}) async-start(bf16[16,48,2048]{2,1,0:T(8,128)(2,1)} %bitcast.122), calls=%async_computation.3 | async-start | bytes 6291456 | tf_op jit(solution)/shard_map/all_to_all | solution.py:194
  341.0 5.5 copy-start.8
  341.0 6.5 %copy-start.11 = (f32[1,768,256]{2,1,0:T(8,128)S(1)}, f32[1,768,256]{2,1,0:T(8,128)}, u32[]{:S(2)}) copy-start(f32[1,768,256]{2,1,0:T(8,128)} %param.21) | copy-start | bytes 2359300
  341.0 10.2 %copy-start.12 = (f32[1,768,256]{2,1,0:T(8,128)S(1)}, f32[1,768,256]{2,1,0:T(8,128)}, u32[]{:S(2)}) copy-start(f32[1,768,256]{2,1,0:T(8,128)} %param.22) | copy-start | bytes 2359300
  343.6 247.6 %collective-permute-start.2 = (bf16[1,2,256,768]{3,2,1,0:T(8,128)(2,1)}, bf16[1,2,256,768]{3,2,1,0:T(8,128)(2,1)}, u32[]{:S(2)}, u32[]{:S(2)}) collective-permute-start(bf16[1,2,256,768]{3,2,1,0:T(8,128)(2,1)} %convert_element_type.95), channel_id=1, source_target_pairs={{64,0},{72,8},{80,16},{88,24},{96,32},{104,40},{112,48},{120,56},{... | collective-permute-start | bytes 2359304 | tf_op jit(solution)/shard_map/ppermute | solution.py:20
  347.5 243.7 %collective-permute-start.3 = (bf16[1,2,256,768]{3,2,1,0:T(8,128)(2,1)}, bf16[1,2,256,768]{3,2,1,0:T(8,128)(2,1)}, u32[]{:S(2)}, u32[]{:S(2)}) collective-permute-start(bf16[1,2,256,768]{3,2,1,0:T(8,128)(2,1)} %convert_element_type.98), channel_id=1, source_target_pairs={{64,0},{72,8},{80,16},{88,24},{96,32},{104,40},{112,48},{120,56},{... | collective-permute-start | bytes 2359304 | tf_op jit(solution)/shard_map/ppermute | solution.py:20
  348.3 239.4 %collective-permute-start.4 = (bf16[1,768,256]{2,1,0:T(8,128)(2,1)}, bf16[1,768,256]{2,1,0:T(8,128)(2,1)}, u32[]{:S(2)}, u32[]{:S(2)}) collective-permute-start(bf16[1,768,256]{2,1,0:T(8,128)(2,1)} %convert_element_type.102), channel_id=1, source_target_pairs={{64,0},{72,8},{80,16},{88,24},{96,32},{104,40},{112,48},{120,56},{... | collective-permute-start | bytes 1179656 | tf_op jit(solution)/shard_map/ppermute | solution.py:20
  352.0 235.7 %collective-permute-start.5 = (bf16[1,768,256]{2,1,0:T(8,128)(2,1)}, bf16[1,768,256]{2,1,0:T(8,128)(2,1)}, u32[]{:S(2)}, u32[]{:S(2)}) collective-permute-start(bf16[1,768,256]{2,1,0:T(8,128)(2,1)} %convert_element_type.104), channel_id=1, source_target_pairs={{64,0},{72,8},{80,16},{88,24},{96,32},{104,40},{112,48},{120,56},{... | collective-permute-start | bytes 1179656 | tf_op jit(solution)/shard_map/ppermute | solution.py:20
  380.5 218.3 %all-to-all-start.1 = ((bf16[16,48,2048]{2,1,0:T(8,128)(2,1)}), bf16[16,48,2048]{2,1,0:T(8,128)(2,1)}, u32[]{:S(2)}, u32[]{:S(2)}) async-start(bf16[16,48,2048]{2,1,0:T(8,128)(2,1)} %bitcast.119), calls=%async_computation.1 | async-start | bytes 6291456 | tf_op jit(solution)/shard_map/all_to_all | solution.py:168
  402.7 5.0 copy-start.6
  587.7 3.4 copy-start.5
  587.7 3.5 copy-start.7
  587.7 3.5 copy-start.9
  587.7 3.7 copy-start.10
  598.8 7.9 %copy-start.3 = (bf16[512,2048]{1,0:T(8,128)(2,1)S(1)}, bf16[512,2048]{1,0:T(8,128)(2,1)}, u32[]{:S(2)}) copy-start(bf16[512,2048]{1,0:T(8,128)(2,1)} %gather_fusion.3) | copy-start | bytes 6291460
  611.4 5.3 copy-start.15
  622.8 6.7 %copy-start.1 = (bf16[128,2048]{1,0:T(8,128)(2,1)S(1)}, bf16[128,2048]{1,0:T(8,128)(2,1)}, u32[]{:S(2)}) copy-start(bf16[128,2048]{1,0:T(8,128)(2,1)} %param.13) | copy-start | bytes 1572868

commit v4 on v3

--- a/solution.py
+++ b/solution.py
@@ -136,7 +136,7 @@
     own_partner = jnp.sum(jnp.where(expert_range == row_index, partner, 0))
     take_other = own_partner != row_index
     moved_weights = shifted((w_in, w_down), "expert", halfway)
-    w_in, w_down = (
+    kept_in, kept_down = (
         jnp.where(take_other, moved, owned) for moved, owned in zip(moved_weights, (w_in, w_down))
     )
     moved_states = tuple(
@@ -147,12 +147,15 @@
         jnp.where(take_other, moved, owned)
         for moved, owned in zip(moved_states, (m_in, v_in, m_down, v_down))
     )
-    gate_parts, up_parts, down_parts = exchange((w_in[0, 0], w_in[0, 1], w_down[0]), True, 0)
-    gate_weight = gate_parts.reshape(-1, gate_parts.shape[-1])
-    up_weight = up_parts.reshape(-1, up_parts.shape[-1])
-    down_weight = jnp.transpose(down_parts, (1, 0, 2)).reshape(down_parts.shape[1], -1)
+    in_full, down_full = (
+        lax.all_gather(w_in, "shard", axis=2, tiled=True),
+        lax.all_gather(w_down, "shard", axis=2, tiled=True),
+    )
+    gate_weight = in_full[0, 0]
+    up_weight = in_full[0, 1]
+    down_weight = down_full[0]
     hidden_width = gate_weight.shape[1]
-    position, filler = route_table(expert_ids, partner[expert_ids], groups, capacity)
+    position, filler = route_table(expert_ids, expert_ids, groups, capacity)
     token_fill = jnp.where(filler >= 0, filler // top_count, -1)
     send_rows = fill_rows(tokens, token_fill, groups, capacity)
     arrived = lax.all_to_all(send_rows, "expert", split_axis=0, concat_axis=0, tiled=True)
@@ -211,14 +214,15 @@
     (arrived_parts,) = exchange(
         (partial.reshape(shard_count, share_rows, partial.shape[1]),), False, 1
     )
-    shares = jnp.sum(arrived_parts.astype(jnp.float32), axis=0)
+    summed = jnp.sum(arrived_parts.astype(jnp.float32), axis=0).astype(jnp.bfloat16)
+    shares = jnp.where(take_other, shifted(summed, "expert", halfway), summed).astype(jnp.float32)
     grad_in = jnp.transpose(
         shares[:, : 2 * hidden_width].reshape(share_rows, 2, hidden_width), (1, 0, 2)
     )[None]
     grad_down = jnp.transpose(shares[:, 2 * hidden_width :])[None]
-    new_in, first_in, second_in = adam_update(w_in, own_moments[0], own_moments[1], grad_in)
+    new_in, first_in, second_in = adam_update(kept_in, own_moments[0], own_moments[1], grad_in)
     new_down, first_down, second_down = adam_update(
-        w_down, own_moments[2], own_moments[3], grad_down
+        kept_down, own_moments[2], own_moments[3], grad_down
     )
     return (mixed, token_grad, new_in, new_down, first_in, second_in, first_down, second_down)
 

time: 638 us -> 647 us (1.014)
  waiting for transfers between devices: 112 us -> 257 us
  Pallas kernels: 299 us -> 158 us
  between operations: 1.81 us -> 15.3 us
  local copies, waits for them, and re-layouts: 72 us -> 63 us
  other arithmetic: 61.6 us -> 52.7 us
    pallas_call x2 -> x1, Pallas kernels: 299 us -> 158 us  [exchange(): pl.pallas_call(functools.partial(exchange_kernel, count, spread, width),...]
    all_gather x0 -> x2, waiting for transfers between devices: none -> 135 us  [the longest x1 80.9 us: body(): lax.all_gather(w_in, 'shard', axis=2, tiled=True)]
    ppermute x6 -> x7, waiting for transfers between devices: 64.1 us -> 101 us  [shifted(): return lax.ppermute(block, axis, route)]
    all_to_all x1, waiting for transfers between devices: 31.8 us -> 0.01 us  [body(): lax.all_to_all(send_grads, 'expert', split_axis=0, concat_axis=0, tiled=T...]
    all_to_all x1, waiting for transfers between devices: 0.01 us -> 19.6 us  [body(): lax.all_to_all(send_rows, 'expert', split_axis=0, concat_axis=0, tiled=True)]
    all_to_all x1, waiting for transfers between devices: 16.2 us -> 0.01 us  [body(): lax.all_to_all(entry_grads.reshape(groups, capacity, width), 'expert', sp...]
    mul x1, other arithmetic: 11 us -> 0.69 us  [route_table(): position = dest_rows.reshape(entry_count) * capacity + slot_index]
    unnamed x51 -> x50, local copies, waits for them, and re-layouts: 4.88 us -> 12.4 us
  transfers between devices with their start and end apart: 10 -> 13, of which waited for: 3 -> 6; matrix products, arithmetic and copies ran while one was open for 14% -> 18% of each run, Pallas kernels for 47% -> 25%
where the time goes in v4:
time: 647 us; the launch traced here: 635 us
  waiting for transfers between devices  257 us (40%)
  Pallas kernels  158 us (24%)
  local copies, waits for them, and re-layouts  63 us (10%)
  other arithmetic  52.7 us (8%)
  matrix products  50.1 us (8%)
  starting transfers between devices  39.3 us (6%)
  between operations  15.3 us (2%)
    pallas_call x1, Pallas kernels, exchange(): pl.pallas_call(functools.partial(exchange_kernel, count, spread, width),...  158 us
    ppermute x7, waiting for transfers between devices, shifted(): return lax.ppermute(block, axis, route)  101 us
    all_gather x1, waiting for transfers between devices, body(): lax.all_gather(w_in, 'shard', axis=2, tiled=True)  80.9 us
    all_gather x1, waiting for transfers between devices, body(): lax.all_gather(w_down, 'shard', axis=2, tiled=True)  54.1 us
    all_to_all x1, waiting for transfers between devices, body(): lax.all_to_all(send_rows, 'expert', split_axis=0, concat_axis=0, tiled=True)  19.6 us
    dot_general x3, matrix products, contract_cols(): lax.dot_general(left, right, (((1,), (1,)), ((), ())), preferred_element_...  19.4 us
  transfers between devices with their start and end apart: 13, of which 6 were waited for; matrix products, arithmetic and copies ran while one was open for 18% of the time, Pallas kernels for 25%

profile of v4, /device:TPU:1, one launch (start us, length us, event | category | flops | bytes accessed | tf_op | source)
XLA Modules:
  0.0 634.8 jit_solution(780032930054851962)
XLA Ops:
  11.4 2.4 scatter_custom_fusion
  14.1 4.3 gather_fusion
  18.4 3.4 select_select_fusion.1
  21.8 7.5 %all-to-all-start = ((bf16[16,48,2048]{2,1,0:T(8,128)(2,1)}), bf16[16,48,2048]{2,1,0:T(8,128)(2,1)}, u32[]{:S(2)}, u32[]{:S(2)}) async-start(bf16[16,48,2048]{2,1,0:T(8,128)(2,1)} %select_select_fusion.1), calls=%async_computation | async-start | bytes 6291456 | tf_op jit(solution)/shard_map/all_to_all | solution.py:161
  30.0 3.1 mul.162
  33.2 5.4 mul.163
  39.3 2.6 multiply_convert_fusion
  41.9 4.3 gather_fusion.1
  46.2 3.4 select_select_fusion
  49.6 19.6 %all-to-all-done = bf16[16,48,2048]{2,1,0:T(8,128)(2,1)} async-done(((bf16[16,48,2048]{2,1,0:T(8,128)(2,1)}), bf16[16,48,2048]{2,1,0:T(8,128)(2,1)}, u32[]{:S(2)}, u32[]{:S(2)}) %all-to-all-start) | async-done | bytes 3145760 | tf_op jit(solution)/shard_map/all_to_all | solution.py:161
  69.2 8.5 %all-to-all-start.2 = ((bf16[16,48,2048]{2,1,0:T(8,128)(2,1)}), bf16[16,48,2048]{2,1,0:T(8,128)(2,1)S(1)}, u32[]{:S(2)}, u32[]{:S(2)}) async-start(bf16[16,48,2048]{2,1,0:T(8,128)(2,1)} %select_select_fusion), calls=%async_computation.2 | async-start | bytes 6291456 | tf_op jit(solution)/shard_map/all_to_all | solution.py:188
  77.7 80.9 %all-gather.3.cloned.1.call-done = bf16[1,2,2048,768]{3,2,1,0:T(8,128)(2,1)} async-done(((bf16[1,2,256,768]{3,2,1,0:T(8,128)(2,1)}), bf16[1,2,2048,768]{3,2,1,0:T(8,128)(2,1)}) %all-gather.3.cloned.1.call-update) | async-done | bytes 6291472 | tf_op jit(solution)/shard_map/all_gather | solution.py:151
  158.6 7.0 %fusion.4 = f32[768,768]{0,1:T(8,128)} fusion(bf16[768,2048]{1,0:T(8,128)(2,1)} %bitcast.4, bf16[1,2,2048,768]{3,2,1,0:T(8,128)(2,1)} %all-gather.3.cloned.1.call-done), kind=kOutput, calls=%fused_computation.19 | convolution fusion | flops 2415919104 | bytes 8650752 | tf_op jit(solution)/shard_map/dot_general | solution.py:164
  165.6 6.1 fusion.5
  171.7 54.1 %all-gather.5.cloned.1.call-done = bf16[1,768,2048]{2,1,0:T(8,128)(2,1)} async-done(((bf16[1,768,256]{2,1,0:T(8,128)(2,1)}), bf16[1,768,2048]{2,1,0:T(8,128)(2,1)}) %all-gather.5.cloned.1.call-update) | async-done | bytes 3145744 | tf_op jit(solution)/shard_map/all_gather | solution.py:152
  225.8 7.7 %multiply_convert_fusion.1 = (bf16[768,768]{0,1:T(8,128)(2,1)S(1)}, bf16[768,768]{0,1:T(8,128)(2,1)S(1)}, bf16[768,768]{0,1:T(8,128)(2,1)}) fusion(f32[768,768]{0,1:T(8,128)} %fusion.4, f32[768,768]{0,1:T(8,128)} %fusion.5, bf16[768,2048]{1,0:T(8,128)(2,1)S(1)} %bitcast.116, bf16[1,768,2048]{2,1,0:T(8,128)(2,1)} %all-gather.5.cloned.1.call-done), kind=kOutput, calls=%fused_computation.25 | convolution fusion | flops 2424766464 | bytes 14548992 | tf_op jit(solution)/shard_map/dot_general | solution.py:120
  233.5 5.4 fusion.3
  239.0 6.3 add_convert_fusion
  245.3 5.9 all-to-all-start.3
  251.2 4.6 copy.44
  255.8 4.7 copy.42
  260.5 5.0 convolution_convert_fusion.2
  265.6 6.1 convolution_convert_fusion
  271.6 3.9 pad_maximum_fusion.refs_0_
  275.6 157.6 %shard_map.170 = bf16[8,256,2304]{2,1,0:T(8,128)(2,1)} custom-call(bf16[8,256,2304]{2,1,0:T(8,128)(2,1)} %pad_maximum_fusion.refs_0_), custom_call_target="tpu_custom_call" | custom-call | bytes 18874368 | tf_op jit(solution)/shard_map/pallas_call | solution.py:64
  433.2 6.3 reduce_sum.58
  439.5 2.4 collective-permute-start.2
  441.9 6.5 %convolution_convert_fusion.1 = bf16[768,2048]{1,0:T(8,128)(2,1)} fusion(bf16[768,768]{0,1:T(8,128)(2,1)} %get-tuple-element.27, bf16[1,768,2048]{2,1,0:T(8,128)(2,1)} %all-gather.5.cloned.1.call-done), kind=kOutput, calls=%fused_computation.10 | convolution fusion | flops 2417491968 | bytes 7471104 | tf_op jit(solution)/shard_map/dot_general | solution.py:168
  448.5 5.7 all-to-all-start.1
  454.2 3.0 collective-permute-start
  457.2 2.4 convert_element_type.97
  460.7 2.8 collective-permute-start.3
  465.9 2.3 copy.49
  470.1 2.3 copy.51
  473.5 87.7 %collective-permute-done.4 = bf16[1,768,256]{1,2,0:T(8,128)(2,1)S(1)} collective-permute-done((bf16[1,768,256]{1,2,0:T(8,128)(2,1)}, bf16[1,768,256]{1,2,0:T(8,128)(2,1)S(1)}, u32[]{:S(2)}, u32[]{:S(2)}) %collective-permute-start.4) | collective-permute-done | bytes 393248 | tf_op jit(solution)/shard_map/ppermute | solution.py:20
  567.0 4.7 collective-permute-done.5
  571.8 8.4 %collective-permute-done.6 = bf16[1,768,256]{1,2,0:T(8,128)(2,1)S(1)} collective-permute-done((bf16[1,768,256]{1,2,0:T(8,128)(2,1)S(1)}, bf16[1,768,256]{1,2,0:T(8,128)(2,1)S(1)}, u32[]{:S(2)}, u32[]{:S(2)}) %collective-permute-start.6) | collective-permute-done | bytes 393248 | tf_op jit(solution)/shard_map/ppermute | solution.py:20
  580.2 2.9 subtract_convert_fusion.1
  584.0 2.3 copy.54
  586.3 2.3 copy.55
  588.6 5.0 subtract_convert_fusion
  593.6 3.6 gather_fusion.3
  597.2 7.7 %gather_fusion.2 = bf16[512,2048]{1,0:T(8,128)(2,1)} fusion(bf16[768,2048]{1,0:T(8,128)(2,1)} %bitcast.9, s32[1024]{0:T(1024)S(1)} %pad_clamp_fusion.1), kind=kCustom, calls=%fused_computation.clone | custom fusion | bytes 4196352 | tf_op jit(solution)/shard_map/jit(_take)/gather | solution.py:178
  604.9 4.6 broadcast_select_fusion
  609.5 5.3 reshape.156
  614.8 6.2 multiply_reduce_fusion
  621.0 2.8 reshape.154
  623.8 3.9 reduce_sum.56
  (90 shorter events, 18.6 us)
Async XLA Ops:
  7.2 6.9 %copy-start = (bf16[128,2048]{1,0:T(8,128)(2,1)S(1)}, bf16[128,2048]{1,0:T(8,128)(2,1)}, u32[]{:S(2)}) copy-start(bf16[128,2048]{1,0:T(8,128)(2,1)} %param.13) | copy-start | bytes 1572868
  7.2 151.4 %all-gather.3.cloned.1.call-start = ((), (), s32[]{:S(2)}) async-start(), calls=%async_computation.4 | async-start | bytes 7077888 | tf_op jit(solution)/shard_map/all_gather | solution.py:151
  21.8 8.3 %copy-start.12 = (bf16[128,2048]{1,0:T(8,128)(2,1)S(1)}, bf16[128,2048]{1,0:T(8,128)(2,1)}, u32[]{:S(2)}) copy-start(bf16[128,2048]{1,0:T(8,128)(2,1)} %param.23) | copy-start | bytes 1572868
  21.8 47.4 %all-to-all-start = ((bf16[16,48,2048]{2,1,0:T(8,128)(2,1)}), bf16[16,48,2048]{2,1,0:T(8,128)(2,1)}, u32[]{:S(2)}, u32[]{:S(2)}) async-start(bf16[16,48,2048]{2,1,0:T(8,128)(2,1)} %select_select_fusion.1), calls=%async_computation | async-start | bytes 6291456 | tf_op jit(solution)/shard_map/all_to_all | solution.py:161
  29.3 196.6 %all-gather.5.cloned.1.call-start = ((), (), s32[]{:S(2)}) async-start(), calls=%async_computation.5 | async-start | bytes 3538944 | tf_op jit(solution)/shard_map/all_gather | solution.py:152
  33.2 5.4 copy-start.14
  38.6 0.6 copy-start.10
  69.2 102.5 %all-to-all-start.2 = ((bf16[16,48,2048]{2,1,0:T(8,128)(2,1)}), bf16[16,48,2048]{2,1,0:T(8,128)(2,1)S(1)}, u32[]{:S(2)}, u32[]{:S(2)}) async-start(bf16[16,48,2048]{2,1,0:T(8,128)(2,1)} %select_select_fusion), calls=%async_computation.2 | async-start | bytes 6291456 | tf_op jit(solution)/shard_map/all_to_all | solution.py:188
  158.6 7.0 %copy-start.15 = (bf16[1,2,2048,768]{3,2,1,0:T(8,128)(2,1)S(1)}, bf16[1,2,2048,768]{3,2,1,0:T(8,128)(2,1)}, u32[]{:S(2)}) copy-start(bf16[1,2,2048,768]{3,2,1,0:T(8,128)(2,1)} %all-gather.3.cloned.1.call-done) | copy-start | bytes 18874372
  171.7 61.8 %copy-start.2 = (bf16[16,48,2048]{2,1,0:T(8,128)(2,1)}, bf16[16,48,2048]{2,1,0:T(8,128)(2,1)S(1)}, u32[]{:S(2)}) copy-start(bf16[16,48,2048]{2,1,0:T(8,128)(2,1)S(1)} %all-to-all-done.2) | copy-start | bytes 9437188
  233.5 5.4 copy-start.17
  233.5 5.4 copy-start.19
  245.3 203.2 %all-to-all-start.3 = ((bf16[16,48,2048]{2,1,0:T(8,128)(2,1)}), bf16[16,48,2048]{2,1,0:T(8,128)(2,1)S(1)}, u32[]{:S(2)}, u32[]{:S(2)}) async-start(bf16[16,48,2048]{2,1,0:T(8,128)(2,1)} %bitcast.122), calls=%async_computation.3 | async-start | bytes 6291456 | tf_op jit(solution)/shard_map/all_to_all | solution.py:197
  260.5 5.0 copy-start.7
  260.5 5.0 copy-start.18
  260.5 5.0 copy-start.20
  439.5 123.2 %collective-permute-start.2 = (bf16[256,2304]{1,0:T(8,128)(2,1)}, bf16[256,2304]{1,0:T(8,128)(2,1)}, u32[]{:S(2)}, u32[]{:S(2)}) collective-permute-start(bf16[256,2304]{1,0:T(8,128)(2,1)} %reduce_sum.58), channel_id=1, source_target_pairs={{64,0},{72,8},{80,16},{88,24},{96,32},{104,40},{112,48},{120,56},{... | collective-permute-start | bytes 3538952 | tf_op jit(solution)/shard_map/ppermute | solution.py:20
  448.5 148.7 %all-to-all-start.1 = ((bf16[16,48,2048]{2,1,0:T(8,128)(2,1)}), bf16[16,48,2048]{2,1,0:T(8,128)(2,1)}, u32[]{:S(2)}, u32[]{:S(2)}) async-start(bf16[16,48,2048]{2,1,0:T(8,128)(2,1)} %bitcast.121), calls=%async_computation.1 | async-start | bytes 6291456 | tf_op jit(solution)/shard_map/all_to_all | solution.py:171
  454.1 5.6 copy-start.6
  454.2 9.3 %copy-start.8 = (bf16[1,768,256]{2,1,0:T(8,128)(2,1)S(1)}, bf16[1,768,256]{2,1,0:T(8,128)(2,1)}, u32[]{:S(2)}) copy-start(bf16[1,768,256]{2,1,0:T(8,128)(2,1)} %param.18) | copy-start | bytes 1179652
  454.2 10.4 %copy-start.16 = (s32[16]{0:T(128)S(1)}, s32[16]{0:T(128)}, u32[]{:S(2)}) copy-start(s32[16]{0:T(128)} %param.16) | copy-start | bytes 196
  454.2 134.4 %collective-permute-start = (bf16[1,2,256,768]{3,2,1,0:T(8,128)(2,1)}, bf16[1,2,256,768]{3,2,1,0:T(8,128)(2,1)}, u32[]{:S(2)}, u32[]{:S(2)}) collective-permute-start(bf16[1,2,256,768]{3,2,1,0:T(8,128)(2,1)} %param.17), channel_id=1, source_target_pairs={{64,0},{72,8},{80,16},{88,24},{96,32},{104,40},{112,48},{120,56},{... | collective-permute-start | bytes 2359304 | tf_op jit(solution)/shard_map/ppermute | solution.py:20
  459.6 129.0 %collective-permute-start.1 = (bf16[1,2,256,768]{3,2,1,0:T(8,128)(2,1)}, bf16[1,2,256,768]{3,2,1,0:T(8,128)(2,1)}, u32[]{:S(2)}, u32[]{:S(2)}) collective-permute-start(bf16[1,2,256,768]{3,2,1,0:T(8,128)(2,1)} %convert_element_type.97), channel_id=1, source_target_pairs={{64,0},{72,8},{80,16},{88,24},{96,32},{104,40},{112,48},{120,56},{... | collective-permute-start | bytes 2359304 | tf_op jit(solution)/shard_map/ppermute | solution.py:20
  460.7 127.9 %collective-permute-start.3 = (bf16[1,2,256,768]{3,2,1,0:T(8,128)(2,1)}, bf16[1,2,256,768]{3,2,1,0:T(8,128)(2,1)}, u32[]{:S(2)}, u32[]{:S(2)}) collective-permute-start(bf16[1,2,256,768]{3,2,1,0:T(8,128)(2,1)} %convert_element_type.100), channel_id=1, source_target_pairs={{64,0},{72,8},{80,16},{88,24},{96,32},{104,40},{112,48},{120,56},{... | collective-permute-start | bytes 2359304 | tf_op jit(solution)/shard_map/ppermute | solution.py:20
  464.4 96.8 %collective-permute-start.4 = (bf16[1,768,256]{1,2,0:T(8,128)(2,1)}, bf16[1,768,256]{1,2,0:T(8,128)(2,1)S(1)}, u32[]{:S(2)}, u32[]{:S(2)}) collective-permute-start(bf16[1,768,256]{1,2,0:T(8,128)(2,1)} %copy.47), channel_id=1, source_target_pairs={{64,0},{72,8},{80,16},{88,24},{96,32},{104,40},{112,48},{120,56},{... | collective-permute-start | bytes 1179656 | tf_op jit(solution)/shard_map/ppermute | solution.py:20
  561.2 4.4 copy-start.13
  561.2 10.6 %collective-permute-start.5 = (bf16[1,768,256]{1,2,0:T(8,128)(2,1)}, bf16[1,768,256]{1,2,0:T(8,128)(2,1)S(1)}, u32[]{:S(2)}, u32[]{:S(2)}) collective-permute-start(bf16[1,768,256]{1,2,0:T(8,128)(2,1)} %convert_element_type.104), channel_id=1, source_target_pairs={{64,0},{72,8},{80,16},{88,24},{96,32},{104,40},{112,48},{120,56},{... | collective-permute-start | bytes 1179656 | tf_op jit(solution)/shard_map/ppermute | solution.py:20
  562.7 17.5 %collective-permute-start.6 = (bf16[1,768,256]{1,2,0:T(8,128)(2,1)S(1)}, bf16[1,768,256]{1,2,0:T(8,128)(2,1)S(1)}, u32[]{:S(2)}, u32[]{:S(2)}) collective-permute-start(bf16[1,768,256]{1,2,0:T(8,128)(2,1)S(1)} %convert_element_type.106), channel_id=1, source_target_pairs={{64,0},{72,8},{80,16},{88,24},{96,32},{104,40},{112,48},{120,56},{... | collective-permute-start | bytes 1179656 | tf_op jit(solution)/shard_map/ppermute | solution.py:20
  565.6 14.6 %copy-start.4 = (f32[1,768,256]{1,2,0:T(8,128)S(1)}, f32[1,768,256]{1,2,0:T(8,128)}, u32[]{:S(2)}) copy-start(f32[1,768,256]{1,2,0:T(8,128)} %copy.49) | copy-start | bytes 2359300
  565.6 14.6 %copy-start.5 = (f32[1,768,256]{1,2,0:T(8,128)S(1)}, f32[1,768,256]{1,2,0:T(8,128)}, u32[]{:S(2)}) copy-start(f32[1,768,256]{1,2,0:T(8,128)} %copy.51) | copy-start | bytes 2359300
  565.7 14.5 %copy-start.9 = (bf16[1,768,256]{1,2,0:T(8,128)(2,1)S(1)}, bf16[1,768,256]{1,2,0:T(8,128)(2,1)}, u32[]{:S(2)}) copy-start(bf16[1,768,256]{1,2,0:T(8,128)(2,1)} %copy.47) | copy-start | bytes 1179652
  597.2 7.7 %copy-start.3 = (bf16[512,2048]{1,0:T(8,128)(2,1)S(1)}, bf16[512,2048]{1,0:T(8,128)(2,1)}, u32[]{:S(2)}) copy-start(bf16[512,2048]{1,0:T(8,128)(2,1)} %gather_fusion.3) | copy-start | bytes 6291460
  609.5 5.3 copy-start.11
  621.0 6.7 %copy-start.1 = (bf16[128,2048]{1,0:T(8,128)(2,1)S(1)}, bf16[128,2048]{1,0:T(8,128)(2,1)}, u32[]{:S(2)}) copy-start(bf16[128,2048]{1,0:T(8,128)(2,1)} %param.13) | copy-start | bytes 1572868
Sparse Core Ops, SparseCore 0:
  10.3 148.2 all-gather.2
  160.8 65.0 all-gather.4

commit v5 on v3

--- a/solution.py
+++ b/solution.py
@@ -136,7 +136,7 @@
     own_partner = jnp.sum(jnp.where(expert_range == row_index, partner, 0))
     take_other = own_partner != row_index
     moved_weights = shifted((w_in, w_down), "expert", halfway)
-    w_in, w_down = (
+    kept_in, kept_down = (
         jnp.where(take_other, moved, owned) for moved, owned in zip(moved_weights, (w_in, w_down))
     )
     moved_states = tuple(
@@ -148,11 +148,16 @@
         for moved, owned in zip(moved_states, (m_in, v_in, m_down, v_down))
     )
     gate_parts, up_parts, down_parts = exchange((w_in[0, 0], w_in[0, 1], w_down[0]), True, 0)
+    (gate_parts, up_parts, down_parts), kept_in, kept_down, m_in, v_in, m_down, v_down = (
+        lax.optimization_barrier(
+            ((gate_parts, up_parts, down_parts), kept_in, kept_down, m_in, v_in, m_down, v_down)
+        )
+    )
     gate_weight = gate_parts.reshape(-1, gate_parts.shape[-1])
     up_weight = up_parts.reshape(-1, up_parts.shape[-1])
     down_weight = jnp.transpose(down_parts, (1, 0, 2)).reshape(down_parts.shape[1], -1)
     hidden_width = gate_weight.shape[1]
-    position, filler = route_table(expert_ids, partner[expert_ids], groups, capacity)
+    position, filler = route_table(expert_ids, expert_ids, groups, capacity)
     token_fill = jnp.where(filler >= 0, filler // top_count, -1)
     send_rows = fill_rows(tokens, token_fill, groups, capacity)
     arrived = lax.all_to_all(send_rows, "expert", split_axis=0, concat_axis=0, tiled=True)
@@ -204,21 +209,22 @@
     token_grad = jnp.sum(per_back.astype(jnp.float32), axis=1).astype(jnp.bfloat16)
     grad_both = jnp.concatenate([grad_gate, grad_up], axis=1)
     share_rows = width // lax.axis_size("shard")
-    partial = jnp.concatenate(
-        [contract_rows(rows_x, grad_both), contract_rows(dout_rows, hidden)], axis=1
-    ).astype(jnp.bfloat16)
-    shard_count = lax.axis_size("shard")
-    (arrived_parts,) = exchange(
-        (partial.reshape(shard_count, share_rows, partial.shape[1]),), False, 1
-    )
-    shares = jnp.sum(arrived_parts.astype(jnp.float32), axis=0)
+    shares = lax.psum_scatter(
+        jnp.concatenate(
+            [contract_rows(rows_x, grad_both), contract_rows(dout_rows, hidden)], axis=1
+        ).astype(jnp.bfloat16),
+        "shard",
+        scatter_dimension=0,
+        tiled=True,
+    )
+    shares = jnp.where(take_other, shifted(shares, "expert", halfway), shares).astype(jnp.float32)
     grad_in = jnp.transpose(
         shares[:, : 2 * hidden_width].reshape(share_rows, 2, hidden_width), (1, 0, 2)
     )[None]
     grad_down = jnp.transpose(shares[:, 2 * hidden_width :])[None]
-    new_in, first_in, second_in = adam_update(w_in, own_moments[0], own_moments[1], grad_in)
+    new_in, first_in, second_in = adam_update(kept_in, own_moments[0], own_moments[1], grad_in)
     new_down, first_down, second_down = adam_update(
-        w_down, own_moments[2], own_moments[3], grad_down
+        kept_down, own_moments[2], own_moments[3], grad_down
     )
     return (mixed, token_grad, new_in, new_down, first_in, second_in, first_down, second_down)
 

time: 638 us -> 542 us (0.85)
  Pallas kernels: 299 us -> 133 us
  waiting for transfers between devices: 112 us -> 185 us
  local copies, waits for them, and re-layouts: 72 us -> 51.4 us
  between operations: 1.81 us -> 15.3 us
    pallas_call x2 -> x1, Pallas kernels: 299 us -> 133 us  [exchange(): pl.pallas_call(functools.partial(exchange_kernel, count, spread, width),...]
    reduce_scatter x0 -> x1, waiting for transfers between devices: none -> 131 us  [body(): lax.psum_scatter(jnp.concatenate([contract_rows(rows_x, grad_both), contr...]
    ppermute x6 -> x7, waiting for transfers between devices: 64.1 us -> 0.16 us  [shifted(): return lax.ppermute(block, axis, route)]
    all_to_all x1, waiting for transfers between devices: 16.2 us -> 38 us  [body(): lax.all_to_all(entry_grads.reshape(groups, capacity, width), 'expert', sp...]
    all_to_all x1, waiting for transfers between devices: 31.8 us -> 16.3 us  [body(): lax.all_to_all(send_grads, 'expert', split_axis=0, concat_axis=0, tiled=T...]
    mul x1, other arithmetic: 11 us -> 0.74 us  [route_table(): position = dest_rows.reshape(entry_count) * capacity + slot_index]
    dot_general x2 -> x0, local copies, waits for them, and re-layouts: 9.37 us -> none  [contract_rows(): lax.dot_general(left, right, (((0,), (0,)), ((), ())), preferred_element_...]
    select_n x1 -> x6, other arithmetic: 1.22 us -> 10.3 us  [body(): jnp.where(take_other, moved, owned)]
  transfers between devices with their start and end apart: 10 -> 12, of which waited for: 3 -> 4; matrix products, arithmetic and copies ran while one was open for 14% -> 19% of each run, Pallas kernels for 47% -> 25%
where the time goes in v5:
time: 542 us; the launch traced here: 534 us
  waiting for transfers between devices  185 us (34%)
  Pallas kernels  133 us (25%)
  other arithmetic  58.3 us (11%)
  local copies, waits for them, and re-layouts  51.4 us (9%)
  matrix products  49.6 us (9%)
  starting transfers between devices  40.7 us (8%)
  between operations  15.3 us (3%)
    pallas_call x1, Pallas kernels, exchange(): pl.pallas_call(functools.partial(exchange_kernel, count, spread, width),...  133 us
    reduce_scatter x1, waiting for transfers between devices, body(): lax.psum_scatter(jnp.concatenate([contract_rows(rows_x, grad_both), contr...  131 us
    all_to_all x1, waiting for transfers between devices, body(): lax.all_to_all(entry_grads.reshape(groups, capacity, width), 'expert', sp...  38 us
    all_to_all x1, waiting for transfers between devices, body(): lax.all_to_all(send_grads, 'expert', split_axis=0, concat_axis=0, tiled=T...  16.3 us
    ppermute x7, starting transfers between devices, shifted(): return lax.ppermute(block, axis, route)  14.6 us
    dot_general x3, matrix products, contract_cols(): lax.dot_general(left, right, (((1,), (1,)), ((), ())), preferred_element_...  14.5 us
    dot_general x2, matrix products, contract_rows(): lax.dot_general(left, right, (((0,), (0,)), ((), ())), preferred_element_...  14.3 us
    concatenate x1, other arithmetic, body(): jnp.concatenate([contract_rows(rows_x, grad_both), contract_rows(dout_row...  11.7 us
  transfers between devices with their start and end apart: 12, of which 4 were waited for; matrix products, arithmetic and copies ran while one was open for 19% of the time, Pallas kernels for 25%

profile of v5, /device:TPU:1, one launch (start us, length us, event | category | flops | bytes accessed | tf_op | source)
XLA Modules:
  0.0 533.7 jit_solution(13161722188444444272)
XLA Ops:
  9.2 1.2 reduce-window.6
  10.7 2.4 scatter_custom_fusion
  13.4 4.3 gather_fusion
  17.7 3.3 select_select_fusion.1
  21.0 7.6 %all-to-all-start = ((bf16[16,48,2048]{2,1,0:T(8,128)(2,1)}), bf16[16,48,2048]{2,1,0:T(8,128)(2,1)}, u32[]{:S(2)}, u32[]{:S(2)}) async-start(bf16[16,48,2048]{2,1,0:T(8,128)(2,1)} %select_select_fusion.1), calls=%async_computation | async-start | bytes 6291456 | tf_op jit(solution)/shard_map/all_to_all | solution.py:163
  28.6 3.0 collective-permute-start
  32.7 2.9 collective-permute-start.2
  37.2 2.9 collective-permute-start.5
  40.1 3.1 mul.162
  43.1 5.3 mul.163
  49.3 2.5 multiply_convert_fusion
  51.7 4.3 gather_fusion.1
  56.0 3.3 select_select_fusion
  62.5 133.3 %shard_map.170 = (bf16[8,256,768]{2,1,0:T(8,128)(2,1)}, bf16[8,256,768]{2,1,0:T(8,128)(2,1)}, bf16[8,768,256]{2,1,0:T(8,128)(2,1)}) custom-call(bf16[256,768]{1,0:T(8,128)(2,1)} %get-tuple-element.45.refs_0_, bf16[256,768]{1,0:T(8,128)(2,1)} %get-tuple-element.44.refs_1_, bf16[768,256]{1,0:T(8,128)(2,1)} %bitcast.94), custom_call_target="tpu_custom_call" | custom-call | bytes 18874368 | tf_op jit(solution)/shard_map/pallas_call | solution.py:64
  195.8 2.7 collective-permute-start.3
  198.6 7.0 %all-to-all-start.2 = ((bf16[16,48,2048]{2,1,0:T(8,128)(2,1)}), bf16[16,48,2048]{2,1,0:T(8,128)(2,1)}, u32[]{:S(2)}, u32[]{:S(2)}) async-start(bf16[16,48,2048]{2,1,0:T(8,128)(2,1)} %select_select_fusion), calls=%async_computation.2 | async-start | bytes 6291456 | tf_op jit(solution)/shard_map/all_to_all | solution.py:190
  206.1 2.3 convert_select_fusion.3
  208.4 2.1 convert_select_fusion.2
  211.5 2.5 convert_select_fusion.1
  214.1 2.4 convert_select_fusion
  216.6 3.2 copy.26
  219.8 8.1 %fusion.21 = f32[768,768]{0,1:T(8,128)} fusion(bf16[768,2048]{1,0:T(8,128)(2,1)} %bitcast.4, bf16[2048,768]{1,0:T(8,128)(2,1)} %bitcast.99), kind=kOutput, calls=%fused_computation.80 | convolution fusion | flops 2415919104 | bytes 8650752 | tf_op jit(solution)/shard_map/dot_general | solution.py:166
  227.9 6.1 %fusion.22 = f32[768,768]{0,1:T(8,128)} fusion(bf16[768,2048]{1,0:T(8,128)(2,1)} %bitcast.4, bf16[2048,768]{1,0:T(8,128)(2,1)S(1)} %bitcast.97), kind=kOutput, calls=%fused_computation.81 | convolution fusion | flops 2415919104 | bytes 8650752 | tf_op jit(solution)/shard_map/dot_general | solution.py:167
  234.0 16.3 %all-to-all-done.2 = bf16[16,48,2048]{2,1,0:T(8,128)(2,1)} async-done(((bf16[16,48,2048]{2,1,0:T(8,128)(2,1)}), bf16[16,48,2048]{2,1,0:T(8,128)(2,1)}, u32[]{:S(2)}, u32[]{:S(2)}) %all-to-all-start.2) | async-done | bytes 3145760 | tf_op jit(solution)/shard_map/all_to_all | solution.py:190
  250.3 6.3 %multiply_convert_fusion.1 = (bf16[768,768]{0,1:T(8,128)(2,1)S(1)}, bf16[768,768]{0,1:T(8,128)(2,1)S(1)}, bf16[768,768]{0,1:T(8,128)(2,1)S(1)}) fusion(f32[768,768]{0,1:T(8,128)} %fusion.21, f32[768,768]{0,1:T(8,128)} %fusion.22, bf16[768,2048]{1,0:T(8,128)(2,1)} %bitcast.15, bf16[768,2048]{0,1:T(8,128)(2,1)S(1)} %bitcast.90), kind=kOutput, calls=%fused_computation.18 | convolution fusion | flops 2424766464 | bytes 14548992 | tf_op jit(solution)/shard_map/dot_general | solution.py:120
  256.6 6.0 %convolution_convert_fusion.1 = bf16[2048,768]{0,1:T(8,128)(2,1)S(1)} fusion(bf16[768,768]{0,1:T(8,128)(2,1)S(1)} %get-tuple-element.43, bf16[768,2048]{1,0:T(8,128)(2,1)} %bitcast.15), kind=kOutput, calls=%fused_computation.10 | convolution fusion | flops 2417491968 | bytes 7471104 | tf_op jit(solution)/shard_map/dot_general | solution.py:114
  262.7 8.3 %convolution_convert_fusion = bf16[2048,1536]{0,1:T(8,128)(2,1)S(1)} fusion(bf16[768,2048]{1,0:T(8,128)(2,1)} %bitcast.4, bf16[768,768]{0,1:T(8,128)(2,1)S(1)} %get-tuple-element.41, bf16[768,768]{0,1:T(8,128)(2,1)S(1)} %get-tuple-element.42), kind=kOutput, calls=%fused_computation.6 | convolution fusion | flops 4839702528 | bytes 11796480 | tf_op jit(solution)/shard_map/dot_general | solution.py:114
  271.0 11.7 %pad_maximum_fusion = bf16[2048,2304]{0,1:T(8,128)(2,1)} fusion(bf16[2048,768]{0,1:T(8,128)(2,1)S(1)} %convolution_convert_fusion.1, bf16[2048,1536]{0,1:T(8,128)(2,1)S(1)} %convolution_convert_fusion), kind=kLoop, calls=%fused_computation.5 | loop fusion | flops 18874368 | bytes 18874368 | tf_op jit(solution)/shard_map/concatenate | solution.py:213
  282.8 1.9 copy-done.24
  284.6 4.1 fusion.23
  288.7 4.1 add_convert_fusion
  292.8 6.5 %all-to-all-start.3 = ((bf16[16,48,2048]{2,1,0:T(8,128)(2,1)}), bf16[16,48,2048]{2,1,0:T(8,128)(2,1)S(1)}, u32[]{:S(2)}, u32[]{:S(2)}) async-start(bf16[16,48,2048]{2,1,0:T(8,128)(2,1)} %bitcast.93), calls=%async_computation.3 | async-start | bytes 6291456 | tf_op jit(solution)/shard_map/all_to_all | solution.py:199
  299.4 6.6 %convolution_convert_fusion.2 = bf16[768,2048]{1,0:T(8,128)(2,1)} fusion(bf16[768,768]{0,1:T(8,128)(2,1)} %copy-done.27, bf16[768,2048]{0,1:T(8,128)(2,1)} %bitcast.91), kind=kOutput, calls=%fused_computation.11 | convolution fusion | flops 2417491968 | bytes 7471104 | tf_op jit(solution)/shard_map/dot_general | solution.py:170
  306.0 38.0 %all-to-all-done.3 = bf16[16,48,2048]{2,1,0:T(8,128)(2,1)S(1)} async-done(((bf16[16,48,2048]{2,1,0:T(8,128)(2,1)}), bf16[16,48,2048]{2,1,0:T(8,128)(2,1)S(1)}, u32[]{:S(2)}, u32[]{:S(2)}) %all-to-all-start.3) | async-done | bytes 3145760 | tf_op jit(solution)/shard_map/all_to_all | solution.py:199
  344.0 4.5 all-to-all-start.1
  348.4 130.7 %reduce-scatter.2.cloned.1.call-done = bf16[256,2304]{0,1:T(8,128)(2,1)} async-done(((bf16[2048,2304]{0,1:T(8,128)(2,1)}), bf16[256,2304]{0,1:T(8,128)(2,1)}) %reduce-scatter.2.cloned.1.call-update) | async-done | bytes 1179664 | tf_op jit(solution)/shard_map/reduce_scatter | solution.py:212
  479.1 3.0 collective-permute-start.6
  482.1 3.5 gather_fusion.3
  485.6 7.7 %gather_fusion.2 = bf16[512,2048]{1,0:T(8,128)(2,1)} fusion(bf16[768,2048]{1,0:T(8,128)(2,1)} %bitcast.13, s32[1024]{0:T(1024)S(1)} %pad_clamp_fusion.1), kind=kCustom, calls=%fused_computation.clone | custom fusion | bytes 4196352 | tf_op jit(solution)/shard_map/jit(_take)/gather | solution.py:180
  493.3 4.7 broadcast_select_fusion
  498.0 5.3 reshape.163
  503.2 2.7 reshape.161
  506.0 3.9 reduce_sum.45
  509.9 6.3 %multiply_reduce_fusion = bf16[128,2048]{1,0:T(8,128)(2,1)} fusion(f32[128,4,2048]{2,1,0:T(4,128)} %reshape.163, f32[128,4]{1,0:T(8,128)S(1)} %copy-done.19), kind=kLoop, calls=%fused_computation.9 | loop fusion | flops 1835008 | bytes 4720640 | tf_op jit(solution)/shard_map/reduce_sum | solution.py:183
  516.5 1.2 slice.33
  517.7 3.1 copy.28
  520.8 3.2 subtract_convert_fusion.1
  524.0 2.7 subtract_convert_fusion
  (105 shorter events, 10.8 us)
Async XLA Ops:
  7.2 6.2 %copy-start = (bf16[128,2048]{1,0:T(8,128)(2,1)S(1)}, bf16[128,2048]{1,0:T(8,128)(2,1)}, u32[]{:S(2)}) copy-start(bf16[128,2048]{1,0:T(8,128)(2,1)} %param.13) | copy-start | bytes 1572868
  21.0 7.6 %copy-start.10 = (bf16[1,2,256,768]{3,2,1,0:T(8,128)(2,1)S(1)}, bf16[1,2,256,768]{3,2,1,0:T(8,128)(2,1)}, u32[]{:S(2)}) copy-start(bf16[1,2,256,768]{3,2,1,0:T(8,128)(2,1)} %param.17) | copy-start | bytes 2359300
  21.0 10.6 %copy-start.15 = (bf16[1,768,256]{2,1,0:T(8,128)(2,1)S(1)}, bf16[1,768,256]{2,1,0:T(8,128)(2,1)}, u32[]{:S(2)}) copy-start(bf16[1,768,256]{2,1,0:T(8,128)(2,1)} %param.18) | copy-start | bytes 1179652
  21.0 10.7 %copy-start.6 = (f32[1,2,256,768]{3,2,1,0:T(8,128)S(1)}, f32[1,2,256,768]{3,2,1,0:T(8,128)}, u32[]{:S(2)}) copy-start(f32[1,2,256,768]{3,2,1,0:T(8,128)} %param.19) | copy-start | bytes 4718596
  21.0 177.6 %all-to-all-start = ((bf16[16,48,2048]{2,1,0:T(8,128)(2,1)}), bf16[16,48,2048]{2,1,0:T(8,128)(2,1)}, u32[]{:S(2)}, u32[]{:S(2)}) async-start(bf16[16,48,2048]{2,1,0:T(8,128)(2,1)} %select_select_fusion.1), calls=%async_computation | async-start | bytes 6291456 | tf_op jit(solution)/shard_map/all_to_all | solution.py:163
  28.6 6.9 %copy-start.12 = (f32[1,768,256]{2,1,0:T(8,128)S(1)}, f32[1,768,256]{2,1,0:T(8,128)}, u32[]{:S(2)}) copy-start(f32[1,768,256]{2,1,0:T(8,128)} %param.21) | copy-start | bytes 2359300
  28.6 7.8 %copy-start.13 = (f32[1,768,256]{2,1,0:T(8,128)S(1)}, f32[1,768,256]{2,1,0:T(8,128)}, u32[]{:S(2)}) copy-start(f32[1,768,256]{2,1,0:T(8,128)} %param.22) | copy-start | bytes 2359300
  28.6 11.5 %copy-start.20 = (bf16[128,2048]{1,0:T(8,128)(2,1)S(1)}, bf16[128,2048]{1,0:T(8,128)(2,1)}, u32[]{:S(2)}) copy-start(bf16[128,2048]{1,0:T(8,128)(2,1)} %param.23) | copy-start | bytes 1572868
  28.6 181.9 %collective-permute-start = (bf16[1,2,256,768]{3,2,1,0:T(8,128)(2,1)S(1)}, bf16[1,2,256,768]{3,2,1,0:T(8,128)(2,1)}, u32[]{:S(2)}, u32[]{:S(2)}) collective-permute-start(bf16[1,2,256,768]{3,2,1,0:T(8,128)(2,1)S(1)} %copy-done.10), channel_id=1, source_target_pairs={{64,0},{72,8},{80,16},{88,24},{96,32},{104,40},{112,48},{120,56},{... | collective-permute-start | bytes 2359304 | tf_op jit(solution)/shard_map/ppermute | solution.py:20
  31.6 178.9 %collective-permute-start.1 = (bf16[1,768,256]{2,1,0:T(8,128)(2,1)S(1)}, bf16[1,768,256]{2,1,0:T(8,128)(2,1)}, u32[]{:S(2)}, u32[]{:S(2)}) collective-permute-start(bf16[1,768,256]{2,1,0:T(8,128)(2,1)S(1)} %copy-done.15), channel_id=1, source_target_pairs={{64,0},{72,8},{80,16},{88,24},{96,32},{104,40},{112,48},{120,56},{... | collective-permute-start | bytes 1179656 | tf_op jit(solution)/shard_map/ppermute | solution.py:20
  32.7 178.8 %collective-permute-start.2 = (bf16[1,2,256,768]{3,2,1,0:T(8,128)(2,1)}, bf16[1,2,256,768]{3,2,1,0:T(8,128)(2,1)}, u32[]{:S(2)}, u32[]{:S(2)}) collective-permute-start(bf16[1,2,256,768]{3,2,1,0:T(8,128)(2,1)} %convert_element_type.83), channel_id=1, source_target_pairs={{64,0},{72,8},{80,16},{88,24},{96,32},{104,40},{112,48},{120,56},{... | collective-permute-start | bytes 2359304 | tf_op jit(solution)/shard_map/ppermute | solution.py:20
  36.3 159.5 %collective-permute-start.4 = (bf16[1,768,256]{2,1,0:T(8,128)(2,1)}, bf16[1,768,256]{2,1,0:T(8,128)(2,1)}, u32[]{:S(2)}, u32[]{:S(2)}) collective-permute-start(bf16[1,768,256]{2,1,0:T(8,128)(2,1)} %convert_element_type.87), channel_id=1, source_target_pairs={{64,0},{72,8},{80,16},{88,24},{96,32},{104,40},{112,48},{120,56},{... | collective-permute-start | bytes 1179656 | tf_op jit(solution)/shard_map/ppermute | solution.py:20
  37.2 171.2 %collective-permute-start.5 = (bf16[1,768,256]{2,1,0:T(8,128)(2,1)}, bf16[1,768,256]{2,1,0:T(8,128)(2,1)}, u32[]{:S(2)}, u32[]{:S(2)}) collective-permute-start(bf16[1,768,256]{2,1,0:T(8,128)(2,1)} %convert_element_type.89), channel_id=1, source_target_pairs={{64,0},{72,8},{80,16},{88,24},{96,32},{104,40},{112,48},{120,56},{... | collective-permute-start | bytes 1179656 | tf_op jit(solution)/shard_map/ppermute | solution.py:20
  43.1 5.3 copy-start.21
  48.5 0.6 copy-start.18
  56.0 4.3 copy-start.25
  59.3 2.2 copy-start.8
  195.8 18.3 %collective-permute-start.3 = (bf16[1,2,256,768]{3,2,1,0:T(8,128)(2,1)}, bf16[1,2,256,768]{3,2,1,0:T(8,128)(2,1)}, u32[]{:S(2)}, u32[]{:S(2)}) collective-permute-start(bf16[1,2,256,768]{3,2,1,0:T(8,128)(2,1)} %convert_element_type.85), channel_id=1, source_target_pairs={{64,0},{72,8},{80,16},{88,24},{96,32},{104,40},{112,48},{120,56},{... | collective-permute-start | bytes 2359304 | tf_op jit(solution)/shard_map/ppermute | solution.py:20
  198.6 51.7 %all-to-all-start.2 = ((bf16[16,48,2048]{2,1,0:T(8,128)(2,1)}), bf16[16,48,2048]{2,1,0:T(8,128)(2,1)}, u32[]{:S(2)}, u32[]{:S(2)}) async-start(bf16[16,48,2048]{2,1,0:T(8,128)(2,1)} %select_select_fusion), calls=%async_computation.2 | async-start | bytes 6291456 | tf_op jit(solution)/shard_map/all_to_all | solution.py:190
  205.5 4.9 copy-start.16
  205.5 273.6 %reduce-scatter.2.cloned.1.call-start = ((), (), s32[]{:S(2)}) async-start(), calls=%async_computation.5 | async-start | bytes 10616832 | tf_op jit(solution)/shard_map/reduce_scatter | solution.py:212
  206.0 2.3 copy-start.14
  208.4 3.1 copy-start.7
  219.8 30.6 %copy-start.11 = (bf16[768,8,256]{0,2,1:T(8,128)(2,1)}, bf16[768,8,256]{0,2,1:T(8,128)(2,1)S(1)}, u32[]{:S(2)}) copy-start(bf16[768,8,256]{0,2,1:T(8,128)(2,1)S(1)} %copy.26) | copy-start | bytes 9437188
  219.8 8.1 %copy-start.22 = (bf16[8,256,768]{2,1,0:T(8,128)(2,1)S(1)}, bf16[8,256,768]{2,1,0:T(8,128)(2,1)}, u32[]{:S(2)}) copy-start(bf16[8,256,768]{2,1,0:T(8,128)(2,1)} %get-tuple-element.25) | copy-start | bytes 9437188
  256.6 6.0 %copy-start.27 = (bf16[768,768]{0,1:T(8,128)(2,1)}, bf16[768,768]{0,1:T(8,128)(2,1)S(1)}, u32[]{:S(2)}) copy-start(bf16[768,768]{0,1:T(8,128)(2,1)S(1)} %get-tuple-element.43) | copy-start | bytes 3538948
  256.6 6.0 %copy-start.26 = (bf16[768,768]{0,1:T(8,128)(2,1)}, bf16[768,768]{0,1:T(8,128)(2,1)S(1)}, u32[]{:S(2)}) copy-start(bf16[768,768]{0,1:T(8,128)(2,1)S(1)} %get-tuple-element.42) | copy-start | bytes 3538948
  256.6 6.0 %copy-start.28 = (bf16[768,768]{0,1:T(8,128)(2,1)}, bf16[768,768]{0,1:T(8,128)(2,1)S(1)}, u32[]{:S(2)}) copy-start(bf16[768,768]{0,1:T(8,128)(2,1)S(1)} %get-tuple-element.41) | copy-start | bytes 3538948
  282.7 1.9 copy-start.24
  284.6 4.1 copy-start.23
  284.6 4.1 copy-start.29
  292.8 51.1 %all-to-all-start.3 = ((bf16[16,48,2048]{2,1,0:T(8,128)(2,1)}), bf16[16,48,2048]{2,1,0:T(8,128)(2,1)S(1)}, u32[]{:S(2)}, u32[]{:S(2)}) async-start(bf16[16,48,2048]{2,1,0:T(8,128)(2,1)} %bitcast.93), calls=%async_computation.3 | async-start | bytes 6291456 | tf_op jit(solution)/shard_map/all_to_all | solution.py:199
  344.0 141.7 %all-to-all-start.1 = ((bf16[16,48,2048]{2,1,0:T(8,128)(2,1)}), bf16[16,48,2048]{2,1,0:T(8,128)(2,1)}, u32[]{:S(2)}, u32[]{:S(2)}) async-start(bf16[16,48,2048]{2,1,0:T(8,128)(2,1)} %bitcast.92), calls=%async_computation.1 | async-start | bytes 6291456 | tf_op jit(solution)/shard_map/all_to_all | solution.py:173
  479.1 37.0 %collective-permute-start.6 = (bf16[256,2304]{0,1:T(8,128)(2,1)}, bf16[256,2304]{0,1:T(8,128)(2,1)}, u32[]{:S(2)}, u32[]{:S(2)}) collective-permute-start(bf16[256,2304]{0,1:T(8,128)(2,1)} %reduce-scatter.2.cloned.1.call-done), channel_id=1, source_target_pairs={{64,0},{72,8},{80,16},{88,24},{96,32},{104,40},{112,48},{120,56},{... | collective-permute-start | bytes 3538952 | tf_op jit(solution)/shard_map/ppermute | solution.py:20
  485.6 7.7 %copy-start.2 = (bf16[512,2048]{1,0:T(8,128)(2,1)S(1)}, bf16[512,2048]{1,0:T(8,128)(2,1)}, u32[]{:S(2)}) copy-start(bf16[512,2048]{1,0:T(8,128)(2,1)} %gather_fusion.3) | copy-start | bytes 6291460
  506.0 3.9 copy-start.19
  509.9 6.3 %copy-start.17 = (bf16[256,2304]{0,1:T(8,128)(2,1)S(1)}, bf16[256,2304]{0,1:T(8,128)(2,1)}, u32[]{:S(2)}) copy-start(bf16[256,2304]{0,1:T(8,128)(2,1)} %reduce-scatter.2.cloned.1.call-done) | copy-start | bytes 3538948
  517.7 6.3 %copy-start.9 = (bf16[1,2,256,768]{3,2,1,0:T(8,128)(2,1)S(1)}, bf16[1,2,256,768]{3,2,1,0:T(8,128)(2,1)}, u32[]{:S(2)}) copy-start(bf16[1,2,256,768]{3,2,1,0:T(8,128)(2,1)} %broadcast_select_fusion.1) | copy-start | bytes 2359300
  520.8 3.2 copy-start.3
  520.8 3.2 copy-start.4
  520.8 3.2 copy-start.5
  524.0 2.7 copy-start.1
Sparse Core Ops, SparseCore 0:
  282.9 196.1 reduce-scatter.1

commit v6 on v4

--- a/solution.py
+++ b/solution.py
@@ -136,7 +136,7 @@
     own_partner = jnp.sum(jnp.where(expert_range == row_index, partner, 0))
     take_other = own_partner != row_index
     moved_weights = shifted((w_in, w_down), "expert", halfway)
-    kept_in, kept_down = (
+    w_in, w_down = (
         jnp.where(take_other, moved, owned) for moved, owned in zip(moved_weights, (w_in, w_down))
     )
     moved_states = tuple(
@@ -155,7 +155,7 @@
     up_weight = in_full[0, 1]
     down_weight = down_full[0]
     hidden_width = gate_weight.shape[1]
-    position, filler = route_table(expert_ids, expert_ids, groups, capacity)
+    position, filler = route_table(expert_ids, partner[expert_ids], groups, capacity)
     token_fill = jnp.where(filler >= 0, filler // top_count, -1)
     send_rows = fill_rows(tokens, token_fill, groups, capacity)
     arrived = lax.all_to_all(send_rows, "expert", split_axis=0, concat_axis=0, tiled=True)
@@ -207,22 +207,25 @@
     token_grad = jnp.sum(per_back.astype(jnp.float32), axis=1).astype(jnp.bfloat16)
     grad_both = jnp.concatenate([grad_gate, grad_up], axis=1)
     share_rows = width // lax.axis_size("shard")
-    partial = jnp.concatenate(
-        [contract_rows(rows_x, grad_both), contract_rows(dout_rows, hidden)], axis=1
-    ).astype(jnp.bfloat16)
+    down_part, in_part = lax.optimization_barrier(
+        (
+            contract_rows(dout_rows, hidden).astype(jnp.bfloat16),
+            contract_rows(rows_x, grad_both).astype(jnp.bfloat16),
+        )
+    )
+    down_share = lax.psum_scatter(
+        down_part, "shard", scatter_dimension=0, tiled=True
+    ).astype(jnp.float32)
     shard_count = lax.axis_size("shard")
     (arrived_parts,) = exchange(
-        (partial.reshape(shard_count, share_rows, partial.shape[1]),), False, 1
-    )
-    summed = jnp.sum(arrived_parts.astype(jnp.float32), axis=0).astype(jnp.bfloat16)
-    shares = jnp.where(take_other, shifted(summed, "expert", halfway), summed).astype(jnp.float32)
-    grad_in = jnp.transpose(
-        shares[:, : 2 * hidden_width].reshape(share_rows, 2, hidden_width), (1, 0, 2)
-    )[None]
-    grad_down = jnp.transpose(shares[:, 2 * hidden_width :])[None]
-    new_in, first_in, second_in = adam_update(kept_in, own_moments[0], own_moments[1], grad_in)
+        (in_part.reshape(shard_count, share_rows, in_part.shape[1]),), False, 1
+    )
+    in_share = jnp.sum(arrived_parts.astype(jnp.float32), axis=0)
+    grad_in = jnp.transpose(in_share.reshape(share_rows, 2, hidden_width), (1, 0, 2))[None]
+    grad_down = jnp.transpose(down_share)[None]
+    new_in, first_in, second_in = adam_update(w_in, own_moments[0], own_moments[1], grad_in)
     new_down, first_down, second_down = adam_update(
-        kept_down, own_moments[2], own_moments[3], grad_down
+        w_down, own_moments[2], own_moments[3], grad_down
     )
     return (mixed, token_grad, new_in, new_down, first_in, second_in, first_down, second_down)
 

time: 647 us -> 506 us (0.78)
  the two profiles are of different devices: /device:TPU:1 before, /device:TPU:57 now
where the time goes in v6:
time: 506 us; the launch traced here: 499 us
  waiting for transfers between devices  160 us (32%)
  Pallas kernels  107 us (21%)
  local copies, waits for them, and re-layouts  68.9 us (14%)
  other arithmetic  61 us (12%)
  matrix products  45.2 us (9%)
  starting transfers between devices  42.8 us (8%)
  between operations  14.9 us (3%)
    pallas_call x1, Pallas kernels, exchange(): pl.pallas_call(functools.partial(exchange_kernel, count, spread, width),...  107 us
    all_gather x1, waiting for transfers between devices, body(): lax.all_gather(w_in, 'shard', axis=2, tiled=True)  55.2 us
    all_to_all x1, waiting for transfers between devices, body(): lax.all_to_all(send_rows, 'expert', split_axis=0, concat_axis=0, tiled=True)  31.4 us
    all_to_all x1, waiting for transfers between devices, body(): lax.all_to_all(send_grads, 'expert', split_axis=0, concat_axis=0, tiled=T...  30.6 us
    ppermute x6, waiting for transfers between devices, shifted(): return lax.ppermute(block, axis, route)  26.6 us
    unnamed x50, local copies, waits for them, and re-layouts  25.4 us
    all_to_all x1, waiting for transfers between devices, body(): lax.all_to_all(entry_grads.reshape(groups, capacity, width), 'expert', sp...  15.6 us
    dot_general x2, matrix products, contract_rows(): lax.dot_general(left, right, (((0,), (0,)), ((), ())), preferred_element_...  15.5 us
  transfers between devices with their start and end apart: 13, of which 6 were waited for; matrix products, arithmetic and copies ran while one was open for 30% of the time, Pallas kernels for 21%

profile of v6, /device:TPU:57, one launch (start us, length us, event | category | flops | bytes accessed | tf_op | source)
XLA Modules:
  0.0 499.5 jit_solution(6555147841310745960)
XLA Ops:
  11.5 8.6 %collective-permute-done.1 = bf16[1,768,256]{1,2,0:T(8,128)(2,1)S(1)} collective-permute-done((bf16[1,768,256]{1,2,0:T(8,128)(2,1)S(1)}, bf16[1,768,256]{1,2,0:T(8,128)(2,1)S(1)}, u32[]{:S(2)}, u32[]{:S(2)}) %collective-permute-start.1) | collective-permute-done | bytes 393248 | tf_op jit(solution)/shard_map/ppermute | solution.py:20
  22.3 18.0 %collective-permute-done = bf16[1,2,256,768]{2,3,1,0:T(8,128)(2,1)S(1)} collective-permute-done((bf16[1,2,256,768]{2,3,1,0:T(8,128)(2,1)S(1)}, bf16[1,2,256,768]{2,3,1,0:T(8,128)(2,1)S(1)}, u32[]{:S(2)}, u32[]{:S(2)}) %collective-permute-start) | collective-permute-done | bytes 786464 | tf_op jit(solution)/shard_map/ppermute | solution.py:20
  42.4 10.1 %select_multiply_fusion = s32[128,4]{0,1:T(4,128)S(1)} fusion(s32[128,4]{0,1:T(4,128)S(1)} %copy-done.13, s32[]{:T(128)} %bitcast, s32[]{:T(128)} %bitcast.1, s32[]{:T(128)} %bitcast.2, s32[]{:T(128)} %bitcast.3, s32[]{:T(128)} %bitcast.4, s32[]{:T(128)} %bitcast.5, s32[]{:T(128)} %bitcast.6, s32[]{:T(128)} %bitcast.7, s32[]{:T(128)} %bitcast.8, s32[]{:T(128)} %bitcast.9, ...), kind=kLoop, calls=%fused_computation.68 | loop fusion | flops 17408 | bytes 4160 | tf_op jit(solution)/shard_map/mul | solution.py:101
  54.4 3.2 mul.160
  57.6 5.3 %mul.161 = f32[512,2048]{1,0:T(8,128)} reshape(f32[128,4,2048]{2,1,0:T(4,128)} %mul.160) | data formatting | bytes 8388608 | tf_op jit(solution)/shard_map/mul | solution.py:184
  63.0 2.4 scatter_custom_fusion
  65.7 2.5 multiply_convert_fusion
  68.2 4.3 gather_fusion.1
  72.4 3.3 select_select_fusion
  75.8 7.7 %all-to-all-start.2 = ((bf16[16,48,2048]{2,1,0:T(8,128)(2,1)}), bf16[16,48,2048]{2,1,0:T(8,128)(2,1)}, u32[]{:S(2)}, u32[]{:S(2)}) async-start(bf16[16,48,2048]{2,1,0:T(8,128)(2,1)} %select_select_fusion), calls=%async_computation.2 | async-start | bytes 6291456 | tf_op jit(solution)/shard_map/all_to_all | solution.py:188
  83.6 4.3 gather_fusion
  87.9 3.3 select_select_fusion.1
  91.2 30.6 %all-to-all-done.2 = bf16[16,48,2048]{2,1,0:T(8,128)(2,1)} async-done(((bf16[16,48,2048]{2,1,0:T(8,128)(2,1)}), bf16[16,48,2048]{2,1,0:T(8,128)(2,1)}, u32[]{:S(2)}, u32[]{:S(2)}) %all-to-all-start.2) | async-done | bytes 3145760 | tf_op jit(solution)/shard_map/all_to_all | solution.py:188
  121.9 10.0 %all-to-all-start = ((bf16[16,48,2048]{2,1,0:T(8,128)(2,1)}), bf16[16,48,2048]{2,1,0:T(8,128)(2,1)S(1)}, u32[]{:S(2)}, u32[]{:S(2)}) async-start(bf16[16,48,2048]{2,1,0:T(8,128)(2,1)} %select_select_fusion.1), calls=%async_computation | async-start | bytes 6291456 | tf_op jit(solution)/shard_map/all_to_all | solution.py:161
  131.9 6.9 %fusion = f32[768,768]{0,1:T(8,128)} fusion(bf16[768,2048]{1,0:T(8,128)(2,1)} %bitcast.27, bf16[1,768,2048]{1,2,0:T(8,128)(2,1)} %all-gather.5.cloned.1.call-done), kind=kOutput, calls=%fused_computation.14 | convolution fusion | flops 2415919104 | bytes 8650752 | tf_op jit(solution)/shard_map/dot_general | solution.py:120
  138.8 31.4 %all-to-all-done = bf16[16,48,2048]{2,1,0:T(8,128)(2,1)S(1)} async-done(((bf16[16,48,2048]{2,1,0:T(8,128)(2,1)}), bf16[16,48,2048]{2,1,0:T(8,128)(2,1)S(1)}, u32[]{:S(2)}, u32[]{:S(2)}) %all-to-all-start) | async-done | bytes 3145760 | tf_op jit(solution)/shard_map/all_to_all | solution.py:161
  170.2 55.2 %all-gather.3.cloned.1.call-done = bf16[1,2,2048,768]{2,3,1,0:T(8,128)(2,1)} async-done(((bf16[1,2,256,768]{2,3,1,0:T(8,128)(2,1)}), bf16[1,2,2048,768]{2,3,1,0:T(8,128)(2,1)}) %all-gather.3.cloned.1.call-update) | async-done | bytes 6291472 | tf_op jit(solution)/shard_map/all_gather | solution.py:151
  225.4 4.7 fusion.5
  230.1 4.6 multiply_convert_fusion.2
  234.7 2.7 fusion.4
  237.4 4.3 add_convert_fusion
  241.7 6.6 %all-to-all-start.3 = ((bf16[16,48,2048]{2,1,0:T(8,128)(2,1)}), bf16[16,48,2048]{2,1,0:T(8,128)(2,1)S(1)}, u32[]{:S(2)}, u32[]{:S(2)}) async-start(bf16[16,48,2048]{2,1,0:T(8,128)(2,1)} %bitcast.105), calls=%async_computation.3 | async-start | bytes 6291456 | tf_op jit(solution)/shard_map/all_to_all | solution.py:197
  248.6 9.2 %convolution_convert_fusion = bf16[2048,1536]{1,0:T(8,128)(2,1)} fusion(bf16[768,2048]{1,0:T(8,128)(2,1)} %bitcast.104, bf16[768,768]{0,1:T(8,128)(2,1)} %copy-done.9, bf16[768,768]{0,1:T(8,128)(2,1)} %copy-done.16), kind=kOutput, calls=%fused_computation.6 | convolution fusion | flops 4839702528 | bytes 11796480 | tf_op jit(solution)/shard_map/dot_general | solution.py:114
  257.8 6.3 %convolution_convert_fusion.1 = bf16[2048,768]{1,0:T(8,128)(2,1)} fusion(bf16[768,2048]{1,0:T(8,128)(2,1)} %bitcast.27, bf16[768,768]{0,1:T(8,128)(2,1)S(1)} %copy-done.17), kind=kOutput, calls=%fused_computation.10 | convolution fusion | flops 2417491968 | bytes 7471104 | tf_op jit(solution)/shard_map/dot_general | solution.py:114
  264.1 6.6 %convolution_convert_fusion.2 = bf16[768,2048]{1,0:T(8,128)(2,1)} fusion(bf16[768,768]{0,1:T(8,128)(2,1)} %get-tuple-element.47, bf16[1,768,2048]{1,2,0:T(8,128)(2,1)} %all-gather.5.cloned.1.call-done), kind=kOutput, calls=%fused_computation.11 | convolution fusion | flops 2417491968 | bytes 7471104 | tf_op jit(solution)/shard_map/dot_general | solution.py:168
  270.7 15.6 %all-to-all-done.3 = bf16[16,48,2048]{2,1,0:T(8,128)(2,1)S(1)} async-done(((bf16[16,48,2048]{2,1,0:T(8,128)(2,1)}), bf16[16,48,2048]{2,1,0:T(8,128)(2,1)S(1)}, u32[]{:S(2)}, u32[]{:S(2)}) %all-to-all-start.3) | async-done | bytes 3145760 | tf_op jit(solution)/shard_map/all_to_all | solution.py:197
  286.3 9.8 %all-to-all-start.1 = ((bf16[16,48,2048]{2,1,0:T(8,128)(2,1)}), bf16[16,48,2048]{2,1,0:T(8,128)(2,1)}, u32[]{:S(2)}, u32[]{:S(2)}) async-start(bf16[16,48,2048]{2,1,0:T(8,128)(2,1)} %bitcast.101), calls=%async_computation.1 | async-start | bytes 6291456 | tf_op jit(solution)/shard_map/all_to_all | solution.py:171
  296.1 3.1 copy.65
  299.2 2.4 convert_element_type.100
  302.7 3.1 copy.68
  305.8 2.4 convert_element_type.105
  309.9 2.3 copy.70
  321.9 107.1 %shard_map.170 = bf16[8,256,1536]{2,1,0:T(8,128)(2,1)} custom-call(bf16[8,256,1536]{2,1,0:T(8,128)(2,1)} %bitcast.99), custom_call_target="tpu_custom_call" | custom-call | bytes 12582912 | tf_op jit(solution)/shard_map/pallas_call | solution.py:64
  428.9 5.0 convert_reduce_fusion
  433.9 3.0 copy.67
  436.9 5.9 %subtract_convert_fusion = (bf16[1,2,256,768]{2,3,1,0:T(8,128)(2,1)}, f32[1,2,256,768]{2,3,1,0:T(8,128)}, f32[1,2,256,768]{2,3,1,0:T(8,128)}) fusion(bf16[1,2,256,768]{2,3,1,0:T(8,128)(2,1)} %broadcast_select_fusion.1, f32[2,256,768]{1,2,0:T(8,128)} %bitcast.100, f32[1,2,256,768]{2,3,1,0:T(8,128)} %copy.65, ...), kind=kLoop, calls=%fused_computation.36 | loop fusion | flops 7077888 | bytes 11010049 | tf_op jit(solution)/shard_map/convert_element_type | solution.py:92
  442.8 3.0 copy.76
  445.8 3.0 copy.77
  448.8 2.4 copy.74
  451.3 3.3 gather_fusion.3
  454.5 7.8 %gather_fusion.2 = bf16[512,2048]{1,0:T(8,128)(2,1)} fusion(bf16[768,2048]{1,0:T(8,128)(2,1)} %bitcast.25, s32[1024]{0:T(1024)S(1)} %pad_clamp_fusion.1), kind=kCustom, calls=%fused_computation.clone | custom fusion | bytes 4196352 | tf_op jit(solution)/shard_map/jit(_take)/gather | solution.py:178
  462.3 4.8 broadcast_select_fusion
  467.1 5.2 %reshape.157 = f32[128,4,2048]{2,1,0:T(4,128)} reshape(f32[512,2048]{1,0:T(8,128)} %get-tuple-element.55) | data formatting | bytes 8388608 | tf_op jit(solution)/shard_map/convert_element_type | solution.py:181
  472.2 2.9 reshape.154
  475.1 3.9 reduce_sum.54
  479.0 6.3 %multiply_reduce_fusion = bf16[128,2048]{1,0:T(8,128)(2,1)} fusion(f32[128,4,2048]{2,1,0:T(4,128)} %reshape.157, f32[128,4]{1,0:T(8,128)S(1)} %copy.54), kind=kLoop, calls=%fused_computation.9 | loop fusion | flops 1835008 | bytes 4720640 | tf_op jit(solution)/shard_map/reduce_sum | solution.py:181
  485.4 3.0 subtract_convert_fusion.1
  488.3 2.3 copy.78
  (91 shorter events, 25.2 us)
Async XLA Ops:
  7.2 76.5 %copy-start = (bf16[128,2048]{1,0:T(8,128)(2,1)S(1)}, bf16[128,2048]{1,0:T(8,128)(2,1)}, u32[]{:S(2)}) copy-start(bf16[128,2048]{1,0:T(8,128)(2,1)} %param.13) | copy-start | bytes 1572868
  7.2 13.8 %copy-start.10 = (bf16[1,2,256,768]{3,2,1,0:T(8,128)(2,1)S(1)}, bf16[1,2,256,768]{3,2,1,0:T(8,128)(2,1)}, u32[]{:S(2)}) copy-start(bf16[1,2,256,768]{3,2,1,0:T(8,128)(2,1)} %param.17) | copy-start | bytes 2359300
  7.2 124.7 %all-gather.5.cloned.1.call-start = ((), (), s32[]{:S(2)}) async-start(), calls=%async_computation.6 | async-start | bytes 3538944 | tf_op jit(solution)/shard_map/all_gather | solution.py:152
  8.5 11.6 %collective-permute-start.1 = (bf16[1,768,256]{1,2,0:T(8,128)(2,1)S(1)}, bf16[1,768,256]{1,2,0:T(8,128)(2,1)S(1)}, u32[]{:S(2)}, u32[]{:S(2)}) collective-permute-start(bf16[1,768,256]{1,2,0:T(8,128)(2,1)S(1)} %copy.62), channel_id=1, source_target_pairs={{64,0},{72,8},{80,16},{88,24},{96,32},{104,40},{112,48},{120,56},{... | collective-permute-start | bytes 1179656 | tf_op jit(solution)/shard_map/ppermute | solution.py:20
  20.9 20.4 %copy-start.13 = (s32[128,4]{0,1:T(4,128)S(1)}, s32[128,4]{0,1:T(4,128)}, u32[]{:S(2)}) copy-start(s32[128,4]{0,1:T(4,128)} %param.14) | copy-start | bytes 6148
  20.9 20.8 %copy-start.12 = (s32[16]{0:T(128)S(1)}, s32[16]{0:T(128)}, u32[]{:S(2)}) copy-start(s32[16]{0:T(128)} %param.16) | copy-start | bytes 196
  20.9 33.3 %copy-start.14 = (f32[128,4]{0,1:T(4,128)S(1)}, f32[128,4]{0,1:T(4,128)}, u32[]{:S(2)}) copy-start(f32[128,4]{0,1:T(4,128)} %param.15) | copy-start | bytes 6148
  20.9 33.5 %copy-start.11 = (bf16[128,2048]{1,0:T(8,128)(2,1)S(1)}, bf16[128,2048]{1,0:T(8,128)(2,1)}, u32[]{:S(2)}) copy-start(bf16[128,2048]{1,0:T(8,128)(2,1)} %param.23) | copy-start | bytes 1572868
  20.9 204.5 %all-gather.3.cloned.1.call-start = ((), (), s32[]{:S(2)}) async-start(), calls=%async_computation.5 | async-start | bytes 7077888 | tf_op jit(solution)/shard_map/all_gather | solution.py:151
  21.3 19.1 %collective-permute-start = (bf16[1,2,256,768]{2,3,1,0:T(8,128)(2,1)S(1)}, bf16[1,2,256,768]{2,3,1,0:T(8,128)(2,1)S(1)}, u32[]{:S(2)}, u32[]{:S(2)}) collective-permute-start(bf16[1,2,256,768]{2,3,1,0:T(8,128)(2,1)S(1)} %copy.60), channel_id=1, source_target_pairs={{64,0},{72,8},{80,16},{88,24},{96,32},{104,40},{112,48},{120,56},{... | collective-permute-start | bytes 2359304 | tf_op jit(solution)/shard_map/ppermute | solution.py:20
  75.8 46.1 %all-to-all-start.2 = ((bf16[16,48,2048]{2,1,0:T(8,128)(2,1)}), bf16[16,48,2048]{2,1,0:T(8,128)(2,1)}, u32[]{:S(2)}, u32[]{:S(2)}) async-start(bf16[16,48,2048]{2,1,0:T(8,128)(2,1)} %select_select_fusion), calls=%async_computation.2 | async-start | bytes 6291456 | tf_op jit(solution)/shard_map/all_to_all | solution.py:188
  121.9 48.3 %all-to-all-start = ((bf16[16,48,2048]{2,1,0:T(8,128)(2,1)}), bf16[16,48,2048]{2,1,0:T(8,128)(2,1)S(1)}, u32[]{:S(2)}, u32[]{:S(2)}) async-start(bf16[16,48,2048]{2,1,0:T(8,128)(2,1)} %select_select_fusion.1), calls=%async_computation | async-start | bytes 6291456 | tf_op jit(solution)/shard_map/all_to_all | solution.py:161
  170.2 59.9 %copy-start.6 = (bf16[16,48,2048]{2,1,0:T(8,128)(2,1)}, bf16[16,48,2048]{2,1,0:T(8,128)(2,1)S(1)}, u32[]{:S(2)}) copy-start(bf16[16,48,2048]{2,1,0:T(8,128)(2,1)S(1)} %all-to-all-done) | copy-start | bytes 9437188
  225.4 4.7 copy-start.7
  225.4 4.7 copy-start.15
  234.7 2.7 copy-start.9
  234.7 2.7 copy-start.16
  241.7 44.6 %all-to-all-start.3 = ((bf16[16,48,2048]{2,1,0:T(8,128)(2,1)}), bf16[16,48,2048]{2,1,0:T(8,128)(2,1)S(1)}, u32[]{:S(2)}, u32[]{:S(2)}) async-start(bf16[16,48,2048]{2,1,0:T(8,128)(2,1)} %bitcast.105), calls=%async_computation.3 | async-start | bytes 6291456 | tf_op jit(solution)/shard_map/all_to_all | solution.py:197
  248.3 237.0 %reduce-scatter.2.cloned.1.call-start = ((), (), s32[]{:S(2)}) async-start(), calls=%async_computation.7 | async-start | bytes 3538944 | tf_op jit(solution)/shard_map/reduce_scatter | solution.py:216
  248.6 9.2 %copy-start.17 = (bf16[768,768]{0,1:T(8,128)(2,1)S(1)}, bf16[768,768]{0,1:T(8,128)(2,1)}, u32[]{:S(2)}) copy-start(bf16[768,768]{0,1:T(8,128)(2,1)} %get-tuple-element.47) | copy-start | bytes 3538948
  286.3 168.2 %all-to-all-start.1 = ((bf16[16,48,2048]{2,1,0:T(8,128)(2,1)}), bf16[16,48,2048]{2,1,0:T(8,128)(2,1)}, u32[]{:S(2)}, u32[]{:S(2)}) async-start(bf16[16,48,2048]{2,1,0:T(8,128)(2,1)} %bitcast.101), calls=%async_computation.1 | async-start | bytes 6291456 | tf_op jit(solution)/shard_map/all_to_all | solution.py:171
  301.5 135.4 %collective-permute-start.2 = (bf16[1,2,256,768]{2,3,1,0:T(8,128)(2,1)}, bf16[1,2,256,768]{2,3,1,0:T(8,128)(2,1)}, u32[]{:S(2)}, u32[]{:S(2)}) collective-permute-start(bf16[1,2,256,768]{2,3,1,0:T(8,128)(2,1)} %convert_element_type.100), channel_id=1, source_target_pairs={{64,0},{72,8},{80,16},{88,24},{96,32},{104,40},{112,48},{120,56},{... | collective-permute-start | bytes 2359304 | tf_op jit(solution)/shard_map/ppermute | solution.py:20
  308.1 128.8 %collective-permute-start.3 = (bf16[1,2,256,768]{2,3,1,0:T(8,128)(2,1)}, bf16[1,2,256,768]{2,3,1,0:T(8,128)(2,1)}, u32[]{:S(2)}, u32[]{:S(2)}) collective-permute-start(bf16[1,2,256,768]{2,3,1,0:T(8,128)(2,1)} %convert_element_type.105), channel_id=1, source_target_pairs={{64,0},{72,8},{80,16},{88,24},{96,32},{104,40},{112,48},{120,56},{... | collective-permute-start | bytes 2359304 | tf_op jit(solution)/shard_map/ppermute | solution.py:20
  314.2 171.2 %collective-permute-start.4 = (bf16[1,768,256]{1,2,0:T(8,128)(2,1)}, bf16[1,768,256]{1,2,0:T(8,128)(2,1)}, u32[]{:S(2)}, u32[]{:S(2)}) collective-permute-start(bf16[1,768,256]{1,2,0:T(8,128)(2,1)} %convert_element_type.109), channel_id=1, source_target_pairs={{64,0},{72,8},{80,16},{88,24},{96,32},{104,40},{112,48},{120,56},{... | collective-permute-start | bytes 1179656 | tf_op jit(solution)/shard_map/ppermute | solution.py:20
  319.5 165.8 %collective-permute-start.5 = (bf16[1,768,256]{1,2,0:T(8,128)(2,1)}, bf16[1,768,256]{1,2,0:T(8,128)(2,1)}, u32[]{:S(2)}, u32[]{:S(2)}) collective-permute-start(bf16[1,768,256]{1,2,0:T(8,128)(2,1)} %convert_element_type.111), channel_id=1, source_target_pairs={{64,0},{72,8},{80,16},{88,24},{96,32},{104,40},{112,48},{120,56},{... | collective-permute-start | bytes 1179656 | tf_op jit(solution)/shard_map/ppermute | solution.py:20
  454.5 7.8 %copy-start.2 = (bf16[512,2048]{1,0:T(8,128)(2,1)S(1)}, bf16[512,2048]{1,0:T(8,128)(2,1)}, u32[]{:S(2)}) copy-start(bf16[512,2048]{1,0:T(8,128)(2,1)} %gather_fusion.3) | copy-start | bytes 6291460
  479.0 6.3 %copy-start.3 = (f32[1,768,256]{1,2,0:T(8,128)S(1)}, f32[1,768,256]{1,2,0:T(8,128)}, u32[]{:S(2)}) copy-start(f32[1,768,256]{1,2,0:T(8,128)} %copy.70) | copy-start | bytes 2359300
  479.0 6.4 %copy-start.4 = (f32[1,768,256]{1,2,0:T(8,128)S(1)}, f32[1,768,256]{1,2,0:T(8,128)}, u32[]{:S(2)}) copy-start(f32[1,768,256]{1,2,0:T(8,128)} %copy.72) | copy-start | bytes 2359300
  479.0 6.4 %copy-start.5 = (bf16[1,768,256]{1,2,0:T(8,128)(2,1)S(1)}, bf16[1,768,256]{1,2,0:T(8,128)(2,1)}, u32[]{:S(2)}) copy-start(bf16[1,768,256]{1,2,0:T(8,128)(2,1)} %broadcast_select_fusion.2) | copy-start | bytes 1179652
  485.4 7.4 %copy-start.1 = (bf16[128,2048]{1,0:T(8,128)(2,1)S(1)}, bf16[128,2048]{1,0:T(8,128)(2,1)}, u32[]{:S(2)}) copy-start(bf16[128,2048]{1,0:T(8,128)(2,1)} %param.13) | copy-start | bytes 1572868
  488.3 3.5 copy-start.8
Sparse Core Ops, SparseCore 0:
  21.0 64.4 all-gather.4
  88.2 137.1 all-gather.2
  264.2 199.2 reduce-scatter.1

commit v7 on v5

--- a/solution.py
+++ b/solution.py
@@ -136,7 +136,7 @@
     own_partner = jnp.sum(jnp.where(expert_range == row_index, partner, 0))
     take_other = own_partner != row_index
     moved_weights = shifted((w_in, w_down), "expert", halfway)
-    kept_in, kept_down = (
+    w_in, w_down = (
         jnp.where(take_other, moved, owned) for moved, owned in zip(moved_weights, (w_in, w_down))
     )
     moved_states = tuple(
@@ -147,17 +147,13 @@
         jnp.where(take_other, moved, owned)
         for moved, owned in zip(moved_states, (m_in, v_in, m_down, v_down))
     )
-    gate_parts, up_parts, down_parts = exchange((w_in[0, 0], w_in[0, 1], w_down[0]), True, 0)
-    (gate_parts, up_parts, down_parts), kept_in, kept_down, m_in, v_in, m_down, v_down = (
-        lax.optimization_barrier(
-            ((gate_parts, up_parts, down_parts), kept_in, kept_down, m_in, v_in, m_down, v_down)
-        )
-    )
+    down_full = lax.all_gather(w_down, "shard", axis=2, tiled=True)
+    gate_parts, up_parts = exchange((w_in[0, 0], w_in[0, 1]), True, 0)
     gate_weight = gate_parts.reshape(-1, gate_parts.shape[-1])
     up_weight = up_parts.reshape(-1, up_parts.shape[-1])
-    down_weight = jnp.transpose(down_parts, (1, 0, 2)).reshape(down_parts.shape[1], -1)
+    down_weight = down_full[0]
     hidden_width = gate_weight.shape[1]
-    position, filler = route_table(expert_ids, expert_ids, groups, capacity)
+    position, filler = route_table(expert_ids, partner[expert_ids], groups, capacity)
     token_fill = jnp.where(filler >= 0, filler // top_count, -1)
     send_rows = fill_rows(tokens, token_fill, groups, capacity)
     arrived = lax.all_to_all(send_rows, "expert", split_axis=0, concat_axis=0, tiled=True)
@@ -216,15 +212,14 @@
         "shard",
         scatter_dimension=0,
         tiled=True,
-    )
-    shares = jnp.where(take_other, shifted(shares, "expert", halfway), shares).astype(jnp.float32)
+    ).astype(jnp.float32)
     grad_in = jnp.transpose(
         shares[:, : 2 * hidden_width].reshape(share_rows, 2, hidden_width), (1, 0, 2)
     )[None]
     grad_down = jnp.transpose(shares[:, 2 * hidden_width :])[None]
-    new_in, first_in, second_in = adam_update(kept_in, own_moments[0], own_moments[1], grad_in)
+    new_in, first_in, second_in = adam_update(w_in, own_moments[0], own_moments[1], grad_in)
     new_down, first_down, second_down = adam_update(
-        kept_down, own_moments[2], own_moments[3], grad_down
+        w_down, own_moments[2], own_moments[3], grad_down
     )
     return (mixed, token_grad, new_in, new_down, first_in, second_in, first_down, second_down)
 

time: 542 us -> 511 us (0.943)
  Pallas kernels: 133 us -> 97.7 us
  waiting for transfers between devices: 185 us -> 191 us
    reduce_scatter x1, waiting for transfers between devices: 131 us -> 51.8 us  [body(): lax.psum_scatter(jnp.concatenate([contract_rows(rows_x, grad_both), contr...]
    ppermute x7 -> x6, waiting for transfers between devices: 0.16 us -> 56.8 us  [shifted(): return lax.ppermute(block, axis, route)]
    pallas_call x1, Pallas kernels: 133 us -> 97.7 us  [exchange(): pl.pallas_call(functools.partial(exchange_kernel, count, spread, width),...]
    all_to_all x1, waiting for transfers between devices: 0.01 us -> 30.5 us  [body(): lax.all_to_all(expert_out.reshape(groups, capacity, width), 'expert', spl...]
    all_to_all x1, waiting for transfers between devices: 0.01 us -> 18.6 us  [body(): lax.all_to_all(send_rows, 'expert', split_axis=0, concat_axis=0, tiled=True)]
    all_to_all x1, waiting for transfers between devices: 16.3 us -> 0.01 us  [body(): lax.all_to_all(send_grads, 'expert', split_axis=0, concat_axis=0, tiled=T...]
    mul x1, other arithmetic: 0.74 us -> 10.8 us  [route_table(): position = dest_rows.reshape(entry_count) * capacity + slot_index]
    select_n x6 -> x2, other arithmetic: 10.3 us -> 0.88 us  [body(): jnp.where(take_other, moved, owned)]
  transfers between devices with their start and end apart: 12 -> 12, of which waited for: 4 -> 5; matrix products, arithmetic and copies ran while one was open for 19% -> 24% of each run, Pallas kernels for 25% -> 19%
where the time goes in v7:
time: 511 us; the launch traced here: 504 us
  waiting for transfers between devices  191 us (37%)
  Pallas kernels  97.7 us (19%)
  other arithmetic  62.6 us (12%)
  local copies, waits for them, and re-layouts  50.6 us (10%)
  matrix products  46.1 us (9%)
  starting transfers between devices  41.3 us (8%)
  between operations  15.3 us (3%)
    pallas_call x1, Pallas kernels, exchange(): pl.pallas_call(functools.partial(exchange_kernel, count, spread, width),...  97.7 us
    ppermute x6, waiting for transfers between devices, shifted(): return lax.ppermute(block, axis, route)  56.8 us
    reduce_scatter x1, waiting for transfers between devices, body(): lax.psum_scatter(jnp.concatenate([contract_rows(rows_x, grad_both), contr...  51.8 us
    all_to_all x1, waiting for transfers between devices, body(): lax.all_to_all(entry_grads.reshape(groups, capacity, width), 'expert', sp...  33.1 us
    all_to_all x1, waiting for transfers between devices, body(): lax.all_to_all(expert_out.reshape(groups, capacity, width), 'expert', spl...  30.5 us
    all_to_all x1, waiting for transfers between devices, body(): lax.all_to_all(send_rows, 'expert', split_axis=0, concat_axis=0, tiled=True)  18.6 us
    dot_general x3, matrix products, contract_cols(): lax.dot_general(left, right, (((1,), (1,)), ((), ())), preferred_element_...  14.8 us
    ppermute x6, starting transfers between devices, shifted(): return lax.ppermute(block, axis, route)  13 us
  transfers between devices with their start and end apart: 12, of which 5 were waited for; matrix products, arithmetic and copies ran while one was open for 24% of the time, Pallas kernels for 19%

profile of v7, /device:TPU:1, one launch (start us, length us, event | category | flops | bytes accessed | tf_op | source)
XLA Modules:
  0.0 504.4 jit_solution(8549346635612564179)
XLA Ops:
  7.2 3.8 collective-permute-start.1
  12.0 2.0 fusion.24
  14.0 10.8 %select_multiply_fusion = s32[128,4]{0,1:T(4,128)S(1)} fusion(s32[128,4]{0,1:T(4,128)} %param.14, s32[]{:T(128)} %bitcast, s32[]{:T(128)} %bitcast.1, s32[]{:T(128)} %bitcast.2, s32[]{:T(128)} %bitcast.3, s32[]{:T(128)} %bitcast.4, s32[]{:T(128)} %bitcast.5, s32[]{:T(128)} %bitcast.6, s32[]{:T(128)} %bitcast.7, s32[]{:T(128)} %bitcast.8, s32[]{:T(128)} %bitcast.9, ...), kind=kLoop, calls=%fused_computation.66 | loop fusion | flops 17408 | bytes 4160 | tf_op jit(solution)/shard_map/mul | solution.py:101
  25.0 1.2 reduce-window.6
  26.6 2.4 scatter_custom_fusion
  29.3 4.3 gather_fusion
  33.5 3.3 select_select_fusion.1
  36.9 5.3 %all-to-all-start = ((bf16[16,48,2048]{2,1,0:T(8,128)(2,1)}), bf16[16,48,2048]{2,1,0:T(8,128)(2,1)}, u32[]{:S(2)}, u32[]{:S(2)}) async-start(bf16[16,48,2048]{2,1,0:T(8,128)(2,1)} %select_select_fusion.1), calls=%async_computation | async-start | bytes 6291456 | tf_op jit(solution)/shard_map/all_to_all | solution.py:159
  44.4 3.1 mul.160
  47.5 5.3 %mul.161 = f32[512,2048]{1,0:T(8,128)} reshape(f32[128,4,2048]{2,1,0:T(4,128)} %mul.160) | data formatting | bytes 8388608 | tf_op jit(solution)/shard_map/mul | solution.py:182
  53.3 2.5 multiply_convert_fusion
  55.8 4.3 gather_fusion.1
  60.0 3.4 select_select_fusion
  63.4 18.6 %all-to-all-done = bf16[16,48,2048]{2,1,0:T(8,128)(2,1)} async-done(((bf16[16,48,2048]{2,1,0:T(8,128)(2,1)}), bf16[16,48,2048]{2,1,0:T(8,128)(2,1)}, u32[]{:S(2)}, u32[]{:S(2)}) %all-to-all-start) | async-done | bytes 3145760 | tf_op jit(solution)/shard_map/all_to_all | solution.py:159
  82.0 7.8 %all-to-all-start.2 = ((bf16[16,48,2048]{2,1,0:T(8,128)(2,1)}), bf16[16,48,2048]{2,1,0:T(8,128)(2,1)S(1)}, u32[]{:S(2)}, u32[]{:S(2)}) async-start(bf16[16,48,2048]{2,1,0:T(8,128)(2,1)} %select_select_fusion), calls=%async_computation.2 | async-start | bytes 6291456 | tf_op jit(solution)/shard_map/all_to_all | solution.py:186
  89.8 3.3 collective-permute-start
  93.1 56.8 %collective-permute-done = bf16[1,2,256,768]{3,2,1,0:T(8,128)(2,1)S(1)} collective-permute-done((bf16[1,2,256,768]{3,2,1,0:T(8,128)(2,1)}, bf16[1,2,256,768]{3,2,1,0:T(8,128)(2,1)S(1)}, u32[]{:S(2)}, u32[]{:S(2)}) %collective-permute-start) | collective-permute-done | bytes 786464 | tf_op jit(solution)/shard_map/ppermute | solution.py:20
  151.8 97.7 %shard_map.170 = (bf16[8,256,768]{2,1,0:T(8,128)(2,1)}, bf16[8,256,768]{2,1,0:T(8,128)(2,1)}) custom-call(bf16[256,768]{1,0:T(8,128)(2,1)} %get-tuple-element.25.refs_0_, bf16[256,768]{1,0:T(8,128)(2,1)} %get-tuple-element.24.refs_1_), custom_call_target="tpu_custom_call" | custom-call | bytes 12582912 | tf_op jit(solution)/shard_map/pallas_call | solution.py:64
  249.5 7.0 %fusion.25 = f32[768,768]{0,1:T(8,128)} fusion(bf16[768,2048]{1,0:T(8,128)(2,1)} %bitcast.20, bf16[2048,768]{1,0:T(8,128)(2,1)} %bitcast.115), kind=kOutput, calls=%fused_computation.80 | convolution fusion | flops 2415919104 | bytes 8650752 | tf_op jit(solution)/shard_map/dot_general | solution.py:162
  256.6 6.0 %fusion.26 = f32[768,768]{0,1:T(8,128)} fusion(bf16[768,2048]{1,0:T(8,128)(2,1)} %bitcast.20, bf16[2048,768]{1,0:T(8,128)(2,1)S(1)} %bitcast.113), kind=kOutput, calls=%fused_computation.81 | convolution fusion | flops 2415919104 | bytes 8650752 | tf_op jit(solution)/shard_map/dot_general | solution.py:163
  262.6 6.7 %multiply_convert_fusion.1 = (bf16[768,768]{0,1:T(8,128)(2,1)S(1)}, bf16[768,768]{0,1:T(8,128)(2,1)S(1)}, bf16[768,768]{0,1:T(8,128)(2,1)S(1)}) fusion(f32[768,768]{0,1:T(8,128)} %fusion.25, f32[768,768]{0,1:T(8,128)} %fusion.26, bf16[768,2048]{1,0:T(8,128)(2,1)S(1)} %bitcast.108, bf16[1,768,2048]{2,1,0:T(8,128)(2,1)} %all-gather.2.cloned.1.call-done), kind=kOutput, calls=%fused_computation.21 | convolution fusion | flops 2424766464 | bytes 14548992 | tf_op jit(solution)/shard_map/dot_general | solution.py:120
  269.3 3.3 convolution_convert_fusion.1
  272.7 8.3 %convolution_convert_fusion = bf16[2048,1536]{0,1:T(8,128)(2,1)S(1)} fusion(bf16[768,2048]{1,0:T(8,128)(2,1)} %bitcast.20, bf16[768,768]{0,1:T(8,128)(2,1)S(1)} %get-tuple-element.21, bf16[768,768]{0,1:T(8,128)(2,1)S(1)} %get-tuple-element.22), kind=kOutput, calls=%fused_computation.6 | convolution fusion | flops 4839702528 | bytes 11796480 | tf_op jit(solution)/shard_map/dot_general | solution.py:114
  281.0 11.6 %pad_maximum_fusion = bf16[2048,2304]{0,1:T(8,128)(2,1)} fusion(bf16[2048,768]{0,1:T(8,128)(2,1)S(1)} %convolution_convert_fusion.1, bf16[2048,1536]{0,1:T(8,128)(2,1)S(1)} %convolution_convert_fusion), kind=kLoop, calls=%fused_computation.5 | loop fusion | flops 18874368 | bytes 18874368 | tf_op jit(solution)/shard_map/concatenate | solution.py:209
  292.6 1.9 copy-done.19
  294.5 4.1 fusion.27
  298.6 4.1 add_convert_fusion
  302.7 7.1 %all-to-all-start.3 = ((bf16[16,48,2048]{2,1,0:T(8,128)(2,1)}), bf16[16,48,2048]{2,1,0:T(8,128)(2,1)S(1)}, u32[]{:S(2)}, u32[]{:S(2)}) async-start(bf16[16,48,2048]{2,1,0:T(8,128)(2,1)} %bitcast.110), calls=%async_computation.3 | async-start | bytes 6291456 | tf_op jit(solution)/shard_map/all_to_all | solution.py:195
  309.7 6.5 %convolution_convert_fusion.2 = bf16[768,2048]{1,0:T(8,128)(2,1)} fusion(bf16[768,768]{0,1:T(8,128)(2,1)} %copy-done.21, bf16[1,768,2048]{2,1,0:T(8,128)(2,1)} %all-gather.2.cloned.1.call-done), kind=kOutput, calls=%fused_computation.11 | convolution fusion | flops 2417491968 | bytes 7471104 | tf_op jit(solution)/shard_map/dot_general | solution.py:166
  316.3 33.1 %all-to-all-done.3 = bf16[16,48,2048]{2,1,0:T(8,128)(2,1)S(1)} async-done(((bf16[16,48,2048]{2,1,0:T(8,128)(2,1)}), bf16[16,48,2048]{2,1,0:T(8,128)(2,1)S(1)}, u32[]{:S(2)}, u32[]{:S(2)}) %all-to-all-start.3) | async-done | bytes 3145760 | tf_op jit(solution)/shard_map/all_to_all | solution.py:195
  349.4 8.0 %all-to-all-start.1 = ((bf16[16,48,2048]{2,1,0:T(8,128)(2,1)}), bf16[16,48,2048]{2,1,0:T(8,128)(2,1)}, u32[]{:S(2)}, u32[]{:S(2)}) async-start(bf16[16,48,2048]{2,1,0:T(8,128)(2,1)} %bitcast.107), calls=%async_computation.1 | async-start | bytes 6291456 | tf_op jit(solution)/shard_map/all_to_all | solution.py:169
  357.4 2.7 convert_element_type.94
  360.1 2.9 collective-permute-start.2
  363.0 1.0 convert_element_type.97
  364.8 2.9 collective-permute-start.4
  368.7 3.3 gather_fusion.3
  372.0 30.5 %all-to-all-done.1 = bf16[16,48,2048]{2,1,0:T(8,128)(2,1)} async-done(((bf16[16,48,2048]{2,1,0:T(8,128)(2,1)}), bf16[16,48,2048]{2,1,0:T(8,128)(2,1)}, u32[]{:S(2)}, u32[]{:S(2)}) %all-to-all-start.1) | async-done | bytes 3145760 | tf_op jit(solution)/shard_map/all_to_all | solution.py:169
  402.5 7.7 %gather_fusion.2 = bf16[512,2048]{1,0:T(8,128)(2,1)} fusion(bf16[768,2048]{1,0:T(8,128)(2,1)} %bitcast.27, s32[1024]{0:T(1024)S(1)} %pad_clamp_fusion.1), kind=kCustom, calls=%fused_computation.clone | custom fusion | bytes 4196352 | tf_op jit(solution)/shard_map/jit(_take)/gather | solution.py:176
  410.2 4.8 broadcast_select_fusion
  415.0 5.1 %reshape.161 = f32[128,4,2048]{2,1,0:T(4,128)} reshape(f32[512,2048]{1,0:T(8,128)} %get-tuple-element.33) | data formatting | bytes 8388608 | tf_op jit(solution)/shard_map/convert_element_type | solution.py:179
  420.2 2.9 reshape.159
  423.1 3.9 reduce_sum.45
  427.0 6.4 %multiply_reduce_fusion = bf16[128,2048]{1,0:T(8,128)(2,1)} fusion(f32[128,4,2048]{2,1,0:T(4,128)} %reshape.161, f32[128,4]{1,0:T(8,128)S(1)} %copy.20), kind=kLoop, calls=%fused_computation.9 | loop fusion | flops 1835008 | bytes 4720640 | tf_op jit(solution)/shard_map/reduce_sum | solution.py:179
  433.4 51.8 %reduce-scatter.2.cloned.1.call-done = bf16[256,2304]{0,1:T(8,128)(2,1)} async-done(((bf16[2048,2304]{0,1:T(8,128)(2,1)}), bf16[256,2304]{0,1:T(8,128)(2,1)}) %reduce-scatter.2.cloned.1.call-update) | async-done | bytes 1179664 | tf_op jit(solution)/shard_map/reduce_scatter | solution.py:208
  485.2 1.2 slice.52
  486.4 1.6 copy.27
  489.7 4.7 subtract_convert_fusion
  494.5 2.9 subtract_convert_fusion.1
  (91 shorter events, 9.2 us)
Async XLA Ops:
  7.2 22.1 %copy-start = (bf16[128,2048]{1,0:T(8,128)(2,1)S(1)}, bf16[128,2048]{1,0:T(8,128)(2,1)}, u32[]{:S(2)}) copy-start(bf16[128,2048]{1,0:T(8,128)(2,1)} %param.13) | copy-start | bytes 1572868
  7.2 36.4 %collective-permute-start.1 = (bf16[1,768,256]{2,1,0:T(8,128)(2,1)}, bf16[1,768,256]{2,1,0:T(8,128)(2,1)S(1)}, u32[]{:S(2)}, u32[]{:S(2)}) collective-permute-start(bf16[1,768,256]{2,1,0:T(8,128)(2,1)} %param.18), channel_id=1, source_target_pairs={{64,0},{72,8},{80,16},{88,24},{96,32},{104,40},{112,48},{120,56},{... | collective-permute-start | bytes 1179656 | tf_op jit(solution)/shard_map/ppermute | solution.py:20
  36.9 5.4 %copy-start.15 = (s32[16]{0:T(128)S(1)}, s32[16]{0:T(128)}, u32[]{:S(2)}) copy-start(s32[16]{0:T(128)} %param.16) | copy-start | bytes 196
  36.9 6.7 %copy-start.14 = (bf16[1,768,256]{2,1,0:T(8,128)(2,1)S(1)}, bf16[1,768,256]{2,1,0:T(8,128)(2,1)}, u32[]{:S(2)}) copy-start(bf16[1,768,256]{2,1,0:T(8,128)(2,1)} %param.18) | copy-start | bytes 1179652
  36.9 7.5 %copy-start.13 = (bf16[128,2048]{1,0:T(8,128)(2,1)S(1)}, bf16[128,2048]{1,0:T(8,128)(2,1)}, u32[]{:S(2)}) copy-start(bf16[128,2048]{1,0:T(8,128)(2,1)} %param.23) | copy-start | bytes 1572868
  36.9 45.2 %all-to-all-start = ((bf16[16,48,2048]{2,1,0:T(8,128)(2,1)}), bf16[16,48,2048]{2,1,0:T(8,128)(2,1)}, u32[]{:S(2)}, u32[]{:S(2)}) async-start(bf16[16,48,2048]{2,1,0:T(8,128)(2,1)} %select_select_fusion.1), calls=%async_computation | async-start | bytes 6291456 | tf_op jit(solution)/shard_map/all_to_all | solution.py:159
  42.2 220.4 %all-gather.2.cloned.1.call-start = ((), (), s32[]{:S(2)}) async-start(), calls=%async_computation.5 | async-start | bytes 3538944 | tf_op jit(solution)/shard_map/all_gather | solution.py:150
  47.5 5.3 %copy-start.16 = (f32[128,4]{0,1:T(4,128)S(1)}, f32[128,4]{0,1:T(4,128)}, u32[]{:S(2)}) copy-start(f32[128,4]{0,1:T(4,128)} %param.15) | copy-start | bytes 6148
  82.0 180.6 %all-to-all-start.2 = ((bf16[16,48,2048]{2,1,0:T(8,128)(2,1)}), bf16[16,48,2048]{2,1,0:T(8,128)(2,1)S(1)}, u32[]{:S(2)}, u32[]{:S(2)}) async-start(bf16[16,48,2048]{2,1,0:T(8,128)(2,1)} %select_select_fusion), calls=%async_computation.2 | async-start | bytes 6291456 | tf_op jit(solution)/shard_map/all_to_all | solution.py:186
  89.8 395.4 %reduce-scatter.2.cloned.1.call-start = ((), (), s32[]{:S(2)}) async-start(), calls=%async_computation.6 | async-start | bytes 10616832 | tf_op jit(solution)/shard_map/reduce_scatter | solution.py:208
  89.8 60.0 %collective-permute-start = (bf16[1,2,256,768]{3,2,1,0:T(8,128)(2,1)}, bf16[1,2,256,768]{3,2,1,0:T(8,128)(2,1)S(1)}, u32[]{:S(2)}, u32[]{:S(2)}) collective-permute-start(bf16[1,2,256,768]{3,2,1,0:T(8,128)(2,1)} %param.17), channel_id=1, source_target_pairs={{64,0},{72,8},{80,16},{88,24},{96,32},{104,40},{112,48},{120,56},{... | collective-permute-start | bytes 2359304 | tf_op jit(solution)/shard_map/ppermute | solution.py:20
  150.0 0.9 copy-start.3
  249.5 7.1 %copy-start.17 = (bf16[8,256,768]{2,1,0:T(8,128)(2,1)S(1)}, bf16[8,256,768]{2,1,0:T(8,128)(2,1)}, u32[]{:S(2)}) copy-start(bf16[8,256,768]{2,1,0:T(8,128)(2,1)} %get-tuple-element.12) | copy-start | bytes 9437188
  269.3 3.4 copy-start.21
  269.3 3.4 copy-start.20
  269.3 3.4 copy-start.22
  292.6 1.9 copy-start.19
  294.4 4.1 copy-start.18
  294.5 4.1 copy-start.23
  302.7 46.7 %all-to-all-start.3 = ((bf16[16,48,2048]{2,1,0:T(8,128)(2,1)}), bf16[16,48,2048]{2,1,0:T(8,128)(2,1)S(1)}, u32[]{:S(2)}, u32[]{:S(2)}) async-start(bf16[16,48,2048]{2,1,0:T(8,128)(2,1)} %bitcast.110), calls=%async_computation.3 | async-start | bytes 6291456 | tf_op jit(solution)/shard_map/all_to_all | solution.py:195
  349.4 53.2 %all-to-all-start.1 = ((bf16[16,48,2048]{2,1,0:T(8,128)(2,1)}), bf16[16,48,2048]{2,1,0:T(8,128)(2,1)}, u32[]{:S(2)}, u32[]{:S(2)}) async-start(bf16[16,48,2048]{2,1,0:T(8,128)(2,1)} %bitcast.107), calls=%async_computation.1 | async-start | bytes 6291456 | tf_op jit(solution)/shard_map/all_to_all | solution.py:169
  357.4 5.6 %copy-start.7 = (f32[1,2,256,768]{3,2,1,0:T(8,128)S(1)}, f32[1,2,256,768]{3,2,1,0:T(8,128)}, u32[]{:S(2)}) copy-start(f32[1,2,256,768]{3,2,1,0:T(8,128)} %param.20) | copy-start | bytes 4718596
  357.4 6.6 %copy-start.9 = (f32[1,768,256]{2,1,0:T(8,128)S(1)}, f32[1,768,256]{2,1,0:T(8,128)}, u32[]{:S(2)}) copy-start(f32[1,768,256]{2,1,0:T(8,128)} %param.21) | copy-start | bytes 2359300
  357.4 10.3 %copy-start.11 = (f32[1,768,256]{2,1,0:T(8,128)S(1)}, f32[1,768,256]{2,1,0:T(8,128)}, u32[]{:S(2)}) copy-start(f32[1,768,256]{2,1,0:T(8,128)} %param.22) | copy-start | bytes 2359300
  360.1 128.2 %collective-permute-start.2 = (bf16[1,2,256,768]{3,2,1,0:T(8,128)(2,1)}, bf16[1,2,256,768]{3,2,1,0:T(8,128)(2,1)}, u32[]{:S(2)}, u32[]{:S(2)}) collective-permute-start(bf16[1,2,256,768]{3,2,1,0:T(8,128)(2,1)} %convert_element_type.94), channel_id=1, source_target_pairs={{64,0},{72,8},{80,16},{88,24},{96,32},{104,40},{112,48},{120,56},{... | collective-permute-start | bytes 2359304 | tf_op jit(solution)/shard_map/ppermute | solution.py:20
  363.9 124.4 %collective-permute-start.3 = (bf16[1,2,256,768]{3,2,1,0:T(8,128)(2,1)}, bf16[1,2,256,768]{3,2,1,0:T(8,128)(2,1)}, u32[]{:S(2)}, u32[]{:S(2)}) collective-permute-start(bf16[1,2,256,768]{3,2,1,0:T(8,128)(2,1)} %convert_element_type.97), channel_id=1, source_target_pairs={{64,0},{72,8},{80,16},{88,24},{96,32},{104,40},{112,48},{120,56},{... | collective-permute-start | bytes 2359304 | tf_op jit(solution)/shard_map/ppermute | solution.py:20
  364.8 129.6 %collective-permute-start.4 = (bf16[1,768,256]{2,1,0:T(8,128)(2,1)}, bf16[1,768,256]{2,1,0:T(8,128)(2,1)}, u32[]{:S(2)}, u32[]{:S(2)}) collective-permute-start(bf16[1,768,256]{2,1,0:T(8,128)(2,1)} %convert_element_type.101), channel_id=1, source_target_pairs={{64,0},{72,8},{80,16},{88,24},{96,32},{104,40},{112,48},{120,56},{... | collective-permute-start | bytes 1179656 | tf_op jit(solution)/shard_map/ppermute | solution.py:20
  368.5 126.0 %collective-permute-start.5 = (bf16[1,768,256]{2,1,0:T(8,128)(2,1)}, bf16[1,768,256]{2,1,0:T(8,128)(2,1)}, u32[]{:S(2)}, u32[]{:S(2)}) collective-permute-start(bf16[1,768,256]{2,1,0:T(8,128)(2,1)} %convert_element_type.103), channel_id=1, source_target_pairs={{64,0},{72,8},{80,16},{88,24},{96,32},{104,40},{112,48},{120,56},{... | collective-permute-start | bytes 1179656 | tf_op jit(solution)/shard_map/ppermute | solution.py:20
  402.5 7.7 %copy-start.2 = (bf16[512,2048]{1,0:T(8,128)(2,1)S(1)}, bf16[512,2048]{1,0:T(8,128)(2,1)}, u32[]{:S(2)}) copy-start(bf16[512,2048]{1,0:T(8,128)(2,1)} %gather_fusion.3) | copy-start | bytes 6291460
  486.4 1.6 copy-start.5
  488.0 1.1 copy-start.4
  488.0 1.7 copy-start.6
  488.2 6.2 %copy-start.8 = (bf16[1,768,256]{2,1,0:T(8,128)(2,1)S(1)}, bf16[1,768,256]{2,1,0:T(8,128)(2,1)}, u32[]{:S(2)}) copy-start(bf16[1,768,256]{2,1,0:T(8,128)(2,1)} %broadcast_select_fusion.2) | copy-start | bytes 1179652
  488.2 6.2 %copy-start.10 = (f32[1,768,256]{2,1,0:T(8,128)S(1)}, f32[1,768,256]{2,1,0:T(8,128)}, u32[]{:S(2)}) copy-start(f32[1,768,256]{2,1,0:T(8,128)} %param.21) | copy-start | bytes 2359300
  488.3 6.2 %copy-start.12 = (f32[1,768,256]{2,1,0:T(8,128)S(1)}, f32[1,768,256]{2,1,0:T(8,128)}, u32[]{:S(2)}) copy-start(f32[1,768,256]{2,1,0:T(8,128)} %param.22) | copy-start | bytes 2359300
  489.7 7.7 %copy-start.1 = (bf16[128,2048]{1,0:T(8,128)(2,1)S(1)}, bf16[128,2048]{1,0:T(8,128)(2,1)}, u32[]{:S(2)}) copy-start(bf16[128,2048]{1,0:T(8,128)(2,1)} %param.13) | copy-start | bytes 1572868
Sparse Core Ops, SparseCore 0:
  45.2 113.6 all-gather.1
  292.7 192.4 reduce-scatter.1

commit v8 on v7

--- a/solution.py
+++ b/solution.py
@@ -156,6 +156,7 @@
     position, filler = route_table(expert_ids, partner[expert_ids], groups, capacity)
     token_fill = jnp.where(filler >= 0, filler // top_count, -1)
     send_rows = fill_rows(tokens, token_fill, groups, capacity)
+    send_rows, w_in, w_down = lax.optimization_barrier((send_rows, w_in, w_down))
     arrived = lax.all_to_all(send_rows, "expert", split_axis=0, concat_axis=0, tiled=True)
     rows_x = arrived.reshape(groups * capacity, width)
     own_moments = (m_in, v_in, m_down, v_down)

time: 511 us -> 484 us (0.947)
  waiting for transfers between devices: 191 us -> 141 us
  Pallas kernels: 97.7 us -> 122 us
    ppermute x6, waiting for transfers between devices: 56.8 us -> 0.02 us  [shifted(): return lax.ppermute(block, axis, route)]
    pallas_call x1, Pallas kernels: 97.7 us -> 122 us  [exchange(): pl.pallas_call(functools.partial(exchange_kernel, count, spread, width),...]
  transfers between devices with their start and end apart: 12 -> 12, of which waited for: 5 -> 4; matrix products, arithmetic and copies ran while one was open for 24% -> 26% of each run, Pallas kernels for 19% -> 25%
where the time goes in v8:
time: 484 us; the launch traced here: 477 us
  waiting for transfers between devices  141 us (29%)
  Pallas kernels  122 us (25%)
  other arithmetic  63.6 us (13%)
  matrix products  50.6 us (10%)
  local copies, waits for them, and re-layouts  48.1 us (10%)
  starting transfers between devices  36.8 us (8%)
  between operations  15.3 us (3%)
    pallas_call x1, Pallas kernels, exchange(): pl.pallas_call(functools.partial(exchange_kernel, count, spread, width),...  122 us
    reduce_scatter x1, waiting for transfers between devices, body(): lax.psum_scatter(jnp.concatenate([contract_rows(rows_x, grad_both), contr...  55.5 us
    all_to_all x1, waiting for transfers between devices, body(): lax.all_to_all(entry_grads.reshape(groups, capacity, width), 'expert', sp...  35.6 us
    all_to_all x1, waiting for transfers between devices, body(): lax.all_to_all(expert_out.reshape(groups, capacity, width), 'expert', spl...  29.2 us
    all_to_all x1, waiting for transfers between devices, body(): lax.all_to_all(send_rows, 'expert', split_axis=0, concat_axis=0, tiled=True)  20.1 us
    dot_general x3, matrix products, contract_cols(): lax.dot_general(left, right, (((1,), (1,)), ((), ())), preferred_element_...  16.7 us
    dot_general x2, matrix products, contract_rows(): lax.dot_general(left, right, (((0,), (0,)), ((), ())), preferred_element_...  14.2 us
    concatenate x1, other arithmetic, body(): jnp.concatenate([contract_rows(rows_x, grad_both), contract_rows(dout_row...  11.6 us
  transfers between devices with their start and end apart: 12, of which 4 were waited for; matrix products, arithmetic and copies ran while one was open for 26% of the time, Pallas kernels for 25%

profile of v8, /device:TPU:1, one launch (start us, length us, event | category | flops | bytes accessed | tf_op | source)
XLA Modules:
  0.0 477.1 jit_solution(12207443594640613266)
XLA Ops:
  7.2 3.8 collective-permute-start
  12.1 2.0 fusion.24
  14.1 11.0 %select_multiply_fusion = s32[128,4]{0,1:T(4,128)S(1)} fusion(s32[128,4]{0,1:T(4,128)} %param.14, s32[]{:T(128)} %bitcast, s32[]{:T(128)} %bitcast.1, s32[]{:T(128)} %bitcast.2, s32[]{:T(128)} %bitcast.3, s32[]{:T(128)} %bitcast.4, s32[]{:T(128)} %bitcast.5, s32[]{:T(128)} %bitcast.6, s32[]{:T(128)} %bitcast.7, s32[]{:T(128)} %bitcast.8, s32[]{:T(128)} %bitcast.9, ...), kind=kLoop, calls=%fused_computation.66 | loop fusion | flops 17408 | bytes 4160 | tf_op jit(solution)/shard_map/mul | solution.py:101
  25.3 1.2 reduce-window.6
  26.8 2.4 scatter_custom_fusion
  29.5 1.3 fusion.20
  31.5 4.3 gather_fusion
  35.8 3.4 select_select_fusion.1
  40.1 7.2 %all-to-all-start = ((bf16[16,48,2048]{2,1,0:T(8,128)(2,1)}), bf16[16,48,2048]{2,1,0:T(8,128)(2,1)}, u32[]{:S(2)}, u32[]{:S(2)}) async-start(bf16[16,48,2048]{2,1,0:T(8,128)(2,1)} %select_select_fusion.1), calls=%async_computation | async-start | bytes 6291456 | tf_op jit(solution)/shard_map/all_to_all | solution.py:160
  48.0 3.0 mul.160
  51.0 5.4 %mul.161 = f32[512,2048]{1,0:T(8,128)} reshape(f32[128,4,2048]{2,1,0:T(4,128)} %mul.160) | data formatting | bytes 8388608 | tf_op jit(solution)/shard_map/mul | solution.py:183
  56.8 2.5 multiply_convert_fusion
  59.3 4.3 gather_fusion.1
  63.6 3.3 select_select_fusion
  66.9 20.1 %all-to-all-done = bf16[16,48,2048]{2,1,0:T(8,128)(2,1)} async-done(((bf16[16,48,2048]{2,1,0:T(8,128)(2,1)}), bf16[16,48,2048]{2,1,0:T(8,128)(2,1)}, u32[]{:S(2)}, u32[]{:S(2)}) %all-to-all-start) | async-done | bytes 3145760 | tf_op jit(solution)/shard_map/all_to_all | solution.py:160
  87.0 8.1 %all-to-all-start.2 = ((bf16[16,48,2048]{2,1,0:T(8,128)(2,1)}), bf16[16,48,2048]{2,1,0:T(8,128)(2,1)}, u32[]{:S(2)}, u32[]{:S(2)}) async-start(bf16[16,48,2048]{2,1,0:T(8,128)(2,1)} %select_select_fusion), calls=%async_computation.2 | async-start | bytes 6291456 | tf_op jit(solution)/shard_map/all_to_all | solution.py:187
  95.5 0.9 slice_bitcast_fusion.1
  96.4 121.6 %shard_map.170 = (bf16[8,256,768]{2,1,0:T(8,128)(2,1)}, bf16[8,256,768]{2,1,0:T(8,128)(2,1)}) custom-call(bf16[256,768]{1,0:T(8,128)(2,1)} %get-tuple-element.31.refs_0_, bf16[256,768]{1,0:T(8,128)(2,1)} %get-tuple-element.30.refs_1_), custom_call_target="tpu_custom_call" | custom-call | bytes 12582912 | tf_op jit(solution)/shard_map/pallas_call | solution.py:64
  218.0 7.0 %fusion.25 = f32[768,768]{0,1:T(8,128)} fusion(bf16[768,2048]{1,0:T(8,128)(2,1)} %bitcast.20, bf16[2048,768]{1,0:T(8,128)(2,1)} %bitcast.113), kind=kOutput, calls=%fused_computation.80 | convolution fusion | flops 2415919104 | bytes 8650752 | tf_op jit(solution)/shard_map/dot_general | solution.py:163
  225.1 6.1 %fusion.26 = f32[768,768]{0,1:T(8,128)} fusion(bf16[768,2048]{1,0:T(8,128)(2,1)} %bitcast.20, bf16[2048,768]{1,0:T(8,128)(2,1)S(1)} %bitcast.111), kind=kOutput, calls=%fused_computation.81 | convolution fusion | flops 2415919104 | bytes 8650752 | tf_op jit(solution)/shard_map/dot_general | solution.py:164
  231.1 7.6 %multiply_convert_fusion.1 = (bf16[768,768]{0,1:T(8,128)(2,1)S(1)}, bf16[768,768]{0,1:T(8,128)(2,1)S(1)}, bf16[768,768]{0,1:T(8,128)(2,1)S(1)}) fusion(f32[768,768]{0,1:T(8,128)} %fusion.25, f32[768,768]{0,1:T(8,128)} %fusion.26, bf16[768,2048]{1,0:T(8,128)(2,1)} %bitcast.29, bf16[1,768,2048]{2,1,0:T(8,128)(2,1)} %all-gather.2.cloned.1.call-done), kind=kOutput, calls=%fused_computation.21 | convolution fusion | flops 2424766464 | bytes 14548992 | tf_op jit(solution)/shard_map/dot_general | solution.py:120
  238.7 6.0 %convolution_convert_fusion.1 = bf16[2048,768]{0,1:T(8,128)(2,1)S(1)} fusion(bf16[768,768]{0,1:T(8,128)(2,1)S(1)} %get-tuple-element.29, bf16[768,2048]{1,0:T(8,128)(2,1)} %bitcast.29), kind=kOutput, calls=%fused_computation.10 | convolution fusion | flops 2417491968 | bytes 7471104 | tf_op jit(solution)/shard_map/dot_general | solution.py:114
  244.7 8.3 %convolution_convert_fusion = bf16[2048,1536]{0,1:T(8,128)(2,1)S(1)} fusion(bf16[768,2048]{1,0:T(8,128)(2,1)} %bitcast.20, bf16[768,768]{0,1:T(8,128)(2,1)S(1)} %get-tuple-element.27, bf16[768,768]{0,1:T(8,128)(2,1)S(1)} %get-tuple-element.28), kind=kOutput, calls=%fused_computation.6 | convolution fusion | flops 4839702528 | bytes 11796480 | tf_op jit(solution)/shard_map/dot_general | solution.py:114
  253.0 11.6 %pad_maximum_fusion = bf16[2048,2304]{0,1:T(8,128)(2,1)} fusion(bf16[2048,768]{0,1:T(8,128)(2,1)S(1)} %convolution_convert_fusion.1, bf16[2048,1536]{0,1:T(8,128)(2,1)S(1)} %convolution_convert_fusion), kind=kLoop, calls=%fused_computation.5 | loop fusion | flops 18874368 | bytes 18874368 | tf_op jit(solution)/shard_map/concatenate | solution.py:210
  264.7 5.0 %fusion.27 = f32[768,2048]{1,0:T(8,128)S(1)} fusion(bf16[768,768]{0,1:T(8,128)(2,1)} %copy-done.18, bf16[2048,768]{1,0:T(8,128)(2,1)} %bitcast.114), kind=kOutput, calls=%fused_computation.82 | convolution fusion | flops 2415919104 | bytes 10616832 | tf_op jit(solution)/shard_map/dot_general | solution.py:120
  269.7 4.1 add_convert_fusion
  273.8 5.6 %all-to-all-start.3 = ((bf16[16,48,2048]{2,1,0:T(8,128)(2,1)}), bf16[16,48,2048]{2,1,0:T(8,128)(2,1)S(1)}, u32[]{:S(2)}, u32[]{:S(2)}) async-start(bf16[16,48,2048]{2,1,0:T(8,128)(2,1)} %bitcast.108), calls=%async_computation.3 | async-start | bytes 6291456 | tf_op jit(solution)/shard_map/all_to_all | solution.py:196
  279.4 6.6 %convolution_convert_fusion.2 = bf16[768,2048]{1,0:T(8,128)(2,1)} fusion(bf16[768,768]{0,1:T(8,128)(2,1)} %copy-done.19, bf16[1,768,2048]{2,1,0:T(8,128)(2,1)} %all-gather.2.cloned.1.call-done), kind=kOutput, calls=%fused_computation.11 | convolution fusion | flops 2417491968 | bytes 7471104 | tf_op jit(solution)/shard_map/dot_general | solution.py:167
  286.0 35.6 %all-to-all-done.3 = bf16[16,48,2048]{2,1,0:T(8,128)(2,1)S(1)} async-done(((bf16[16,48,2048]{2,1,0:T(8,128)(2,1)}), bf16[16,48,2048]{2,1,0:T(8,128)(2,1)S(1)}, u32[]{:S(2)}, u32[]{:S(2)}) %all-to-all-start.3) | async-done | bytes 3145760 | tf_op jit(solution)/shard_map/all_to_all | solution.py:196
  321.6 5.7 %all-to-all-start.1 = ((bf16[16,48,2048]{2,1,0:T(8,128)(2,1)}), bf16[16,48,2048]{2,1,0:T(8,128)(2,1)}, u32[]{:S(2)}, u32[]{:S(2)}) async-start(bf16[16,48,2048]{2,1,0:T(8,128)(2,1)} %bitcast.107), calls=%async_computation.1 | async-start | bytes 6291456 | tf_op jit(solution)/shard_map/all_to_all | solution.py:170
  327.3 2.6 convert_element_type.94
  329.9 2.9 collective-permute-start.2
  332.8 1.0 convert_element_type.97
  334.6 2.9 collective-permute-start.4
  338.5 3.3 gather_fusion.3
  341.8 29.2 %all-to-all-done.1 = bf16[16,48,2048]{2,1,0:T(8,128)(2,1)} async-done(((bf16[16,48,2048]{2,1,0:T(8,128)(2,1)}), bf16[16,48,2048]{2,1,0:T(8,128)(2,1)}, u32[]{:S(2)}, u32[]{:S(2)}) %all-to-all-start.1) | async-done | bytes 3145760 | tf_op jit(solution)/shard_map/all_to_all | solution.py:170
  371.0 7.7 %gather_fusion.2 = bf16[512,2048]{1,0:T(8,128)(2,1)} fusion(bf16[768,2048]{1,0:T(8,128)(2,1)} %bitcast.27, s32[1024]{0:T(1024)S(1)} %pad_clamp_fusion.1), kind=kCustom, calls=%fused_computation.clone | custom fusion | bytes 4196352 | tf_op jit(solution)/shard_map/jit(_take)/gather | solution.py:177
  378.7 4.9 %broadcast_select_fusion = (bf16[512,2048]{1,0:T(8,128)(2,1)}, f32[512,2048]{1,0:T(8,128)}) fusion(bf16[512,2048]{1,0:T(8,128)(2,1)S(1)} %copy-done.2, pred[512]{0:T(512)(128)(4,1)S(1)} %get-tuple-element.25, bf16[512,2048]{1,0:T(8,128)(2,1)} %gather_fusion.2), kind=kLoop, calls=%fused_computation.27 | loop fusion | flops 3145728 | bytes 10486272 | tf_op jit(solution)/shard_map/jit(_take)/select_n | solution.py:203
  383.6 5.3 %reshape.161 = f32[128,4,2048]{2,1,0:T(4,128)} reshape(f32[512,2048]{1,0:T(8,128)} %get-tuple-element.39) | data formatting | bytes 8388608 | tf_op jit(solution)/shard_map/convert_element_type | solution.py:180
  388.9 2.9 reshape.159
  391.8 3.9 reduce_sum.45
  395.7 6.2 %multiply_reduce_fusion = bf16[128,2048]{1,0:T(8,128)(2,1)} fusion(f32[128,4,2048]{2,1,0:T(4,128)} %reshape.161, f32[128,4]{1,0:T(8,128)S(1)} %copy.20), kind=kLoop, calls=%fused_computation.9 | loop fusion | flops 1835008 | bytes 4720640 | tf_op jit(solution)/shard_map/reduce_sum | solution.py:180
  401.9 55.5 %reduce-scatter.2.cloned.1.call-done = bf16[256,2304]{0,1:T(8,128)(2,1)} async-done(((bf16[2048,2304]{0,1:T(8,128)(2,1)}), bf16[256,2304]{0,1:T(8,128)(2,1)}) %reduce-scatter.2.cloned.1.call-update) | async-done | bytes 1179664 | tf_op jit(solution)/shard_map/reduce_scatter | solution.py:209
  457.4 1.2 slice.52
  458.7 1.6 copy.27
  460.5 0.9 copy-done.4
  461.9 5.2 %subtract_convert_fusion = (bf16[1,2,256,768]{3,2,1,0:T(8,128)(2,1)}, f32[1,2,256,768]{3,2,1,0:T(8,128)}, f32[1,2,256,768]{3,2,1,0:T(8,128)}) fusion(bf16[1,2,256,768]{3,2,1,0:T(8,128)(2,1)S(1)} %copy-done.4, f32[256,2,768]{2,0,1:T(8,128)} %copy.27, f32[1,2,256,768]{3,2,1,0:T(8,128)S(1)} %copy-done.6, bf16[1,2,256,768]{3,2,1,0:T(8,128)(2,1)} %collective-permute-done.2, ...), kind=kLoop, calls=%fused_computation.32 | loop fusion | flops 7077888 | bytes 11010049 | tf_op jit(solution)/shard_map/convert_element_type | solution.py:92
  467.2 2.9 subtract_convert_fusion.1
  (87 shorter events, 6.9 us)
Async XLA Ops:
  7.2 24.3 %copy-start = (bf16[128,2048]{1,0:T(8,128)(2,1)S(1)}, bf16[128,2048]{1,0:T(8,128)(2,1)}, u32[]{:S(2)}) copy-start(bf16[128,2048]{1,0:T(8,128)(2,1)} %param.13) | copy-start | bytes 1572868
  7.2 32.8 %collective-permute-start = (bf16[1,2,256,768]{3,2,1,0:T(8,128)(2,1)}, bf16[1,2,256,768]{3,2,1,0:T(8,128)(2,1)S(1)}, u32[]{:S(2)}, u32[]{:S(2)}) collective-permute-start(bf16[1,2,256,768]{3,2,1,0:T(8,128)(2,1)} %param.17), channel_id=1, source_target_pairs={{64,0},{72,8},{80,16},{88,24},{96,32},{104,40},{112,48},{120,56},{... | collective-permute-start | bytes 2359304 | tf_op jit(solution)/shard_map/ppermute | solution.py:20
  11.0 28.2 %collective-permute-start.1 = (bf16[1,768,256]{2,1,0:T(8,128)(2,1)}, bf16[1,768,256]{2,1,0:T(8,128)(2,1)S(1)}, u32[]{:S(2)}, u32[]{:S(2)}) collective-permute-start(bf16[1,768,256]{2,1,0:T(8,128)(2,1)} %param.18), channel_id=1, source_target_pairs={{64,0},{72,8},{80,16},{88,24},{96,32},{104,40},{112,48},{120,56},{... | collective-permute-start | bytes 1179656 | tf_op jit(solution)/shard_map/ppermute | solution.py:20
  35.8 3.4 copy-start.15
  35.8 4.2 copy-start.13
  40.1 55.4 %copy-start.3 = (bf16[1,2,256,768]{3,2,1,0:T(8,128)(2,1)}, bf16[1,2,256,768]{3,2,1,0:T(8,128)(2,1)S(1)}, u32[]{:S(2)}) copy-start(bf16[1,2,256,768]{3,2,1,0:T(8,128)(2,1)S(1)} %broadcast_select_fusion.1) | copy-start | bytes 2359300
  40.1 7.9 %copy-start.14 = (bf16[128,2048]{1,0:T(8,128)(2,1)S(1)}, bf16[128,2048]{1,0:T(8,128)(2,1)}, u32[]{:S(2)}) copy-start(bf16[128,2048]{1,0:T(8,128)(2,1)} %param.23) | copy-start | bytes 1572868
  40.1 47.0 %all-to-all-start = ((bf16[16,48,2048]{2,1,0:T(8,128)(2,1)}), bf16[16,48,2048]{2,1,0:T(8,128)(2,1)}, u32[]{:S(2)}, u32[]{:S(2)}) async-start(bf16[16,48,2048]{2,1,0:T(8,128)(2,1)} %select_select_fusion.1), calls=%async_computation | async-start | bytes 6291456 | tf_op jit(solution)/shard_map/all_to_all | solution.py:160
  47.3 183.9 %all-gather.2.cloned.1.call-start = ((), (), s32[]{:S(2)}) async-start(), calls=%async_computation.5 | async-start | bytes 3538944 | tf_op jit(solution)/shard_map/all_gather | solution.py:150
  51.0 5.4 %copy-start.16 = (f32[128,4]{0,1:T(4,128)S(1)}, f32[128,4]{0,1:T(4,128)}, u32[]{:S(2)}) copy-start(f32[128,4]{0,1:T(4,128)} %param.15) | copy-start | bytes 6148
  87.0 144.1 %all-to-all-start.2 = ((bf16[16,48,2048]{2,1,0:T(8,128)(2,1)}), bf16[16,48,2048]{2,1,0:T(8,128)(2,1)}, u32[]{:S(2)}, u32[]{:S(2)}) async-start(bf16[16,48,2048]{2,1,0:T(8,128)(2,1)} %select_select_fusion), calls=%async_computation.2 | async-start | bytes 6291456 | tf_op jit(solution)/shard_map/all_to_all | solution.py:187
  95.2 362.3 %reduce-scatter.2.cloned.1.call-start = ((), (), s32[]{:S(2)}) async-start(), calls=%async_computation.6 | async-start | bytes 10616832 | tf_op jit(solution)/shard_map/reduce_scatter | solution.py:209
  218.0 7.1 %copy-start.17 = (bf16[8,256,768]{2,1,0:T(8,128)(2,1)S(1)}, bf16[8,256,768]{2,1,0:T(8,128)(2,1)}, u32[]{:S(2)}) copy-start(bf16[8,256,768]{2,1,0:T(8,128)(2,1)} %get-tuple-element.16) | copy-start | bytes 9437188
  238.7 6.0 %copy-start.19 = (bf16[768,768]{0,1:T(8,128)(2,1)}, bf16[768,768]{0,1:T(8,128)(2,1)S(1)}, u32[]{:S(2)}) copy-start(bf16[768,768]{0,1:T(8,128)(2,1)S(1)} %get-tuple-element.29) | copy-start | bytes 3538948
  238.7 6.0 %copy-start.18 = (bf16[768,768]{0,1:T(8,128)(2,1)}, bf16[768,768]{0,1:T(8,128)(2,1)S(1)}, u32[]{:S(2)}) copy-start(bf16[768,768]{0,1:T(8,128)(2,1)S(1)} %get-tuple-element.28) | copy-start | bytes 3538948
  238.7 6.0 %copy-start.20 = (bf16[768,768]{0,1:T(8,128)(2,1)}, bf16[768,768]{0,1:T(8,128)(2,1)S(1)}, u32[]{:S(2)}) copy-start(bf16[768,768]{0,1:T(8,128)(2,1)S(1)} %get-tuple-element.27) | copy-start | bytes 3538948
  264.7 5.0 %copy-start.21 = (bf16[768,768]{0,1:T(8,128)(2,1)S(1)}, bf16[768,768]{0,1:T(8,128)(2,1)}, u32[]{:S(2)}) copy-start(bf16[768,768]{0,1:T(8,128)(2,1)} %copy-done.20) | copy-start | bytes 3538948
  273.8 47.8 %all-to-all-start.3 = ((bf16[16,48,2048]{2,1,0:T(8,128)(2,1)}), bf16[16,48,2048]{2,1,0:T(8,128)(2,1)S(1)}, u32[]{:S(2)}, u32[]{:S(2)}) async-start(bf16[16,48,2048]{2,1,0:T(8,128)(2,1)} %bitcast.108), calls=%async_computation.3 | async-start | bytes 6291456 | tf_op jit(solution)/shard_map/all_to_all | solution.py:196
  321.6 49.5 %all-to-all-start.1 = ((bf16[16,48,2048]{2,1,0:T(8,128)(2,1)}), bf16[16,48,2048]{2,1,0:T(8,128)(2,1)}, u32[]{:S(2)}, u32[]{:S(2)}) async-start(bf16[16,48,2048]{2,1,0:T(8,128)(2,1)} %bitcast.107), calls=%async_computation.1 | async-start | bytes 6291456 | tf_op jit(solution)/shard_map/all_to_all | solution.py:170
  327.3 5.5 %copy-start.7 = (f32[1,2,256,768]{3,2,1,0:T(8,128)S(1)}, f32[1,2,256,768]{3,2,1,0:T(8,128)}, u32[]{:S(2)}) copy-start(f32[1,2,256,768]{3,2,1,0:T(8,128)} %param.20) | copy-start | bytes 4718596
  327.3 6.5 %copy-start.9 = (f32[1,768,256]{2,1,0:T(8,128)S(1)}, f32[1,768,256]{2,1,0:T(8,128)}, u32[]{:S(2)}) copy-start(f32[1,768,256]{2,1,0:T(8,128)} %param.21) | copy-start | bytes 2359300
  327.3 10.2 %copy-start.11 = (f32[1,768,256]{2,1,0:T(8,128)S(1)}, f32[1,768,256]{2,1,0:T(8,128)}, u32[]{:S(2)}) copy-start(f32[1,768,256]{2,1,0:T(8,128)} %param.22) | copy-start | bytes 2359300
  329.9 130.6 %collective-permute-start.2 = (bf16[1,2,256,768]{3,2,1,0:T(8,128)(2,1)}, bf16[1,2,256,768]{3,2,1,0:T(8,128)(2,1)}, u32[]{:S(2)}, u32[]{:S(2)}) collective-permute-start(bf16[1,2,256,768]{3,2,1,0:T(8,128)(2,1)} %convert_element_type.94), channel_id=1, source_target_pairs={{64,0},{72,8},{80,16},{88,24},{96,32},{104,40},{112,48},{120,56},{... | collective-permute-start | bytes 2359304 | tf_op jit(solution)/shard_map/ppermute | solution.py:20
  333.7 126.8 %collective-permute-start.3 = (bf16[1,2,256,768]{3,2,1,0:T(8,128)(2,1)}, bf16[1,2,256,768]{3,2,1,0:T(8,128)(2,1)}, u32[]{:S(2)}, u32[]{:S(2)}) collective-permute-start(bf16[1,2,256,768]{3,2,1,0:T(8,128)(2,1)} %convert_element_type.97), channel_id=1, source_target_pairs={{64,0},{72,8},{80,16},{88,24},{96,32},{104,40},{112,48},{120,56},{... | collective-permute-start | bytes 2359304 | tf_op jit(solution)/shard_map/ppermute | solution.py:20
  334.6 132.6 %collective-permute-start.4 = (bf16[1,768,256]{2,1,0:T(8,128)(2,1)}, bf16[1,768,256]{2,1,0:T(8,128)(2,1)}, u32[]{:S(2)}, u32[]{:S(2)}) collective-permute-start(bf16[1,768,256]{2,1,0:T(8,128)(2,1)} %convert_element_type.101), channel_id=1, source_target_pairs={{64,0},{72,8},{80,16},{88,24},{96,32},{104,40},{112,48},{120,56},{... | collective-permute-start | bytes 1179656 | tf_op jit(solution)/shard_map/ppermute | solution.py:20
  338.3 128.9 %collective-permute-start.5 = (bf16[1,768,256]{2,1,0:T(8,128)(2,1)}, bf16[1,768,256]{2,1,0:T(8,128)(2,1)}, u32[]{:S(2)}, u32[]{:S(2)}) collective-permute-start(bf16[1,768,256]{2,1,0:T(8,128)(2,1)} %convert_element_type.103), channel_id=1, source_target_pairs={{64,0},{72,8},{80,16},{88,24},{96,32},{104,40},{112,48},{120,56},{... | collective-permute-start | bytes 1179656 | tf_op jit(solution)/shard_map/ppermute | solution.py:20
  371.0 7.7 %copy-start.2 = (bf16[512,2048]{1,0:T(8,128)(2,1)S(1)}, bf16[512,2048]{1,0:T(8,128)(2,1)}, u32[]{:S(2)}) copy-start(bf16[512,2048]{1,0:T(8,128)(2,1)} %gather_fusion.3) | copy-start | bytes 6291460
  458.7 1.6 copy-start.5
  460.3 1.1 copy-start.4
  460.3 1.7 copy-start.6
  460.5 6.7 %copy-start.8 = (bf16[1,768,256]{2,1,0:T(8,128)(2,1)S(1)}, bf16[1,768,256]{2,1,0:T(8,128)(2,1)}, u32[]{:S(2)}) copy-start(bf16[1,768,256]{2,1,0:T(8,128)(2,1)} %broadcast_select_fusion.2) | copy-start | bytes 1179652
  460.5 6.7 %copy-start.10 = (f32[1,768,256]{2,1,0:T(8,128)S(1)}, f32[1,768,256]{2,1,0:T(8,128)}, u32[]{:S(2)}) copy-start(f32[1,768,256]{2,1,0:T(8,128)} %param.21) | copy-start | bytes 2359300
  460.5 6.7 %copy-start.12 = (f32[1,768,256]{2,1,0:T(8,128)S(1)}, f32[1,768,256]{2,1,0:T(8,128)}, u32[]{:S(2)}) copy-start(f32[1,768,256]{2,1,0:T(8,128)} %param.22) | copy-start | bytes 2359300
  461.9 8.1 %copy-start.1 = (bf16[128,2048]{1,0:T(8,128)(2,1)S(1)}, bf16[128,2048]{1,0:T(8,128)(2,1)}, u32[]{:S(2)}) copy-start(bf16[128,2048]{1,0:T(8,128)(2,1)} %param.13) | copy-start | bytes 1572868
Sparse Core Ops, SparseCore 0:
  50.3 178.1 all-gather.1
  264.8 192.5 reduce-scatter.1

commit v9 on v1

--- a/solution.py
+++ b/solution.py
@@ -146,14 +146,18 @@
     token_grad = jnp.sum(per_back.astype(jnp.float32), axis=1).astype(jnp.bfloat16)
     grad_both = jnp.concatenate([grad_gate, grad_up], axis=1)
     share_rows = width // lax.axis_size("shard")
-    shares = lax.psum_scatter(
-        jnp.concatenate(
-            [contract_rows(rows_x, grad_both), contract_rows(dout_rows, hidden)], axis=1
-        ).astype(jnp.bfloat16),
+    partial = jnp.concatenate(
+        [contract_rows(rows_x, grad_both), contract_rows(dout_rows, hidden)], axis=1
+    ).astype(jnp.bfloat16)
+    shard_count = lax.axis_size("shard")
+    parts = lax.all_to_all(
+        partial.reshape(shard_count, share_rows, partial.shape[1]),
         "shard",
-        scatter_dimension=0,
+        split_axis=0,
+        concat_axis=0,
         tiled=True,
-    ).astype(jnp.float32)
+    )
+    shares = jnp.sum(parts.astype(jnp.float32), axis=0)
     grad_in = jnp.transpose(
         shares[:, : 2 * hidden_width].reshape(share_rows, 2, hidden_width), (1, 0, 2)
     )[None]

time: 467 us -> 514 us (1.10)
  the two profiles are of different devices: /device:TPU:1 before, /device:TPU:102 now
where the time goes in v9:
time: 514 us; the launch traced here: 507 us
  waiting for transfers between devices  278 us (54%)
  other arithmetic  64 us (12%)
  local copies, waits for them, and re-layouts  63.7 us (12%)
  starting transfers between devices  45.6 us (9%)
  matrix products  40.5 us (8%)
  between operations  15.3 us (3%)
    all_to_all x1, waiting for transfers between devices, body(): lax.all_to_all(partial.reshape(shard_count, share_rows, partial.shape[1])...  88.4 us
    all_gather x1, waiting for transfers between devices, body(): lax.all_gather(w_in, 'shard', axis=2, tiled=True)  39.1 us
    all_to_all x1, waiting for transfers between devices, body(): lax.all_to_all(entry_grads.reshape(groups, capacity, width), 'expert', sp...  36.2 us
    all_to_all x1, waiting for transfers between devices, body(): lax.all_to_all(send_rows, 'expert', split_axis=0, concat_axis=0, tiled=True)  36.2 us
    all_to_all x1, waiting for transfers between devices, body(): lax.all_to_all(send_grads, 'expert', split_axis=0, concat_axis=0, tiled=T...  35.5 us
    ppermute x6, waiting for transfers between devices, shifted(): return lax.ppermute(block, axis, route)  24.2 us
    all_to_all x1, waiting for transfers between devices, body(): lax.all_to_all(expert_out.reshape(groups, capacity, width), 'expert', spl...  18.6 us
    unnamed x50, local copies, waits for them, and re-layouts  13.9 us
  transfers between devices with their start and end apart: 13, of which 8 were waited for; matrix products, arithmetic and copies ran while one was open for 28% of the time, Pallas kernels for 0%

profile of v9, /device:TPU:102, one launch (start us, length us, event | category | flops | bytes accessed | tf_op | source)
XLA Modules:
  0.0 507.4 jit_solution(13924750142280850384)
XLA Ops:
  8.5 3.3 collective-permute-start.1
  13.7 7.2 %collective-permute-done.1 = bf16[1,768,256]{1,2,0:T(8,128)(2,1)S(1)} collective-permute-done((bf16[1,768,256]{1,2,0:T(8,128)(2,1)S(1)}, bf16[1,768,256]{1,2,0:T(8,128)(2,1)S(1)}, u32[]{:S(2)}, u32[]{:S(2)}) %collective-permute-start.1) | collective-permute-done | bytes 393248 | tf_op jit(solution)/shard_map/ppermute | solution.py:17
  21.8 3.3 collective-permute-start
  25.1 16.9 %collective-permute-done = bf16[1,2,256,768]{3,2,1,0:T(8,128)(2,1)S(1)} collective-permute-done((bf16[1,2,256,768]{3,2,1,0:T(8,128)(2,1)}, bf16[1,2,256,768]{3,2,1,0:T(8,128)(2,1)S(1)}, u32[]{:S(2)}, u32[]{:S(2)}) %collective-permute-start) | collective-permute-done | bytes 786464 | tf_op jit(solution)/shard_map/ppermute | solution.py:17
  44.5 3.1 mul.160
  47.6 5.3 %mul.161 = f32[512,2048]{1,0:T(8,128)} reshape(f32[128,4,2048]{2,1,0:T(4,128)} %mul.160) | data formatting | bytes 8388608 | tf_op jit(solution)/shard_map/mul | solution.py:123
  53.9 9.9 %select_multiply_fusion = s32[128,4]{0,1:T(4,128)S(1)} fusion(s32[128,4]{0,1:T(4,128)S(1)} %copy-done.13, s32[]{:T(128)} %bitcast, s32[]{:T(128)} %bitcast.1, s32[]{:T(128)} %bitcast.2, s32[]{:T(128)} %bitcast.3, s32[]{:T(128)} %bitcast.4, s32[]{:T(128)} %bitcast.5, s32[]{:T(128)} %bitcast.6, s32[]{:T(128)} %bitcast.7, s32[]{:T(128)} %bitcast.8, s32[]{:T(128)} %bitcast.9, ...), kind=kLoop, calls=%fused_computation.73 | loop fusion | flops 17408 | bytes 4160 | tf_op jit(solution)/shard_map/mul | solution.py:40
  65.5 2.4 scatter_custom_fusion
  68.2 2.5 multiply_convert_fusion
  70.7 4.3 gather_fusion.1
  75.0 3.5 select_select_fusion
  78.5 5.9 %all-to-all-start.2 = ((bf16[16,48,2048]{2,1,0:T(8,128)(2,1)}), bf16[16,48,2048]{2,1,0:T(8,128)(2,1)}, u32[]{:S(2)}, u32[]{:S(2)}) async-start(bf16[16,48,2048]{2,1,0:T(8,128)(2,1)} %select_select_fusion), calls=%async_computation.2 | async-start | bytes 6291456 | tf_op jit(solution)/shard_map/all_to_all | solution.py:127
  84.6 4.3 gather_fusion
  88.9 3.3 select_select_fusion.1
  92.2 35.5 %all-to-all-done.2 = bf16[16,48,2048]{2,1,0:T(8,128)(2,1)} async-done(((bf16[16,48,2048]{2,1,0:T(8,128)(2,1)}), bf16[16,48,2048]{2,1,0:T(8,128)(2,1)}, u32[]{:S(2)}, u32[]{:S(2)}) %all-to-all-start.2) | async-done | bytes 3145760 | tf_op jit(solution)/shard_map/all_to_all | solution.py:127
  127.7 5.4 %all-to-all-start = ((bf16[16,48,2048]{2,1,0:T(8,128)(2,1)}), bf16[16,48,2048]{2,1,0:T(8,128)(2,1)S(1)}, u32[]{:S(2)}, u32[]{:S(2)}) async-start(bf16[16,48,2048]{2,1,0:T(8,128)(2,1)} %select_select_fusion.1), calls=%async_computation | async-start | bytes 6291456 | tf_op jit(solution)/shard_map/all_to_all | solution.py:100
  133.2 6.9 %fusion = f32[768,768]{0,1:T(8,128)} fusion(bf16[768,2048]{1,0:T(8,128)(2,1)} %bitcast.27, bf16[1,768,2048]{1,2,0:T(8,128)(2,1)} %all-gather.5.cloned.1.call-done), kind=kOutput, calls=%fused_computation.14 | convolution fusion | flops 2415919104 | bytes 8650752 | tf_op jit(solution)/shard_map/dot_general | solution.py:59
  140.1 36.2 %all-to-all-done = bf16[16,48,2048]{2,1,0:T(8,128)(2,1)S(1)} async-done(((bf16[16,48,2048]{2,1,0:T(8,128)(2,1)}), bf16[16,48,2048]{2,1,0:T(8,128)(2,1)S(1)}, u32[]{:S(2)}, u32[]{:S(2)}) %all-to-all-start) | async-done | bytes 3145760 | tf_op jit(solution)/shard_map/all_to_all | solution.py:100
  176.2 39.1 %all-gather.3.cloned.1.call-done = bf16[1,2,2048,768]{3,2,1,0:T(8,128)(2,1)} async-done(((bf16[1,2,256,768]{3,2,1,0:T(8,128)(2,1)}), bf16[1,2,2048,768]{3,2,1,0:T(8,128)(2,1)}) %all-gather.3.cloned.1.call-update) | async-done | bytes 6291472 | tf_op jit(solution)/shard_map/all_gather | solution.py:90
  215.4 4.7 fusion.5
  220.1 4.6 multiply_convert_fusion.2
  224.7 2.7 fusion.4
  227.3 4.1 add_convert_fusion
  231.4 6.0 %all-to-all-start.3 = ((bf16[16,48,2048]{2,1,0:T(8,128)(2,1)}), bf16[16,48,2048]{2,1,0:T(8,128)(2,1)S(1)}, u32[]{:S(2)}, u32[]{:S(2)}) async-start(bf16[16,48,2048]{2,1,0:T(8,128)(2,1)} %bitcast.139), calls=%async_computation.3 | async-start | bytes 6291456 | tf_op jit(solution)/shard_map/all_to_all | solution.py:136
  237.4 6.6 %convolution_convert_fusion.1 = bf16[768,2048]{1,0:T(8,128)(2,1)} fusion(bf16[768,768]{0,1:T(8,128)(2,1)} %get-tuple-element.27, bf16[1,768,2048]{1,2,0:T(8,128)(2,1)} %all-gather.5.cloned.1.call-done), kind=kOutput, calls=%fused_computation.11 | convolution fusion | flops 2417491968 | bytes 7471104 | tf_op jit(solution)/shard_map/dot_general | solution.py:107
  244.0 36.2 %all-to-all-done.3 = bf16[16,48,2048]{2,1,0:T(8,128)(2,1)S(1)} async-done(((bf16[16,48,2048]{2,1,0:T(8,128)(2,1)}), bf16[16,48,2048]{2,1,0:T(8,128)(2,1)S(1)}, u32[]{:S(2)}, u32[]{:S(2)}) %all-to-all-start.3) | async-done | bytes 3145760 | tf_op jit(solution)/shard_map/all_to_all | solution.py:136
  280.2 4.8 all-to-all-start.1
  284.9 4.7 copy.48
  289.6 4.7 copy.46
  294.3 5.0 convolution_convert_fusion.2
  299.3 6.1 %convolution_convert_fusion = bf16[8,256,1536]{2,1,0:T(8,128)(2,1)S(1)} fusion(bf16[8,256,768]{2,1,0:T(8,128)(2,1)S(1)} %bitcast.140, bf16[768,768]{0,1:T(8,128)(2,1)S(1)} %copy-done.17, bf16[768,768]{0,1:T(8,128)(2,1)S(1)} %copy-done.20), kind=kOutput, calls=%fused_computation.8 | convolution fusion | flops 4839702528 | bytes 11796480 | tf_op jit(solution)/shard_map/dot_general | solution.py:53
  305.4 4.0 pad_maximum_fusion
  309.3 18.6 %all-to-all-done.1 = bf16[16,48,2048]{2,1,0:T(8,128)(2,1)} async-done(((bf16[16,48,2048]{2,1,0:T(8,128)(2,1)}), bf16[16,48,2048]{2,1,0:T(8,128)(2,1)}, u32[]{:S(2)}, u32[]{:S(2)}) %all-to-all-start.1) | async-done | bytes 3145760 | tf_op jit(solution)/shard_map/all_to_all | solution.py:110
  327.9 9.9 %all-to-all-start.4 = ((bf16[8,256,2304]{2,1,0:T(8,128)(2,1)}), bf16[8,256,2304]{2,1,0:T(8,128)(2,1)}, u32[]{:S(2)}, u32[]{:S(2)}) async-start(bf16[8,256,2304]{2,1,0:T(8,128)(2,1)} %pad_maximum_fusion), calls=%async_computation.4 | async-start | bytes 18874368 | tf_op jit(solution)/shard_map/all_to_all | solution.py:153
  337.8 2.5 convert_element_type.95
  344.7 2.3 copy.51
  356.8 3.3 gather_fusion.3
  360.1 7.7 %gather_fusion.2 = bf16[512,2048]{1,0:T(8,128)(2,1)} fusion(bf16[768,2048]{1,0:T(8,128)(2,1)} %bitcast.25, s32[1024]{0:T(1024)S(1)} %pad_clamp_fusion.1), kind=kCustom, calls=%fused_computation.clone | custom fusion | bytes 4196352 | tf_op jit(solution)/shard_map/jit(_take)/gather | solution.py:117
  367.8 4.7 broadcast_select_fusion
  372.5 5.2 %reshape.158 = f32[128,4,2048]{2,1,0:T(4,128)} reshape(f32[512,2048]{1,0:T(8,128)} %get-tuple-element.35) | data formatting | bytes 8388608 | tf_op jit(solution)/shard_map/convert_element_type | solution.py:120
  377.7 2.9 reshape.156
  380.7 3.9 reduce_sum.54
  384.5 6.2 %multiply_reduce_fusion = bf16[128,2048]{1,0:T(8,128)(2,1)} fusion(f32[128,4,2048]{2,1,0:T(4,128)} %reshape.158, f32[128,4]{1,0:T(8,128)S(1)} %copy.37), kind=kLoop, calls=%fused_computation.10 | loop fusion | flops 1835008 | bytes 4720640 | tf_op jit(solution)/shard_map/reduce_sum | solution.py:120
  390.7 88.4 %all-to-all-done.4 = bf16[8,256,2304]{2,1,0:T(8,128)(2,1)} async-done(((bf16[8,256,2304]{2,1,0:T(8,128)(2,1)}), bf16[8,256,2304]{2,1,0:T(8,128)(2,1)}, u32[]{:S(2)}, u32[]{:S(2)}) %all-to-all-start.4) | async-done | bytes 9437216 | tf_op jit(solution)/shard_map/all_to_all | solution.py:153
  479.1 5.2 %convert_reduce_fusion = f32[256,2304]{1,0:T(8,128)S(1)} fusion(bf16[8,256,2304]{2,1,0:T(8,128)(2,1)} %all-to-all-done.4), kind=kLoop, calls=%fused_computation.5 | loop fusion | flops 8847360 | bytes 11796480 | tf_op jit(solution)/shard_map/reduce_sum | solution.py:160
  486.7 2.9 subtract_convert_fusion.1
  492.8 2.3 copy.57
  495.1 5.2 %subtract_convert_fusion = (bf16[1,2,256,768]{3,2,1,0:T(8,128)(2,1)}, f32[1,2,256,768]{3,2,1,0:T(8,128)}, f32[1,2,256,768]{3,2,1,0:T(8,128)}) fusion(bf16[1,2,256,768]{3,2,1,0:T(8,128)(2,1)S(1)} %copy-done.7, f32[32,2,8,768]{3,2,1,0:T(8,128)S(1)} %bitcast.137, f32[1,2,256,768]{3,2,1,0:T(8,128)} %param.19, ...), kind=kLoop, calls=%fused_computation.40 | loop fusion | flops 7077888 | bytes 11010049 | tf_op jit(solution)/shard_map/convert_element_type | solution.py:31
  (93 shorter events, 28.7 us)
Async XLA Ops:
  7.2 77.4 %copy-start = (bf16[128,2048]{1,0:T(8,128)(2,1)S(1)}, bf16[128,2048]{1,0:T(8,128)(2,1)}, u32[]{:S(2)}) copy-start(bf16[128,2048]{1,0:T(8,128)(2,1)} %param.13) | copy-start | bytes 1572868
  7.2 37.0 %copy-start.13 = (s32[128,4]{0,1:T(4,128)S(1)}, s32[128,4]{0,1:T(4,128)}, u32[]{:S(2)}) copy-start(s32[128,4]{0,1:T(4,128)} %param.14) | copy-start | bytes 6148
  7.2 37.3 %copy-start.11 = (bf16[128,2048]{1,0:T(8,128)(2,1)S(1)}, bf16[128,2048]{1,0:T(8,128)(2,1)}, u32[]{:S(2)}) copy-start(bf16[128,2048]{1,0:T(8,128)(2,1)} %param.23) | copy-start | bytes 1572868
  7.2 125.9 %all-gather.5.cloned.1.call-start = ((), (), s32[]{:S(2)}) async-start(), calls=%async_computation.6 | async-start | bytes 3538944 | tf_op jit(solution)/shard_map/all_gather | solution.py:91
  8.5 12.4 %collective-permute-start.1 = (bf16[1,768,256]{1,2,0:T(8,128)(2,1)S(1)}, bf16[1,768,256]{1,2,0:T(8,128)(2,1)S(1)}, u32[]{:S(2)}, u32[]{:S(2)}) collective-permute-start(bf16[1,768,256]{1,2,0:T(8,128)(2,1)S(1)} %copy.43), channel_id=1, source_target_pairs={{64,0},{72,8},{80,16},{88,24},{96,32},{104,40},{112,48},{120,56},{... | collective-permute-start | bytes 1179656 | tf_op jit(solution)/shard_map/ppermute | solution.py:17
  21.8 193.6 %all-gather.3.cloned.1.call-start = ((), (), s32[]{:S(2)}) async-start(), calls=%async_computation.5 | async-start | bytes 7077888 | tf_op jit(solution)/shard_map/all_gather | solution.py:90
  21.8 20.2 %collective-permute-start = (bf16[1,2,256,768]{3,2,1,0:T(8,128)(2,1)}, bf16[1,2,256,768]{3,2,1,0:T(8,128)(2,1)S(1)}, u32[]{:S(2)}, u32[]{:S(2)}) collective-permute-start(bf16[1,2,256,768]{3,2,1,0:T(8,128)(2,1)} %param.17), channel_id=1, source_target_pairs={{64,0},{72,8},{80,16},{88,24},{96,32},{104,40},{112,48},{120,56},{... | collective-permute-start | bytes 2359304 | tf_op jit(solution)/shard_map/ppermute | solution.py:17
  47.6 5.4 %copy-start.14 = (f32[128,4]{0,1:T(4,128)S(1)}, f32[128,4]{0,1:T(4,128)}, u32[]{:S(2)}) copy-start(f32[128,4]{0,1:T(4,128)} %param.15) | copy-start | bytes 6148
  47.6 5.6 %copy-start.12 = (s32[16]{0:T(128)S(1)}, s32[16]{0:T(128)}, u32[]{:S(2)}) copy-start(s32[16]{0:T(128)} %param.16) | copy-start | bytes 196
  78.5 49.2 %all-to-all-start.2 = ((bf16[16,48,2048]{2,1,0:T(8,128)(2,1)}), bf16[16,48,2048]{2,1,0:T(8,128)(2,1)}, u32[]{:S(2)}, u32[]{:S(2)}) async-start(bf16[16,48,2048]{2,1,0:T(8,128)(2,1)} %select_select_fusion), calls=%async_computation.2 | async-start | bytes 6291456 | tf_op jit(solution)/shard_map/all_to_all | solution.py:127
  127.7 48.5 %all-to-all-start = ((bf16[16,48,2048]{2,1,0:T(8,128)(2,1)}), bf16[16,48,2048]{2,1,0:T(8,128)(2,1)S(1)}, u32[]{:S(2)}, u32[]{:S(2)}) async-start(bf16[16,48,2048]{2,1,0:T(8,128)(2,1)} %select_select_fusion.1), calls=%async_computation | async-start | bytes 6291456 | tf_op jit(solution)/shard_map/all_to_all | solution.py:100
  176.2 43.8 %copy-start.2 = (bf16[16,48,2048]{2,1,0:T(8,128)(2,1)}, bf16[16,48,2048]{2,1,0:T(8,128)(2,1)S(1)}, u32[]{:S(2)}) copy-start(bf16[16,48,2048]{2,1,0:T(8,128)(2,1)S(1)} %all-to-all-done) | copy-start | bytes 9437188
  215.4 4.7 copy-start.15
  215.4 4.7 copy-start.18
  224.7 2.7 copy-start.16
  224.7 2.7 copy-start.19
  231.4 48.8 %all-to-all-start.3 = ((bf16[16,48,2048]{2,1,0:T(8,128)(2,1)}), bf16[16,48,2048]{2,1,0:T(8,128)(2,1)S(1)}, u32[]{:S(2)}, u32[]{:S(2)}) async-start(bf16[16,48,2048]{2,1,0:T(8,128)(2,1)} %bitcast.139), calls=%async_computation.3 | async-start | bytes 6291456 | tf_op jit(solution)/shard_map/all_to_all | solution.py:136
  280.2 47.7 %all-to-all-start.1 = ((bf16[16,48,2048]{2,1,0:T(8,128)(2,1)}), bf16[16,48,2048]{2,1,0:T(8,128)(2,1)}, u32[]{:S(2)}, u32[]{:S(2)}) async-start(bf16[16,48,2048]{2,1,0:T(8,128)(2,1)} %bitcast.138), calls=%async_computation.1 | async-start | bytes 6291456 | tf_op jit(solution)/shard_map/all_to_all | solution.py:110
  294.3 5.0 copy-start.10
  294.3 5.0 copy-start.17
  294.3 5.0 copy-start.20
  327.9 151.2 %all-to-all-start.4 = ((bf16[8,256,2304]{2,1,0:T(8,128)(2,1)}), bf16[8,256,2304]{2,1,0:T(8,128)(2,1)}, u32[]{:S(2)}, u32[]{:S(2)}) async-start(bf16[8,256,2304]{2,1,0:T(8,128)(2,1)} %pad_maximum_fusion), calls=%async_computation.4 | async-start | bytes 18874368 | tf_op jit(solution)/shard_map/all_to_all | solution.py:153
  337.8 4.6 copy-start.8
  340.2 154.9 %collective-permute-start.2 = (bf16[1,2,256,768]{3,2,1,0:T(8,128)(2,1)}, bf16[1,2,256,768]{3,2,1,0:T(8,128)(2,1)}, u32[]{:S(2)}, u32[]{:S(2)}) collective-permute-start(bf16[1,2,256,768]{3,2,1,0:T(8,128)(2,1)} %convert_element_type.95), channel_id=1, source_target_pairs={{64,0},{72,8},{80,16},{88,24},{96,32},{104,40},{112,48},{120,56},{... | collective-permute-start | bytes 2359304 | tf_op jit(solution)/shard_map/ppermute | solution.py:17
  343.3 151.8 %collective-permute-start.3 = (bf16[1,2,256,768]{3,2,1,0:T(8,128)(2,1)}, bf16[1,2,256,768]{3,2,1,0:T(8,128)(2,1)}, u32[]{:S(2)}, u32[]{:S(2)}) collective-permute-start(bf16[1,2,256,768]{3,2,1,0:T(8,128)(2,1)} %convert_element_type.98), channel_id=1, source_target_pairs={{64,0},{72,8},{80,16},{88,24},{96,32},{104,40},{112,48},{120,56},{... | collective-permute-start | bytes 2359304 | tf_op jit(solution)/shard_map/ppermute | solution.py:17
  348.9 135.4 %collective-permute-start.4 = (bf16[1,768,256]{1,2,0:T(8,128)(2,1)}, bf16[1,768,256]{1,2,0:T(8,128)(2,1)}, u32[]{:S(2)}, u32[]{:S(2)}) collective-permute-start(bf16[1,768,256]{1,2,0:T(8,128)(2,1)} %convert_element_type.102), channel_id=1, source_target_pairs={{64,0},{72,8},{80,16},{88,24},{96,32},{104,40},{112,48},{120,56},{... | collective-permute-start | bytes 1179656 | tf_op jit(solution)/shard_map/ppermute | solution.py:17
  355.2 129.2 %collective-permute-start.5 = (bf16[1,768,256]{1,2,0:T(8,128)(2,1)}, bf16[1,768,256]{1,2,0:T(8,128)(2,1)}, u32[]{:S(2)}, u32[]{:S(2)}) collective-permute-start(bf16[1,768,256]{1,2,0:T(8,128)(2,1)} %convert_element_type.104), channel_id=1, source_target_pairs={{64,0},{72,8},{80,16},{88,24},{96,32},{104,40},{112,48},{120,56},{... | collective-permute-start | bytes 1179656 | tf_op jit(solution)/shard_map/ppermute | solution.py:17
  360.1 7.7 %copy-start.4 = (bf16[512,2048]{1,0:T(8,128)(2,1)S(1)}, bf16[512,2048]{1,0:T(8,128)(2,1)}, u32[]{:S(2)}) copy-start(bf16[512,2048]{1,0:T(8,128)(2,1)} %gather_fusion.3) | copy-start | bytes 6291460
  484.3 5.3 %copy-start.3 = (f32[256,2304]{1,0:T(8,128)}, f32[256,2304]{1,0:T(8,128)S(1)}, u32[]{:S(2)}) copy-start(f32[256,2304]{1,0:T(8,128)S(1)} %convert_reduce_fusion) | copy-start | bytes 7077892
  484.3 1.7 copy-start.5
  484.4 2.2 copy-start.6
  484.4 2.3 copy-start.9
  489.6 5.5 %slice-start = ((f32[256,2304]{1,0:T(8,128)}), f32[256,1536]{1,0:T(8,128)S(1)}, s32[]{:S(2)}) async-start(f32[256,2304]{1,0:T(8,128)} %copy-done.3), calls=%async_computation.7 | async-start | bytes 3145728 | tf_op jit(solution)/shard_map/slice | solution.py:162
  489.6 5.5 %copy-start.7 = (bf16[1,2,256,768]{3,2,1,0:T(8,128)(2,1)S(1)}, bf16[1,2,256,768]{3,2,1,0:T(8,128)(2,1)}, u32[]{:S(2)}) copy-start(bf16[1,2,256,768]{3,2,1,0:T(8,128)(2,1)} %broadcast_select_fusion.1) | copy-start | bytes 2359300
  495.1 5.2 %copy-start.1 = (bf16[128,2048]{1,0:T(8,128)(2,1)S(1)}, bf16[128,2048]{1,0:T(8,128)(2,1)}, u32[]{:S(2)}) copy-start(bf16[128,2048]{1,0:T(8,128)(2,1)} %param.13) | copy-start | bytes 1572868
Sparse Core Ops, SparseCore 0:
  21.9 61.8 all-gather.4
  86.6 128.7 all-gather.2

commit v10 on v8

--- a/solution.py
+++ b/solution.py
@@ -148,7 +148,8 @@
         for moved, owned in zip(moved_states, (m_in, v_in, m_down, v_down))
     )
     down_full = lax.all_gather(w_down, "shard", axis=2, tiled=True)
-    gate_parts, up_parts = exchange((w_in[0, 0], w_in[0, 1]), True, 0)
+    gate_shard, up_shard, down_full = lax.optimization_barrier((w_in[0, 0], w_in[0, 1], down_full))
+    gate_parts, up_parts = exchange((gate_shard, up_shard), True, 0)
     gate_weight = gate_parts.reshape(-1, gate_parts.shape[-1])
     up_weight = up_parts.reshape(-1, up_parts.shape[-1])
     down_weight = down_full[0]

time: 484 us -> 521 us (1.076)
  waiting for transfers between devices: 141 us -> 207 us
  Pallas kernels: 122 us -> 91.6 us
    all_gather x1, waiting for transfers between devices: 0.01 us -> 61.7 us  [body(): down_full = lax.all_gather(w_down, 'shard', axis=2, tiled=True)]
    pallas_call x1, Pallas kernels: 122 us -> 91.6 us  [exchange(): pl.pallas_call(functools.partial(exchange_kernel, count, spread, width),...]
    ppermute x6, waiting for transfers between devices: 0.02 us -> 5.35 us  [shifted(): return lax.ppermute(block, axis, route)]
  transfers between devices with their start and end apart: 12 -> 12, of which waited for: 4 -> 6; matrix products, arithmetic and copies ran while one was open for 26% -> 24% of each run, Pallas kernels for 25% -> 18%
where the time goes in v10:
time: 521 us; the launch traced here: 514 us
  waiting for transfers between devices  207 us (40%)
  Pallas kernels  91.6 us (18%)
  other arithmetic  64.8 us (12%)
  local copies, waits for them, and re-layouts  49.9 us (10%)
  matrix products  48.9 us (9%)
  starting transfers between devices  37.3 us (7%)
  between operations  15.3 us (3%)
    pallas_call x1, Pallas kernels, exchange(): pl.pallas_call(functools.partial(exchange_kernel, count, spread, width),...  91.6 us
    all_gather x1, waiting for transfers between devices, body(): down_full = lax.all_gather(w_down, 'shard', axis=2, tiled=True)  61.7 us
    reduce_scatter x1, waiting for transfers between devices, body(): lax.psum_scatter(jnp.concatenate([contract_rows(rows_x, grad_both), contr...  55.4 us
    all_to_all x1, waiting for transfers between devices, body(): lax.all_to_all(entry_grads.reshape(groups, capacity, width), 'expert', sp...  34.3 us
    all_to_all x1, waiting for transfers between devices, body(): lax.all_to_all(expert_out.reshape(groups, capacity, width), 'expert', spl...  29.2 us
    all_to_all x1, waiting for transfers between devices, body(): lax.all_to_all(send_rows, 'expert', split_axis=0, concat_axis=0, tiled=True)  20.8 us
    dot_general x3, matrix products, contract_cols(): lax.dot_general(left, right, (((1,), (1,)), ((), ())), preferred_element_...  14.8 us
    dot_general x2, matrix products, contract_rows(): lax.dot_general(left, right, (((0,), (0,)), ((), ())), preferred_element_...  14.3 us
  transfers between devices with their start and end apart: 12, of which 6 were waited for; matrix products, arithmetic and copies ran while one was open for 24% of the time, Pallas kernels for 18%

profile of v10, /device:TPU:1, one launch (start us, length us, event | category | flops | bytes accessed | tf_op | source)
XLA Modules:
  0.0 514.5 jit_solution(12050726168866318995)
XLA Ops:
  7.2 3.8 collective-permute-start
  12.2 2.0 fusion.24
  14.1 10.8 %select_multiply_fusion = s32[128,4]{0,1:T(4,128)S(1)} fusion(s32[128,4]{0,1:T(4,128)} %param.14, s32[]{:T(128)} %bitcast, s32[]{:T(128)} %bitcast.1, s32[]{:T(128)} %bitcast.2, s32[]{:T(128)} %bitcast.3, s32[]{:T(128)} %bitcast.4, s32[]{:T(128)} %bitcast.5, s32[]{:T(128)} %bitcast.6, s32[]{:T(128)} %bitcast.7, s32[]{:T(128)} %bitcast.8, s32[]{:T(128)} %bitcast.9, ...), kind=kLoop, calls=%fused_computation.66 | loop fusion | flops 17408 | bytes 4160 | tf_op jit(solution)/shard_map/mul | solution.py:101
  26.7 2.4 scatter_custom_fusion
  29.4 1.3 fusion.20
  31.3 5.3 %collective-permute-done.1 = bf16[1,768,256]{2,1,0:T(8,128)(2,1)S(1)} collective-permute-done((bf16[1,768,256]{2,1,0:T(8,128)(2,1)}, bf16[1,768,256]{2,1,0:T(8,128)(2,1)S(1)}, u32[]{:S(2)}, u32[]{:S(2)}) %collective-permute-start.1) | collective-permute-done | bytes 393248 | tf_op jit(solution)/shard_map/ppermute | solution.py:20
  36.7 1.8 broadcast_select_fusion.2
  38.6 4.3 gather_fusion
  42.9 3.4 select_select_fusion.1
  46.4 6.5 %all-to-all-start = ((bf16[16,48,2048]{2,1,0:T(8,128)(2,1)}), bf16[16,48,2048]{2,1,0:T(8,128)(2,1)}, u32[]{:S(2)}, u32[]{:S(2)}) async-start(bf16[16,48,2048]{2,1,0:T(8,128)(2,1)} %select_select_fusion.1), calls=%async_computation | async-start | bytes 6291456 | tf_op jit(solution)/shard_map/all_to_all | solution.py:161
  53.0 3.0 mul.160
  56.0 5.4 %mul.161 = f32[512,2048]{1,0:T(8,128)} reshape(f32[128,4,2048]{2,1,0:T(4,128)} %mul.160) | data formatting | bytes 8388608 | tf_op jit(solution)/shard_map/mul | solution.py:184
  61.8 2.5 multiply_convert_fusion
  64.3 4.3 gather_fusion.1
  68.6 3.4 select_select_fusion
  71.9 20.8 %all-to-all-done = bf16[16,48,2048]{2,1,0:T(8,128)(2,1)} async-done(((bf16[16,48,2048]{2,1,0:T(8,128)(2,1)}), bf16[16,48,2048]{2,1,0:T(8,128)(2,1)}, u32[]{:S(2)}, u32[]{:S(2)}) %all-to-all-start) | async-done | bytes 3145760 | tf_op jit(solution)/shard_map/all_to_all | solution.py:161
  92.8 8.2 %all-to-all-start.2 = ((bf16[16,48,2048]{2,1,0:T(8,128)(2,1)}), bf16[16,48,2048]{2,1,0:T(8,128)(2,1)}, u32[]{:S(2)}, u32[]{:S(2)}) async-start(bf16[16,48,2048]{2,1,0:T(8,128)(2,1)} %select_select_fusion), calls=%async_computation.2 | async-start | bytes 6291456 | tf_op jit(solution)/shard_map/all_to_all | solution.py:188
  102.2 61.7 %all-gather.2.cloned.1.call-done = bf16[1,768,2048]{2,1,0:T(8,128)(2,1)} async-done(((bf16[1,768,256]{2,1,0:T(8,128)(2,1)}), bf16[1,768,2048]{2,1,0:T(8,128)(2,1)}) %all-gather.2.cloned.1.call-update) | async-done | bytes 3145744 | tf_op jit(solution)/shard_map/all_gather | solution.py:150
  163.9 91.6 %shard_map.170 = (bf16[8,256,768]{2,1,0:T(8,128)(2,1)}, bf16[8,256,768]{2,1,0:T(8,128)(2,1)}) custom-call(bf16[256,768]{1,0:T(8,128)(2,1)} %get-tuple-element.18.refs_0_, bf16[256,768]{1,0:T(8,128)(2,1)} %get-tuple-element.19.refs_1_), custom_call_target="tpu_custom_call" | custom-call | bytes 12582912 | tf_op jit(solution)/shard_map/pallas_call | solution.py:64
  255.5 7.1 %fusion.25 = f32[768,768]{0,1:T(8,128)} fusion(bf16[768,2048]{1,0:T(8,128)(2,1)} %bitcast.20, bf16[2048,768]{1,0:T(8,128)(2,1)} %bitcast.113), kind=kOutput, calls=%fused_computation.80 | convolution fusion | flops 2415919104 | bytes 8650752 | tf_op jit(solution)/shard_map/dot_general | solution.py:164
  262.6 6.2 %fusion.26 = f32[768,768]{0,1:T(8,128)} fusion(bf16[768,2048]{1,0:T(8,128)(2,1)} %bitcast.20, bf16[2048,768]{1,0:T(8,128)(2,1)S(1)} %bitcast.111), kind=kOutput, calls=%fused_computation.81 | convolution fusion | flops 2415919104 | bytes 8650752 | tf_op jit(solution)/shard_map/dot_general | solution.py:165
  268.8 6.6 %multiply_convert_fusion.1 = (bf16[768,768]{0,1:T(8,128)(2,1)S(1)}, bf16[768,768]{0,1:T(8,128)(2,1)S(1)}, bf16[768,768]{0,1:T(8,128)(2,1)S(1)}) fusion(f32[768,768]{0,1:T(8,128)} %fusion.25, f32[768,768]{0,1:T(8,128)} %fusion.26, bf16[768,2048]{1,0:T(8,128)(2,1)} %bitcast.29, bf16[1,768,2048]{2,1,0:T(8,128)(2,1)S(1)} %copy-done.16), kind=kOutput, calls=%fused_computation.21 | convolution fusion | flops 2424766464 | bytes 14548992 | tf_op jit(solution)/shard_map/dot_general | solution.py:120
  275.4 6.0 %convolution_convert_fusion.1 = bf16[2048,768]{0,1:T(8,128)(2,1)S(1)} fusion(bf16[768,768]{0,1:T(8,128)(2,1)S(1)} %get-tuple-element.35, bf16[768,2048]{1,0:T(8,128)(2,1)} %bitcast.29), kind=kOutput, calls=%fused_computation.10 | convolution fusion | flops 2417491968 | bytes 7471104 | tf_op jit(solution)/shard_map/dot_general | solution.py:114
  281.5 8.3 %convolution_convert_fusion = bf16[2048,1536]{0,1:T(8,128)(2,1)S(1)} fusion(bf16[768,2048]{1,0:T(8,128)(2,1)} %bitcast.20, bf16[768,768]{0,1:T(8,128)(2,1)S(1)} %get-tuple-element.33, bf16[768,768]{0,1:T(8,128)(2,1)S(1)} %get-tuple-element.34), kind=kOutput, calls=%fused_computation.6 | convolution fusion | flops 4839702528 | bytes 11796480 | tf_op jit(solution)/shard_map/dot_general | solution.py:114
  289.8 11.6 %pad_maximum_fusion = bf16[2048,2304]{0,1:T(8,128)(2,1)} fusion(bf16[2048,768]{0,1:T(8,128)(2,1)S(1)} %convolution_convert_fusion.1, bf16[2048,1536]{0,1:T(8,128)(2,1)S(1)} %convolution_convert_fusion), kind=kLoop, calls=%fused_computation.5 | loop fusion | flops 18874368 | bytes 18874368 | tf_op jit(solution)/shard_map/concatenate | solution.py:211
  301.4 1.9 copy-done.19
  303.3 4.1 fusion.27
  307.4 4.1 add_convert_fusion
  311.4 6.0 %all-to-all-start.3 = ((bf16[16,48,2048]{2,1,0:T(8,128)(2,1)}), bf16[16,48,2048]{2,1,0:T(8,128)(2,1)S(1)}, u32[]{:S(2)}, u32[]{:S(2)}) async-start(bf16[16,48,2048]{2,1,0:T(8,128)(2,1)} %bitcast.108), calls=%async_computation.3 | async-start | bytes 6291456 | tf_op jit(solution)/shard_map/all_to_all | solution.py:197
  317.4 6.6 %convolution_convert_fusion.2 = bf16[768,2048]{1,0:T(8,128)(2,1)} fusion(bf16[768,768]{0,1:T(8,128)(2,1)} %copy-done.21, bf16[1,768,2048]{2,1,0:T(8,128)(2,1)} %all-gather.2.cloned.1.call-done), kind=kOutput, calls=%fused_computation.11 | convolution fusion | flops 2417491968 | bytes 7471104 | tf_op jit(solution)/shard_map/dot_general | solution.py:168
  324.0 34.3 %all-to-all-done.3 = bf16[16,48,2048]{2,1,0:T(8,128)(2,1)S(1)} async-done(((bf16[16,48,2048]{2,1,0:T(8,128)(2,1)}), bf16[16,48,2048]{2,1,0:T(8,128)(2,1)S(1)}, u32[]{:S(2)}, u32[]{:S(2)}) %all-to-all-start.3) | async-done | bytes 3145760 | tf_op jit(solution)/shard_map/all_to_all | solution.py:197
  358.3 6.4 %all-to-all-start.1 = ((bf16[16,48,2048]{2,1,0:T(8,128)(2,1)}), bf16[16,48,2048]{2,1,0:T(8,128)(2,1)}, u32[]{:S(2)}, u32[]{:S(2)}) async-start(bf16[16,48,2048]{2,1,0:T(8,128)(2,1)} %bitcast.107), calls=%async_computation.1 | async-start | bytes 6291456 | tf_op jit(solution)/shard_map/all_to_all | solution.py:171
  364.7 2.6 convert_element_type.94
  367.2 2.9 collective-permute-start.2
  372.0 2.9 collective-permute-start.4
  375.9 3.3 gather_fusion.3
  379.2 29.2 %all-to-all-done.1 = bf16[16,48,2048]{2,1,0:T(8,128)(2,1)} async-done(((bf16[16,48,2048]{2,1,0:T(8,128)(2,1)}), bf16[16,48,2048]{2,1,0:T(8,128)(2,1)}, u32[]{:S(2)}, u32[]{:S(2)}) %all-to-all-start.1) | async-done | bytes 3145760 | tf_op jit(solution)/shard_map/all_to_all | solution.py:171
  408.4 7.7 %gather_fusion.2 = bf16[512,2048]{1,0:T(8,128)(2,1)} fusion(bf16[768,2048]{1,0:T(8,128)(2,1)} %bitcast.27, s32[1024]{0:T(1024)S(1)} %pad_clamp_fusion.1), kind=kCustom, calls=%fused_computation.clone | custom fusion | bytes 4196352 | tf_op jit(solution)/shard_map/jit(_take)/gather | solution.py:178
  416.1 4.9 broadcast_select_fusion
  421.0 5.2 %reshape.161 = f32[128,4,2048]{2,1,0:T(4,128)} reshape(f32[512,2048]{1,0:T(8,128)} %get-tuple-element.45) | data formatting | bytes 8388608 | tf_op jit(solution)/shard_map/convert_element_type | solution.py:181
  426.2 2.9 reshape.159
  429.2 3.9 reduce_sum.45
  433.0 6.3 %multiply_reduce_fusion = bf16[128,2048]{1,0:T(8,128)(2,1)} fusion(f32[128,4,2048]{2,1,0:T(4,128)} %reshape.161, f32[128,4]{1,0:T(8,128)S(1)} %copy.20), kind=kLoop, calls=%fused_computation.9 | loop fusion | flops 1835008 | bytes 4720640 | tf_op jit(solution)/shard_map/reduce_sum | solution.py:181
  439.4 55.4 %reduce-scatter.2.cloned.1.call-done = bf16[256,2304]{0,1:T(8,128)(2,1)} async-done(((bf16[2048,2304]{0,1:T(8,128)(2,1)}), bf16[256,2304]{0,1:T(8,128)(2,1)}) %reduce-scatter.2.cloned.1.call-update) | async-done | bytes 1179664 | tf_op jit(solution)/shard_map/reduce_scatter | solution.py:210
  494.7 1.2 slice.52
  496.0 1.6 copy.27
  499.3 5.2 %subtract_convert_fusion = (bf16[1,2,256,768]{3,2,1,0:T(8,128)(2,1)}, f32[1,2,256,768]{3,2,1,0:T(8,128)}, f32[1,2,256,768]{3,2,1,0:T(8,128)}) fusion(bf16[1,2,256,768]{3,2,1,0:T(8,128)(2,1)S(1)} %copy-done.4, f32[256,2,768]{2,0,1:T(8,128)} %copy.27, f32[1,2,256,768]{3,2,1,0:T(8,128)S(1)} %copy-done.6, bf16[1,2,256,768]{3,2,1,0:T(8,128)(2,1)} %collective-permute-done.2, ...), kind=kLoop, calls=%fused_computation.32 | loop fusion | flops 7077888 | bytes 11010049 | tf_op jit(solution)/shard_map/convert_element_type | solution.py:92
  504.5 2.9 subtract_convert_fusion.1
  (91 shorter events, 9.5 us)
Async XLA Ops:
  7.2 31.4 %copy-start = (bf16[128,2048]{1,0:T(8,128)(2,1)S(1)}, bf16[128,2048]{1,0:T(8,128)(2,1)}, u32[]{:S(2)}) copy-start(bf16[128,2048]{1,0:T(8,128)(2,1)} %param.13) | copy-start | bytes 1572868
  7.2 156.7 %all-gather.2.cloned.1.call-start = ((), (), s32[]{:S(2)}) async-start(), calls=%async_computation.5 | async-start | bytes 3538944 | tf_op jit(solution)/shard_map/all_gather | solution.py:150
  7.2 39.1 %collective-permute-start = (bf16[1,2,256,768]{3,2,1,0:T(8,128)(2,1)}, bf16[1,2,256,768]{3,2,1,0:T(8,128)(2,1)S(1)}, u32[]{:S(2)}, u32[]{:S(2)}) collective-permute-start(bf16[1,2,256,768]{3,2,1,0:T(8,128)(2,1)} %param.17), channel_id=1, source_target_pairs={{64,0},{72,8},{80,16},{88,24},{96,32},{104,40},{112,48},{120,56},{... | collective-permute-start | bytes 2359304 | tf_op jit(solution)/shard_map/ppermute | solution.py:20
  11.1 25.6 %collective-permute-start.1 = (bf16[1,768,256]{2,1,0:T(8,128)(2,1)}, bf16[1,768,256]{2,1,0:T(8,128)(2,1)S(1)}, u32[]{:S(2)}, u32[]{:S(2)}) collective-permute-start(bf16[1,768,256]{2,1,0:T(8,128)(2,1)} %param.18), channel_id=1, source_target_pairs={{64,0},{72,8},{80,16},{88,24},{96,32},{104,40},{112,48},{120,56},{... | collective-permute-start | bytes 1179656 | tf_op jit(solution)/shard_map/ppermute | solution.py:20
  42.9 3.4 copy-start.13
  46.4 54.9 %copy-start.3 = (bf16[1,2,256,768]{3,2,1,0:T(8,128)(2,1)}, bf16[1,2,256,768]{3,2,1,0:T(8,128)(2,1)S(1)}, u32[]{:S(2)}) copy-start(bf16[1,2,256,768]{3,2,1,0:T(8,128)(2,1)S(1)} %broadcast_select_fusion.1) | copy-start | bytes 2359300
  46.4 6.6 %copy-start.14 = (bf16[128,2048]{1,0:T(8,128)(2,1)S(1)}, bf16[128,2048]{1,0:T(8,128)(2,1)}, u32[]{:S(2)}) copy-start(bf16[128,2048]{1,0:T(8,128)(2,1)} %param.23) | copy-start | bytes 1572868
  46.4 46.3 %all-to-all-start = ((bf16[16,48,2048]{2,1,0:T(8,128)(2,1)}), bf16[16,48,2048]{2,1,0:T(8,128)(2,1)}, u32[]{:S(2)}, u32[]{:S(2)}) async-start(bf16[16,48,2048]{2,1,0:T(8,128)(2,1)} %select_select_fusion.1), calls=%async_computation | async-start | bytes 6291456 | tf_op jit(solution)/shard_map/all_to_all | solution.py:161
  56.0 5.4 %copy-start.15 = (f32[128,4]{0,1:T(4,128)S(1)}, f32[128,4]{0,1:T(4,128)}, u32[]{:S(2)}) copy-start(f32[128,4]{0,1:T(4,128)} %param.15) | copy-start | bytes 6148
  92.8 176.0 %all-to-all-start.2 = ((bf16[16,48,2048]{2,1,0:T(8,128)(2,1)}), bf16[16,48,2048]{2,1,0:T(8,128)(2,1)}, u32[]{:S(2)}, u32[]{:S(2)}) async-start(bf16[16,48,2048]{2,1,0:T(8,128)(2,1)} %select_select_fusion), calls=%async_computation.2 | async-start | bytes 6291456 | tf_op jit(solution)/shard_map/all_to_all | solution.py:188
  100.9 393.8 %reduce-scatter.2.cloned.1.call-start = ((), (), s32[]{:S(2)}) async-start(), calls=%async_computation.6 | async-start | bytes 10616832 | tf_op jit(solution)/shard_map/reduce_scatter | solution.py:210
  255.5 7.1 %copy-start.17 = (bf16[8,256,768]{2,1,0:T(8,128)(2,1)S(1)}, bf16[8,256,768]{2,1,0:T(8,128)(2,1)}, u32[]{:S(2)}) copy-start(bf16[8,256,768]{2,1,0:T(8,128)(2,1)} %get-tuple-element.21) | copy-start | bytes 9437188
  262.6 6.2 %copy-start.16 = (bf16[1,768,2048]{2,1,0:T(8,128)(2,1)S(1)}, bf16[1,768,2048]{2,1,0:T(8,128)(2,1)}, u32[]{:S(2)}) copy-start(bf16[1,768,2048]{2,1,0:T(8,128)(2,1)} %all-gather.2.cloned.1.call-done) | copy-start | bytes 9437188
  275.4 6.0 %copy-start.21 = (bf16[768,768]{0,1:T(8,128)(2,1)}, bf16[768,768]{0,1:T(8,128)(2,1)S(1)}, u32[]{:S(2)}) copy-start(bf16[768,768]{0,1:T(8,128)(2,1)S(1)} %get-tuple-element.35) | copy-start | bytes 3538948
  275.4 6.0 %copy-start.20 = (bf16[768,768]{0,1:T(8,128)(2,1)}, bf16[768,768]{0,1:T(8,128)(2,1)S(1)}, u32[]{:S(2)}) copy-start(bf16[768,768]{0,1:T(8,128)(2,1)S(1)} %get-tuple-element.34) | copy-start | bytes 3538948
  275.4 6.0 %copy-start.22 = (bf16[768,768]{0,1:T(8,128)(2,1)}, bf16[768,768]{0,1:T(8,128)(2,1)S(1)}, u32[]{:S(2)}) copy-start(bf16[768,768]{0,1:T(8,128)(2,1)S(1)} %get-tuple-element.33) | copy-start | bytes 3538948
  301.4 1.9 copy-start.19
  303.3 4.1 copy-start.18
  303.3 4.1 copy-start.23
  311.4 46.9 %all-to-all-start.3 = ((bf16[16,48,2048]{2,1,0:T(8,128)(2,1)}), bf16[16,48,2048]{2,1,0:T(8,128)(2,1)S(1)}, u32[]{:S(2)}, u32[]{:S(2)}) async-start(bf16[16,48,2048]{2,1,0:T(8,128)(2,1)} %bitcast.108), calls=%async_computation.3 | async-start | bytes 6291456 | tf_op jit(solution)/shard_map/all_to_all | solution.py:197
  358.3 50.1 %all-to-all-start.1 = ((bf16[16,48,2048]{2,1,0:T(8,128)(2,1)}), bf16[16,48,2048]{2,1,0:T(8,128)(2,1)}, u32[]{:S(2)}, u32[]{:S(2)}) async-start(bf16[16,48,2048]{2,1,0:T(8,128)(2,1)} %bitcast.107), calls=%async_computation.1 | async-start | bytes 6291456 | tf_op jit(solution)/shard_map/all_to_all | solution.py:171
  364.6 5.5 %copy-start.7 = (f32[1,2,256,768]{3,2,1,0:T(8,128)S(1)}, f32[1,2,256,768]{3,2,1,0:T(8,128)}, u32[]{:S(2)}) copy-start(f32[1,2,256,768]{3,2,1,0:T(8,128)} %param.20) | copy-start | bytes 4718596
  364.7 6.5 %copy-start.9 = (f32[1,768,256]{2,1,0:T(8,128)S(1)}, f32[1,768,256]{2,1,0:T(8,128)}, u32[]{:S(2)}) copy-start(f32[1,768,256]{2,1,0:T(8,128)} %param.21) | copy-start | bytes 2359300
  364.7 10.2 %copy-start.11 = (f32[1,768,256]{2,1,0:T(8,128)S(1)}, f32[1,768,256]{2,1,0:T(8,128)}, u32[]{:S(2)}) copy-start(f32[1,768,256]{2,1,0:T(8,128)} %param.22) | copy-start | bytes 2359300
  367.2 130.6 %collective-permute-start.2 = (bf16[1,2,256,768]{3,2,1,0:T(8,128)(2,1)}, bf16[1,2,256,768]{3,2,1,0:T(8,128)(2,1)}, u32[]{:S(2)}, u32[]{:S(2)}) collective-permute-start(bf16[1,2,256,768]{3,2,1,0:T(8,128)(2,1)} %convert_element_type.94), channel_id=1, source_target_pairs={{64,0},{72,8},{80,16},{88,24},{96,32},{104,40},{112,48},{120,56},{... | collective-permute-start | bytes 2359304 | tf_op jit(solution)/shard_map/ppermute | solution.py:20
  371.1 126.8 %collective-permute-start.3 = (bf16[1,2,256,768]{3,2,1,0:T(8,128)(2,1)}, bf16[1,2,256,768]{3,2,1,0:T(8,128)(2,1)}, u32[]{:S(2)}, u32[]{:S(2)}) collective-permute-start(bf16[1,2,256,768]{3,2,1,0:T(8,128)(2,1)} %convert_element_type.97), channel_id=1, source_target_pairs={{64,0},{72,8},{80,16},{88,24},{96,32},{104,40},{112,48},{120,56},{... | collective-permute-start | bytes 2359304 | tf_op jit(solution)/shard_map/ppermute | solution.py:20
  372.0 132.5 %collective-permute-start.4 = (bf16[1,768,256]{2,1,0:T(8,128)(2,1)}, bf16[1,768,256]{2,1,0:T(8,128)(2,1)}, u32[]{:S(2)}, u32[]{:S(2)}) collective-permute-start(bf16[1,768,256]{2,1,0:T(8,128)(2,1)} %convert_element_type.101), channel_id=1, source_target_pairs={{64,0},{72,8},{80,16},{88,24},{96,32},{104,40},{112,48},{120,56},{... | collective-permute-start | bytes 1179656 | tf_op jit(solution)/shard_map/ppermute | solution.py:20
  375.7 128.8 %collective-permute-start.5 = (bf16[1,768,256]{2,1,0:T(8,128)(2,1)}, bf16[1,768,256]{2,1,0:T(8,128)(2,1)}, u32[]{:S(2)}, u32[]{:S(2)}) collective-permute-start(bf16[1,768,256]{2,1,0:T(8,128)(2,1)} %convert_element_type.103), channel_id=1, source_target_pairs={{64,0},{72,8},{80,16},{88,24},{96,32},{104,40},{112,48},{120,56},{... | collective-permute-start | bytes 1179656 | tf_op jit(solution)/shard_map/ppermute | solution.py:20
  408.4 7.7 %copy-start.2 = (bf16[512,2048]{1,0:T(8,128)(2,1)S(1)}, bf16[512,2048]{1,0:T(8,128)(2,1)}, u32[]{:S(2)}) copy-start(bf16[512,2048]{1,0:T(8,128)(2,1)} %gather_fusion.3) | copy-start | bytes 6291460
  496.0 1.6 copy-start.5
  497.6 1.1 copy-start.4
  497.6 1.7 copy-start.6
  497.8 6.7 %copy-start.8 = (bf16[1,768,256]{2,1,0:T(8,128)(2,1)S(1)}, bf16[1,768,256]{2,1,0:T(8,128)(2,1)}, u32[]{:S(2)}) copy-start(bf16[1,768,256]{2,1,0:T(8,128)(2,1)} %broadcast_select_fusion.2) | copy-start | bytes 1179652
  497.8 6.7 %copy-start.10 = (f32[1,768,256]{2,1,0:T(8,128)S(1)}, f32[1,768,256]{2,1,0:T(8,128)}, u32[]{:S(2)}) copy-start(f32[1,768,256]{2,1,0:T(8,128)} %param.21) | copy-start | bytes 2359300
  497.8 6.7 %copy-start.12 = (f32[1,768,256]{2,1,0:T(8,128)S(1)}, f32[1,768,256]{2,1,0:T(8,128)}, u32[]{:S(2)}) copy-start(f32[1,768,256]{2,1,0:T(8,128)} %param.22) | copy-start | bytes 2359300
  499.3 8.1 %copy-start.1 = (bf16[128,2048]{1,0:T(8,128)(2,1)S(1)}, bf16[128,2048]{1,0:T(8,128)(2,1)}, u32[]{:S(2)}) copy-start(bf16[128,2048]{1,0:T(8,128)(2,1)} %param.13) | copy-start | bytes 1572868
Sparse Core Ops, SparseCore 0:
  38.7 125.1 all-gather.1
  301.5 193.1 reduce-scatter.1

commit v11 on v7

--- a/solution.py
+++ b/solution.py
@@ -147,16 +147,17 @@
         jnp.where(take_other, moved, owned)
         for moved, owned in zip(moved_states, (m_in, v_in, m_down, v_down))
     )
-    down_full = lax.all_gather(w_down, "shard", axis=2, tiled=True)
-    gate_parts, up_parts = exchange((w_in[0, 0], w_in[0, 1]), True, 0)
-    gate_weight = gate_parts.reshape(-1, gate_parts.shape[-1])
-    up_weight = up_parts.reshape(-1, up_parts.shape[-1])
-    down_weight = down_full[0]
+    in_full = lax.all_gather(w_in, "shard", axis=2, tiled=True)
+    gate_weight = in_full[0, 0]
+    up_weight = in_full[0, 1]
     hidden_width = gate_weight.shape[1]
     position, filler = route_table(expert_ids, partner[expert_ids], groups, capacity)
     token_fill = jnp.where(filler >= 0, filler // top_count, -1)
     send_rows = fill_rows(tokens, token_fill, groups, capacity)
     arrived = lax.all_to_all(send_rows, "expert", split_axis=0, concat_axis=0, tiled=True)
+    down_shard, arrived = lax.optimization_barrier((w_down[0], arrived))
+    (down_parts,) = exchange((down_shard,), True, 0)
+    down_weight = jnp.transpose(down_parts, (1, 0, 2)).reshape(down_parts.shape[1], -1)
     rows_x = arrived.reshape(groups * capacity, width)
     own_moments = (m_in, v_in, m_down, v_down)
     gate_pre = jnp.dot(rows_x, gate_weight, preferred_element_type=jnp.float32)

time: 511 us -> 492 us (0.963)
  Pallas kernels: 97.7 us -> 63.6 us
  waiting for transfers between devices: 191 us -> 201 us
    pallas_call x1, Pallas kernels: 97.7 us -> 63.6 us  [exchange(): pl.pallas_call(functools.partial(exchange_kernel, count, spread, width),...]
    ppermute x6, waiting for transfers between devices: 56.8 us -> 63.5 us  [shifted(): return lax.ppermute(block, axis, route)]
  transfers between devices with their start and end apart: 12 -> 12, of which waited for: 5 -> 6; matrix products, arithmetic and copies ran while one was open for 24% -> 25% of each run, Pallas kernels for 19% -> 13%
where the time goes in v11:
time: 492 us; the launch traced here: 485 us
  waiting for transfers between devices  201 us (41%)
  other arithmetic  65.6 us (13%)
  Pallas kernels  63.6 us (13%)
  local copies, waits for them, and re-layouts  50 us (10%)
  matrix products  48.3 us (10%)
  starting transfers between devices  40.8 us (8%)
  between operations  15.4 us (3%)
    pallas_call x1, Pallas kernels, exchange(): pl.pallas_call(functools.partial(exchange_kernel, count, spread, width),...  63.6 us
    ppermute x6, waiting for transfers between devices, shifted(): return lax.ppermute(block, axis, route)  63.5 us
    reduce_scatter x1, waiting for transfers between devices, body(): lax.psum_scatter(jnp.concatenate([contract_rows(rows_x, grad_both), contr...  55.1 us
    all_to_all x1, waiting for transfers between devices, body(): lax.all_to_all(entry_grads.reshape(groups, capacity, width), 'expert', sp...  33.9 us
    all_to_all x1, waiting for transfers between devices, body(): lax.all_to_all(expert_out.reshape(groups, capacity, width), 'expert', spl...  28.7 us
    all_to_all x1, waiting for transfers between devices, body(): lax.all_to_all(send_rows, 'expert', split_axis=0, concat_axis=0, tiled=True)  20.1 us
    dot_general x3, matrix products, contract_cols(): lax.dot_general(left, right, (((1,), (1,)), ((), ())), preferred_element_...  16.3 us
    dot_general x2, matrix products, contract_rows(): lax.dot_general(left, right, (((0,), (0,)), ((), ())), preferred_element_...  14.4 us
  transfers between devices with their start and end apart: 12, of which 6 were waited for; matrix products, arithmetic and copies ran while one was open for 25% of the time, Pallas kernels for 13%

profile of v11, /device:TPU:1, one launch (start us, length us, event | category | flops | bytes accessed | tf_op | source)
XLA Modules:
  0.0 485.2 jit_solution(4600986526036710558)
XLA Ops:
  7.2 3.8 collective-permute-start.1
  11.1 1.3 fusion.21
  13.0 15.3 %collective-permute-done.1 = bf16[1,2,256,768]{3,2,1,0:T(8,128)(2,1)S(1)} collective-permute-done((bf16[1,2,256,768]{3,2,1,0:T(8,128)(2,1)}, bf16[1,2,256,768]{3,2,1,0:T(8,128)(2,1)S(1)}, u32[]{:S(2)}, u32[]{:S(2)}) %collective-permute-start.1) | collective-permute-done | bytes 786464 | tf_op jit(solution)/shard_map/ppermute | solution.py:20
  28.3 2.1 broadcast_select_fusion.1
  31.4 10.1 %select_multiply_fusion = s32[128,4]{0,1:T(4,128)S(1)} fusion(s32[128,4]{0,1:T(4,128)S(1)} %copy-done.20, s32[]{:T(128)} %bitcast, s32[]{:T(128)} %bitcast.1, s32[]{:T(128)} %bitcast.2, s32[]{:T(128)} %bitcast.3, s32[]{:T(128)} %bitcast.4, s32[]{:T(128)} %bitcast.5, s32[]{:T(128)} %bitcast.6, s32[]{:T(128)} %bitcast.7, s32[]{:T(128)} %bitcast.8, s32[]{:T(128)} %bitcast.9, ...), kind=kLoop, calls=%fused_computation.67 | loop fusion | flops 17408 | bytes 4160 | tf_op jit(solution)/shard_map/mul | solution.py:101
  43.3 2.4 scatter_custom_fusion
  46.0 4.2 gather_fusion
  50.2 3.4 select_select_fusion.1
  53.6 7.5 %all-to-all-start = ((bf16[16,48,2048]{2,1,0:T(8,128)(2,1)}), bf16[16,48,2048]{2,1,0:T(8,128)(2,1)}, u32[]{:S(2)}, u32[]{:S(2)}) async-start(bf16[16,48,2048]{2,1,0:T(8,128)(2,1)} %select_select_fusion.1), calls=%async_computation | async-start | bytes 6291456 | tf_op jit(solution)/shard_map/all_to_all | solution.py:157
  61.2 3.0 mul.160
  64.2 5.4 %mul.161 = f32[512,2048]{1,0:T(8,128)} reshape(f32[128,4,2048]{2,1,0:T(4,128)} %mul.160) | data formatting | bytes 8388608 | tf_op jit(solution)/shard_map/mul | solution.py:183
  70.4 3.1 multiply_convert_fusion
  73.5 4.3 gather_fusion.1
  77.8 3.4 select_select_fusion
  81.1 20.1 %all-to-all-done = bf16[16,48,2048]{2,1,0:T(8,128)(2,1)} async-done(((bf16[16,48,2048]{2,1,0:T(8,128)(2,1)}), bf16[16,48,2048]{2,1,0:T(8,128)(2,1)}, u32[]{:S(2)}, u32[]{:S(2)}) %all-to-all-start) | async-done | bytes 3145760 | tf_op jit(solution)/shard_map/all_to_all | solution.py:157
  101.2 8.1 %all-to-all-start.2 = ((bf16[16,48,2048]{2,1,0:T(8,128)(2,1)}), bf16[16,48,2048]{2,1,0:T(8,128)(2,1)}, u32[]{:S(2)}, u32[]{:S(2)}) async-start(bf16[16,48,2048]{2,1,0:T(8,128)(2,1)} %select_select_fusion), calls=%async_computation.2 | async-start | bytes 6291456 | tf_op jit(solution)/shard_map/all_to_all | solution.py:187
  109.3 3.4 collective-permute-start
  112.8 48.3 %collective-permute-done = bf16[1,768,256]{2,1,0:T(8,128)(2,1)S(1)} collective-permute-done((bf16[1,768,256]{2,1,0:T(8,128)(2,1)S(1)}, bf16[1,768,256]{2,1,0:T(8,128)(2,1)S(1)}, u32[]{:S(2)}, u32[]{:S(2)}) %collective-permute-start) | collective-permute-done | bytes 393248 | tf_op jit(solution)/shard_map/ppermute | solution.py:20
  162.6 63.6 %shard_map.170 = bf16[8,768,256]{2,1,0:T(8,128)(2,1)} custom-call(bf16[768,256]{1,0:T(8,128)(2,1)} %fusion.11.refs_0_), custom_call_target="tpu_custom_call" | custom-call | bytes 6291456 | tf_op jit(solution)/shard_map/pallas_call | solution.py:64
  226.2 3.2 copy.27
  229.4 7.1 %fusion.26 = f32[768,768]{0,1:T(8,128)} fusion(bf16[768,2048]{1,0:T(8,128)(2,1)} %bitcast.29, bf16[768,2048]{0,1:T(8,128)(2,1)S(1)} %bitcast.107), kind=kOutput, calls=%fused_computation.81 | convolution fusion | flops 2415919104 | bytes 8650752 | tf_op jit(solution)/shard_map/dot_general | solution.py:120
  236.6 5.6 %fusion.2 = f32[768,768]{0,1:T(8,128)S(1)} fusion(bf16[768,2048]{1,0:T(8,128)(2,1)} %bitcast.21, bf16[1,2,2048,768]{3,2,1,0:T(8,128)(2,1)} %all-gather.2.cloned.1.call-done), kind=kOutput, calls=%fused_computation.18 | convolution fusion | flops 2415919104 | bytes 8650752 | tf_op jit(solution)/shard_map/dot_general | solution.py:164
  242.2 5.4 %multiply_convert_fusion.2 = (bf16[768,768]{0,1:T(8,128)(2,1)S(1)}, bf16[768,768]{0,1:T(8,128)(2,1)S(1)}, bf16[768,768]{0,1:T(8,128)(2,1)S(1)}) fusion(f32[768,768]{0,1:T(8,128)S(1)} %copy-done.24, f32[768,768]{0,1:T(8,128)S(1)} %fusion.2, bf16[768,2048]{1,0:T(8,128)(2,1)} %bitcast.21, bf16[1,2,2048,768]{3,2,1,0:T(8,128)(2,1)S(1)} %copy-done.22), kind=kOutput, calls=%fused_computation.24 | convolution fusion | flops 2424766464 | bytes 14548992 | tf_op jit(solution)/shard_map/dot_general | solution.py:163
  247.7 5.9 %convolution_convert_fusion.1 = bf16[2048,768]{0,1:T(8,128)(2,1)S(1)} fusion(bf16[768,768]{0,1:T(8,128)(2,1)S(1)} %get-tuple-element.23, bf16[768,2048]{1,0:T(8,128)(2,1)} %bitcast.29), kind=kOutput, calls=%fused_computation.10 | convolution fusion | flops 2417491968 | bytes 7471104 | tf_op jit(solution)/shard_map/dot_general | solution.py:114
  253.7 8.4 %convolution_convert_fusion = bf16[2048,1536]{0,1:T(8,128)(2,1)S(1)} fusion(bf16[768,2048]{1,0:T(8,128)(2,1)} %bitcast.21, bf16[768,768]{0,1:T(8,128)(2,1)S(1)} %get-tuple-element.22, bf16[768,768]{0,1:T(8,128)(2,1)S(1)} %get-tuple-element.21), kind=kOutput, calls=%fused_computation.6 | convolution fusion | flops 4839702528 | bytes 11796480 | tf_op jit(solution)/shard_map/dot_general | solution.py:114
  262.1 11.6 %pad_maximum_fusion = bf16[2048,2304]{0,1:T(8,128)(2,1)} fusion(bf16[2048,768]{0,1:T(8,128)(2,1)S(1)} %convolution_convert_fusion.1, bf16[2048,1536]{0,1:T(8,128)(2,1)S(1)} %convolution_convert_fusion), kind=kLoop, calls=%fused_computation.5 | loop fusion | flops 18874368 | bytes 18874368 | tf_op jit(solution)/shard_map/concatenate | solution.py:210
  273.7 5.1 %fusion.1 = f32[768,2048]{1,0:T(8,128)S(1)} fusion(bf16[768,768]{0,1:T(8,128)(2,1)} %copy-done.23, bf16[1,2,2048,768]{3,2,1,0:T(8,128)(2,1)} %all-gather.2.cloned.1.call-done), kind=kOutput, calls=%fused_computation.17 | convolution fusion | flops 2415919104 | bytes 10616832 | tf_op jit(solution)/shard_map/dot_general | solution.py:120
  278.8 4.1 add_convert_fusion
  282.9 4.7 all-to-all-start.3
  287.7 6.6 %convolution_convert_fusion.2 = bf16[768,2048]{1,0:T(8,128)(2,1)} fusion(bf16[768,768]{0,1:T(8,128)(2,1)} %copy-done.25, bf16[768,2048]{0,1:T(8,128)(2,1)} %bitcast.108), kind=kOutput, calls=%fused_computation.11 | convolution fusion | flops 2417491968 | bytes 7471104 | tf_op jit(solution)/shard_map/dot_general | solution.py:167
  294.3 33.9 %all-to-all-done.3 = bf16[16,48,2048]{2,1,0:T(8,128)(2,1)S(1)} async-done(((bf16[16,48,2048]{2,1,0:T(8,128)(2,1)}), bf16[16,48,2048]{2,1,0:T(8,128)(2,1)S(1)}, u32[]{:S(2)}, u32[]{:S(2)}) %all-to-all-start.3) | async-done | bytes 3145760 | tf_op jit(solution)/shard_map/all_to_all | solution.py:196
  328.2 7.1 %all-to-all-start.1 = ((bf16[16,48,2048]{2,1,0:T(8,128)(2,1)}), bf16[16,48,2048]{2,1,0:T(8,128)(2,1)}, u32[]{:S(2)}, u32[]{:S(2)}) async-start(bf16[16,48,2048]{2,1,0:T(8,128)(2,1)} %bitcast.109), calls=%async_computation.1 | async-start | bytes 6291456 | tf_op jit(solution)/shard_map/all_to_all | solution.py:170
  335.3 2.5 convert_element_type.94
  337.9 3.1 collective-permute-start.2
  342.8 2.9 collective-permute-start.4
  347.5 3.3 gather_fusion.3
  350.8 28.7 %all-to-all-done.1 = bf16[16,48,2048]{2,1,0:T(8,128)(2,1)} async-done(((bf16[16,48,2048]{2,1,0:T(8,128)(2,1)}), bf16[16,48,2048]{2,1,0:T(8,128)(2,1)}, u32[]{:S(2)}, u32[]{:S(2)}) %all-to-all-start.1) | async-done | bytes 3145760 | tf_op jit(solution)/shard_map/all_to_all | solution.py:170
  379.5 7.7 %gather_fusion.2 = bf16[512,2048]{1,0:T(8,128)(2,1)} fusion(bf16[768,2048]{1,0:T(8,128)(2,1)} %bitcast.27, s32[1024]{0:T(1024)S(1)} %pad_clamp_fusion.1), kind=kCustom, calls=%fused_computation.clone | custom fusion | bytes 4196352 | tf_op jit(solution)/shard_map/jit(_take)/gather | solution.py:177
  387.2 5.0 %broadcast_select_fusion = (bf16[512,2048]{1,0:T(8,128)(2,1)}, f32[512,2048]{1,0:T(8,128)}) fusion(bf16[512,2048]{1,0:T(8,128)(2,1)S(1)} %copy-done.2, pred[512]{0:T(512)(128)(4,1)S(1)} %get-tuple-element.19, bf16[512,2048]{1,0:T(8,128)(2,1)} %gather_fusion.2), kind=kLoop, calls=%fused_computation.29 | loop fusion | flops 3145728 | bytes 10486272 | tf_op jit(solution)/shard_map/jit(_take)/select_n | solution.py:203
  392.1 5.2 %reshape.157 = f32[128,4,2048]{2,1,0:T(4,128)} reshape(f32[512,2048]{1,0:T(8,128)} %get-tuple-element.31) | data formatting | bytes 8388608 | tf_op jit(solution)/shard_map/convert_element_type | solution.py:180
  397.3 2.7 reshape.155
  400.1 3.9 reduce_sum.45
  403.9 6.3 %multiply_reduce_fusion = bf16[128,2048]{1,0:T(8,128)(2,1)} fusion(f32[128,4,2048]{2,1,0:T(4,128)} %reshape.157, f32[128,4]{1,0:T(8,128)S(1)} %copy-done.16), kind=kLoop, calls=%fused_computation.9 | loop fusion | flops 1835008 | bytes 4720640 | tf_op jit(solution)/shard_map/reduce_sum | solution.py:180
  410.3 55.1 %reduce-scatter.2.cloned.1.call-done = bf16[256,2304]{0,1:T(8,128)(2,1)} async-done(((bf16[2048,2304]{0,1:T(8,128)(2,1)}), bf16[256,2304]{0,1:T(8,128)(2,1)}) %reduce-scatter.2.cloned.1.call-update) | async-done | bytes 1179664 | tf_op jit(solution)/shard_map/reduce_scatter | solution.py:209
  465.4 1.2 slice.52
  466.7 1.6 copy.29
  469.9 5.2 %subtract_convert_fusion = (bf16[1,2,256,768]{3,2,1,0:T(8,128)(2,1)}, f32[1,2,256,768]{3,2,1,0:T(8,128)}, f32[1,2,256,768]{3,2,1,0:T(8,128)}) fusion(bf16[1,2,256,768]{3,2,1,0:T(8,128)(2,1)S(1)} %copy-done.3, f32[256,2,768]{2,0,1:T(8,128)} %copy.29, f32[1,2,256,768]{3,2,1,0:T(8,128)S(1)} %copy-done.5, bf16[1,2,256,768]{3,2,1,0:T(8,128)(2,1)} %collective-permute-done.2, ...), kind=kLoop, calls=%fused_computation.34 | loop fusion | flops 7077888 | bytes 11010049 | tf_op jit(solution)/shard_map/convert_element_type | solution.py:92
  475.2 2.9 subtract_convert_fusion.1
  (104 shorter events, 10.9 us)
Async XLA Ops:
  7.2 38.8 %copy-start = (bf16[128,2048]{1,0:T(8,128)(2,1)S(1)}, bf16[128,2048]{1,0:T(8,128)(2,1)}, u32[]{:S(2)}) copy-start(bf16[128,2048]{1,0:T(8,128)(2,1)} %param.13) | copy-start | bytes 1572868
  7.2 23.6 %copy-start.19 = (s32[16]{0:T(128)S(1)}, s32[16]{0:T(128)}, u32[]{:S(2)}) copy-start(s32[16]{0:T(128)} %param.16) | copy-start | bytes 196
  7.2 23.2 %copy-start.20 = (s32[128,4]{0,1:T(4,128)S(1)}, s32[128,4]{0,1:T(4,128)}, u32[]{:S(2)}) copy-start(s32[128,4]{0,1:T(4,128)} %param.14) | copy-start | bytes 6148
  7.2 229.3 %all-gather.2.cloned.1.call-start = ((), (), s32[]{:S(2)}) async-start(), calls=%async_computation.5 | async-start | bytes 7077888 | tf_op jit(solution)/shard_map/all_gather | solution.py:150
  7.2 21.0 %collective-permute-start.1 = (bf16[1,2,256,768]{3,2,1,0:T(8,128)(2,1)}, bf16[1,2,256,768]{3,2,1,0:T(8,128)(2,1)S(1)}, u32[]{:S(2)}, u32[]{:S(2)}) collective-permute-start(bf16[1,2,256,768]{3,2,1,0:T(8,128)(2,1)} %param.17), channel_id=1, source_target_pairs={{64,0},{72,8},{80,16},{88,24},{96,32},{104,40},{112,48},{120,56},{... | collective-permute-start | bytes 2359304 | tf_op jit(solution)/shard_map/ppermute | solution.py:20
  41.7 8.6 %copy-start.17 = (s32[128,4]{1,0:T(8,128)}, s32[128,4]{1,0:T(8,128)S(1)}, u32[]{:S(2)}) copy-start(s32[128,4]{1,0:T(8,128)S(1)} %copy.22) | copy-start | bytes 6148
  53.6 7.5 %copy-start.18 = (bf16[128,2048]{1,0:T(8,128)(2,1)S(1)}, bf16[128,2048]{1,0:T(8,128)(2,1)}, u32[]{:S(2)}) copy-start(bf16[128,2048]{1,0:T(8,128)(2,1)} %param.23) | copy-start | bytes 1572868
  53.6 47.6 %all-to-all-start = ((bf16[16,48,2048]{2,1,0:T(8,128)(2,1)}), bf16[16,48,2048]{2,1,0:T(8,128)(2,1)}, u32[]{:S(2)}, u32[]{:S(2)}) async-start(bf16[16,48,2048]{2,1,0:T(8,128)(2,1)} %select_select_fusion.1), calls=%async_computation | async-start | bytes 6291456 | tf_op jit(solution)/shard_map/all_to_all | solution.py:157
  64.2 5.4 %copy-start.21 = (f32[128,4]{0,1:T(4,128)S(1)}, f32[128,4]{0,1:T(4,128)}, u32[]{:S(2)}) copy-start(f32[128,4]{0,1:T(4,128)} %param.15) | copy-start | bytes 6148
  69.7 0.6 copy-start.15
  81.1 28.2 %copy-start.12 = (bf16[1,768,256]{2,1,0:T(8,128)(2,1)S(1)}, bf16[1,768,256]{2,1,0:T(8,128)(2,1)}, u32[]{:S(2)}) copy-start(bf16[1,768,256]{2,1,0:T(8,128)(2,1)} %param.18) | copy-start | bytes 1179652
  101.2 128.2 %all-to-all-start.2 = ((bf16[16,48,2048]{2,1,0:T(8,128)(2,1)}), bf16[16,48,2048]{2,1,0:T(8,128)(2,1)}, u32[]{:S(2)}, u32[]{:S(2)}) async-start(bf16[16,48,2048]{2,1,0:T(8,128)(2,1)} %select_select_fusion), calls=%async_computation.2 | async-start | bytes 6291456 | tf_op jit(solution)/shard_map/all_to_all | solution.py:187
  109.3 356.1 %reduce-scatter.2.cloned.1.call-start = ((), (), s32[]{:S(2)}) async-start(), calls=%async_computation.6 | async-start | bytes 10616832 | tf_op jit(solution)/shard_map/reduce_scatter | solution.py:209
  109.3 51.7 %collective-permute-start = (bf16[1,768,256]{2,1,0:T(8,128)(2,1)S(1)}, bf16[1,768,256]{2,1,0:T(8,128)(2,1)S(1)}, u32[]{:S(2)}, u32[]{:S(2)}) collective-permute-start(bf16[1,768,256]{2,1,0:T(8,128)(2,1)S(1)} %copy-done.12), channel_id=1, source_target_pairs={{64,0},{72,8},{80,16},{88,24},{96,32},{104,40},{112,48},{120,56},{... | collective-permute-start | bytes 1179656 | tf_op jit(solution)/shard_map/ppermute | solution.py:20
  161.1 0.8 copy-start.13
  229.4 7.1 %copy-start.11 = (bf16[768,8,256]{0,2,1:T(8,128)(2,1)}, bf16[768,8,256]{0,2,1:T(8,128)(2,1)S(1)}, u32[]{:S(2)}) copy-start(bf16[768,8,256]{0,2,1:T(8,128)(2,1)S(1)} %copy.27) | copy-start | bytes 9437188
  236.5 5.7 %copy-start.22 = (bf16[1,2,2048,768]{3,2,1,0:T(8,128)(2,1)S(1)}, bf16[1,2,2048,768]{3,2,1,0:T(8,128)(2,1)}, u32[]{:S(2)}) copy-start(bf16[1,2,2048,768]{3,2,1,0:T(8,128)(2,1)} %all-gather.2.cloned.1.call-done) | copy-start | bytes 18874372
  236.5 5.7 %copy-start.24 = (f32[768,768]{0,1:T(8,128)S(1)}, f32[768,768]{0,1:T(8,128)}, u32[]{:S(2)}) copy-start(f32[768,768]{0,1:T(8,128)} %fusion.26) | copy-start | bytes 7077892
  247.6 6.0 %copy-start.25 = (bf16[768,768]{0,1:T(8,128)(2,1)}, bf16[768,768]{0,1:T(8,128)(2,1)S(1)}, u32[]{:S(2)}) copy-start(bf16[768,768]{0,1:T(8,128)(2,1)S(1)} %get-tuple-element.23) | copy-start | bytes 3538948
  247.6 6.0 %copy-start.23 = (bf16[768,768]{0,1:T(8,128)(2,1)}, bf16[768,768]{0,1:T(8,128)(2,1)S(1)}, u32[]{:S(2)}) copy-start(bf16[768,768]{0,1:T(8,128)(2,1)S(1)} %get-tuple-element.22) | copy-start | bytes 3538948
  247.7 6.0 %copy-start.26 = (bf16[768,768]{0,1:T(8,128)(2,1)}, bf16[768,768]{0,1:T(8,128)(2,1)S(1)}, u32[]{:S(2)}) copy-start(bf16[768,768]{0,1:T(8,128)(2,1)S(1)} %get-tuple-element.21) | copy-start | bytes 3538948
  273.7 5.1 %slice-start = ((s8[6291456]{0:T(1024)(128)(4,1)}), s8[2097152]{0:T(1024)(128)(4,1)S(1)}, s32[]{:S(2)}) async-start(s8[6291456]{0:T(1024)(128)(4,1)} %bitcast.113), calls=%async_computation.7 | async-start | bytes 4194304
  273.7 5.1 %slice-start.1 = ((s8[6291456]{0:T(1024)(128)(4,1)}), s8[4194304]{0:T(1024)(128)(4,1)S(1)}, s32[]{:S(2)}) async-start(s8[6291456]{0:T(1024)(128)(4,1)} %bitcast.113), calls=%async_computation.8 | async-start | bytes 8388608
  273.7 5.1 %copy-start.27 = (bf16[768,768]{0,1:T(8,128)(2,1)S(1)}, bf16[768,768]{0,1:T(8,128)(2,1)}, u32[]{:S(2)}) copy-start(bf16[768,768]{0,1:T(8,128)(2,1)} %copy-done.26) | copy-start | bytes 3538948
  282.9 45.3 %all-to-all-start.3 = ((bf16[16,48,2048]{2,1,0:T(8,128)(2,1)}), bf16[16,48,2048]{2,1,0:T(8,128)(2,1)S(1)}, u32[]{:S(2)}, u32[]{:S(2)}) async-start(bf16[16,48,2048]{2,1,0:T(8,128)(2,1)} %bitcast.110), calls=%async_computation.3 | async-start | bytes 6291456 | tf_op jit(solution)/shard_map/all_to_all | solution.py:196
  328.2 51.2 %all-to-all-start.1 = ((bf16[16,48,2048]{2,1,0:T(8,128)(2,1)}), bf16[16,48,2048]{2,1,0:T(8,128)(2,1)}, u32[]{:S(2)}, u32[]{:S(2)}) async-start(bf16[16,48,2048]{2,1,0:T(8,128)(2,1)} %bitcast.109), calls=%async_computation.1 | async-start | bytes 6291456 | tf_op jit(solution)/shard_map/all_to_all | solution.py:170
  335.3 5.6 %copy-start.6 = (f32[1,2,256,768]{3,2,1,0:T(8,128)S(1)}, f32[1,2,256,768]{3,2,1,0:T(8,128)}, u32[]{:S(2)}) copy-start(f32[1,2,256,768]{3,2,1,0:T(8,128)} %param.20) | copy-start | bytes 4718596
  335.3 6.7 %copy-start.7 = (f32[1,768,256]{2,1,0:T(8,128)S(1)}, f32[1,768,256]{2,1,0:T(8,128)}, u32[]{:S(2)}) copy-start(f32[1,768,256]{2,1,0:T(8,128)} %param.21) | copy-start | bytes 2359300
  335.3 10.3 %copy-start.9 = (f32[1,768,256]{2,1,0:T(8,128)S(1)}, f32[1,768,256]{2,1,0:T(8,128)}, u32[]{:S(2)}) copy-start(f32[1,768,256]{2,1,0:T(8,128)} %param.22) | copy-start | bytes 2359300
  337.9 130.6 %collective-permute-start.2 = (bf16[1,2,256,768]{3,2,1,0:T(8,128)(2,1)}, bf16[1,2,256,768]{3,2,1,0:T(8,128)(2,1)}, u32[]{:S(2)}, u32[]{:S(2)}) collective-permute-start(bf16[1,2,256,768]{3,2,1,0:T(8,128)(2,1)} %convert_element_type.94), channel_id=1, source_target_pairs={{64,0},{72,8},{80,16},{88,24},{96,32},{104,40},{112,48},{120,56},{... | collective-permute-start | bytes 2359304 | tf_op jit(solution)/shard_map/ppermute | solution.py:20
  341.9 126.6 %collective-permute-start.3 = (bf16[1,2,256,768]{3,2,1,0:T(8,128)(2,1)}, bf16[1,2,256,768]{3,2,1,0:T(8,128)(2,1)}, u32[]{:S(2)}, u32[]{:S(2)}) collective-permute-start(bf16[1,2,256,768]{3,2,1,0:T(8,128)(2,1)} %convert_element_type.97), channel_id=1, source_target_pairs={{64,0},{72,8},{80,16},{88,24},{96,32},{104,40},{112,48},{120,56},{... | collective-permute-start | bytes 2359304 | tf_op jit(solution)/shard_map/ppermute | solution.py:20
  342.8 132.4 %collective-permute-start.4 = (bf16[1,768,256]{2,1,0:T(8,128)(2,1)}, bf16[1,768,256]{2,1,0:T(8,128)(2,1)}, u32[]{:S(2)}, u32[]{:S(2)}) collective-permute-start(bf16[1,768,256]{2,1,0:T(8,128)(2,1)} %convert_element_type.101), channel_id=1, source_target_pairs={{64,0},{72,8},{80,16},{88,24},{96,32},{104,40},{112,48},{120,56},{... | collective-permute-start | bytes 1179656 | tf_op jit(solution)/shard_map/ppermute | solution.py:20
  346.4 128.7 %collective-permute-start.5 = (bf16[1,768,256]{2,1,0:T(8,128)(2,1)}, bf16[1,768,256]{2,1,0:T(8,128)(2,1)}, u32[]{:S(2)}, u32[]{:S(2)}) collective-permute-start(bf16[1,768,256]{2,1,0:T(8,128)(2,1)} %convert_element_type.103), channel_id=1, source_target_pairs={{64,0},{72,8},{80,16},{88,24},{96,32},{104,40},{112,48},{120,56},{... | collective-permute-start | bytes 1179656 | tf_op jit(solution)/shard_map/ppermute | solution.py:20
  379.5 7.7 %copy-start.2 = (bf16[512,2048]{1,0:T(8,128)(2,1)S(1)}, bf16[512,2048]{1,0:T(8,128)(2,1)}, u32[]{:S(2)}) copy-start(bf16[512,2048]{1,0:T(8,128)(2,1)} %gather_fusion.3) | copy-start | bytes 6291460
  400.1 3.9 copy-start.16
  466.6 1.6 copy-start.4
  468.3 1.1 copy-start.3
  468.3 1.7 copy-start.5
  468.5 6.7 %copy-start.8 = (f32[1,768,256]{2,1,0:T(8,128)S(1)}, f32[1,768,256]{2,1,0:T(8,128)}, u32[]{:S(2)}) copy-start(f32[1,768,256]{2,1,0:T(8,128)} %param.21) | copy-start | bytes 2359300
  468.5 6.7 %copy-start.10 = (f32[1,768,256]{2,1,0:T(8,128)S(1)}, f32[1,768,256]{2,1,0:T(8,128)}, u32[]{:S(2)}) copy-start(f32[1,768,256]{2,1,0:T(8,128)} %param.22) | copy-start | bytes 2359300
  468.5 6.7 %copy-start.14 = (bf16[1,768,256]{2,1,0:T(8,128)(2,1)S(1)}, bf16[1,768,256]{2,1,0:T(8,128)(2,1)}, u32[]{:S(2)}) copy-start(bf16[1,768,256]{2,1,0:T(8,128)(2,1)} %copy-done.13) | copy-start | bytes 1179652
  469.9 8.2 %copy-start.1 = (bf16[128,2048]{1,0:T(8,128)(2,1)S(1)}, bf16[128,2048]{1,0:T(8,128)(2,1)}, u32[]{:S(2)}) copy-start(bf16[128,2048]{1,0:T(8,128)(2,1)} %param.13) | copy-start | bytes 1572868
Sparse Core Ops, SparseCore 0:
  30.5 169.2 all-gather.1
  273.8 191.5 reduce-scatter.1

commit v12 on v1

--- a/solution.py
+++ b/solution.py
@@ -146,18 +146,19 @@
     token_grad = jnp.sum(per_back.astype(jnp.float32), axis=1).astype(jnp.bfloat16)
     grad_both = jnp.concatenate([grad_gate, grad_up], axis=1)
     share_rows = width // lax.axis_size("shard")
-    shares = lax.psum_scatter(
-        jnp.concatenate(
-            [contract_rows(rows_x, grad_both), contract_rows(dout_rows, hidden)], axis=1
-        ).astype(jnp.bfloat16),
+    in_share, down_share = lax.psum_scatter(
+        (
+            contract_rows(rows_x, grad_both).astype(jnp.bfloat16),
+            contract_rows(dout_rows, hidden).astype(jnp.bfloat16),
+        ),
         "shard",
         scatter_dimension=0,
         tiled=True,
-    ).astype(jnp.float32)
+    )
     grad_in = jnp.transpose(
-        shares[:, : 2 * hidden_width].reshape(share_rows, 2, hidden_width), (1, 0, 2)
+        in_share.astype(jnp.float32).reshape(share_rows, 2, hidden_width), (1, 0, 2)
     )[None]
-    grad_down = jnp.transpose(shares[:, 2 * hidden_width :])[None]
+    grad_down = jnp.transpose(down_share.astype(jnp.float32))[None]
     new_in, first_in, second_in = adam_update(w_in, own_moments[0], own_moments[1], grad_in)
     new_down, first_down, second_down = adam_update(
         w_down, own_moments[2], own_moments[3], grad_down

time: 467 us -> 540 us (1.16)
  waiting for transfers between devices: 250 us -> 318 us
  other arithmetic: 63.4 us -> 50.8 us
  matrix products: 43.3 us -> 52.6 us
  local copies, waits for them, and re-layouts: 45.1 us -> 53.5 us
    all_gather x1, waiting for transfers between devices: 0.02 us -> 62.8 us  [body(): lax.all_gather(w_down, 'shard', axis=2, tiled=True)]
    all_to_all x1, waiting for transfers between devices: 32.1 us -> 0.01 us  [body(): lax.all_to_all(send_grads, 'expert', split_axis=0, concat_axis=0, tiled=T...]
    all_gather x1, waiting for transfers between devices: 46.9 us -> 71.9 us  [body(): lax.all_gather(w_in, 'shard', axis=2, tiled=True)]
    reduce_scatter x1 -> x2, waiting for transfers between devices: 50.9 us -> 72.9 us  [body(): lax.psum_scatter((contract_rows(rows_x, grad_both).astype(jnp.bfloat16),...]
    ppermute x6, waiting for transfers between devices: 23.2 us -> 36.3 us  [shifted(): return lax.ppermute(block, axis, route)]
    concatenate x1 -> x0, other arithmetic: 11.6 us -> none  [body(): jnp.concatenate([contract_rows(rows_x, grad_both), contract_rows(dout_row...]
    all_to_all x1, waiting for transfers between devices: 32.5 us -> 21 us  [body(): lax.all_to_all(send_rows, 'expert', split_axis=0, concat_axis=0, tiled=True)]
    unnamed x50 -> x54, local copies, waits for them, and re-layouts: 1.75 us -> 12.3 us
  transfers between devices with their start and end apart: 13 -> 14, of which waited for: 8 -> 11; matrix products, arithmetic and copies ran while one was open for 25% -> 22% of each run, Pallas kernels for 0% -> 0%
where the time goes in v12:
time: 540 us; the launch traced here: 533 us
  waiting for transfers between devices  318 us (59%)
  local copies, waits for them, and re-layouts  53.5 us (10%)
  matrix products  52.6 us (10%)
  other arithmetic  50.8 us (9%)
  starting transfers between devices  42.7 us (8%)
  between operations  15.1 us (3%)
    reduce_scatter x2, waiting for transfers between devices, body(): lax.psum_scatter((contract_rows(rows_x, grad_both).astype(jnp.bfloat16),...  72.9 us
    all_gather x1, waiting for transfers between devices, body(): lax.all_gather(w_in, 'shard', axis=2, tiled=True)  71.9 us
    all_gather x1, waiting for transfers between devices, body(): lax.all_gather(w_down, 'shard', axis=2, tiled=True)  62.8 us
    ppermute x6, waiting for transfers between devices, shifted(): return lax.ppermute(block, axis, route)  36.3 us
    all_to_all x1, waiting for transfers between devices, body(): lax.all_to_all(expert_out.reshape(groups, capacity, width), 'expert', spl...  29.2 us
    all_to_all x1, waiting for transfers between devices, body(): lax.all_to_all(entry_grads.reshape(groups, capacity, width), 'expert', sp...  23.9 us
    all_to_all x1, waiting for transfers between devices, body(): lax.all_to_all(send_rows, 'expert', split_axis=0, concat_axis=0, tiled=True)  21 us
    dot_general x3, matrix products, contract_cols(): lax.dot_general(left, right, (((1,), (1,)), ((), ())), preferred_element_...  18.7 us
  transfers between devices with their start and end apart: 14, of which 11 were waited for; matrix products, arithmetic and copies ran while one was open for 22% of the time, Pallas kernels for 0%

profile of v12, /device:TPU:1, one launch (start us, length us, event | category | flops | bytes accessed | tf_op | source)
XLA Modules:
  0.0 532.5 jit_solution(3592675209228804814)
XLA Ops:
  7.2 3.8 collective-permute-start
  13.0 15.3 %collective-permute-done = bf16[1,2,256,768]{3,2,1,0:T(8,128)(2,1)S(1)} collective-permute-done((bf16[1,2,256,768]{3,2,1,0:T(8,128)(2,1)}, bf16[1,2,256,768]{3,2,1,0:T(8,128)(2,1)S(1)}, u32[]{:S(2)}, u32[]{:S(2)}) %collective-permute-start) | collective-permute-done | bytes 786464 | tf_op jit(solution)/shard_map/ppermute | solution.py:17
  30.3 10.1 %select_multiply_fusion = s32[128,4]{0,1:T(4,128)S(1)} fusion(s32[128,4]{0,1:T(4,128)S(1)} %copy-done.15, s32[]{:T(128)} %bitcast, s32[]{:T(128)} %bitcast.1, s32[]{:T(128)} %bitcast.2, s32[]{:T(128)} %bitcast.3, s32[]{:T(128)} %bitcast.4, s32[]{:T(128)} %bitcast.5, s32[]{:T(128)} %bitcast.6, s32[]{:T(128)} %bitcast.7, s32[]{:T(128)} %bitcast.8, s32[]{:T(128)} %bitcast.9, ...), kind=kLoop, calls=%fused_computation.70 | loop fusion | flops 17408 | bytes 4160 | tf_op jit(solution)/shard_map/mul | solution.py:40
  42.2 2.4 scatter_custom_fusion
  44.9 4.3 gather_fusion
  49.2 3.4 select_select_fusion.1
  52.6 7.5 %all-to-all-start = ((bf16[16,48,2048]{2,1,0:T(8,128)(2,1)}), bf16[16,48,2048]{2,1,0:T(8,128)(2,1)}, u32[]{:S(2)}, u32[]{:S(2)}) async-start(bf16[16,48,2048]{2,1,0:T(8,128)(2,1)} %select_select_fusion.1), calls=%async_computation | async-start | bytes 6291456 | tf_op jit(solution)/shard_map/all_to_all | solution.py:100
  60.4 3.0 mul.160
  63.4 5.3 mul.161
  68.8 2.8 multiply_convert_fusion
  71.6 4.3 gather_fusion.1
  75.9 3.3 select_select_fusion
  79.3 21.0 %all-to-all-done = bf16[16,48,2048]{2,1,0:T(8,128)(2,1)} async-done(((bf16[16,48,2048]{2,1,0:T(8,128)(2,1)}), bf16[16,48,2048]{2,1,0:T(8,128)(2,1)}, u32[]{:S(2)}, u32[]{:S(2)}) %all-to-all-start) | async-done | bytes 3145760 | tf_op jit(solution)/shard_map/all_to_all | solution.py:100
  100.2 8.1 %all-to-all-start.2 = ((bf16[16,48,2048]{2,1,0:T(8,128)(2,1)}), bf16[16,48,2048]{2,1,0:T(8,128)(2,1)S(1)}, u32[]{:S(2)}, u32[]{:S(2)}) async-start(bf16[16,48,2048]{2,1,0:T(8,128)(2,1)} %select_select_fusion), calls=%async_computation.2 | async-start | bytes 6291456 | tf_op jit(solution)/shard_map/all_to_all | solution.py:127
  108.9 71.9 %all-gather.3.cloned.1.call-done = bf16[1,2,2048,768]{3,2,1,0:T(8,128)(2,1)} async-done(((bf16[1,2,256,768]{3,2,1,0:T(8,128)(2,1)}), bf16[1,2,2048,768]{3,2,1,0:T(8,128)(2,1)}) %all-gather.3.cloned.1.call-update) | async-done | bytes 6291472 | tf_op jit(solution)/shard_map/all_gather | solution.py:90
  180.7 5.8 %fusion.3 = f32[768,768]{0,1:T(8,128)S(1)} fusion(bf16[768,2048]{1,0:T(8,128)(2,1)} %bitcast.20, bf16[1,2,2048,768]{3,2,1,0:T(8,128)(2,1)} %all-gather.3.cloned.1.call-done), kind=kOutput, calls=%fused_computation.18 | convolution fusion | flops 2415919104 | bytes 8650752 | tf_op jit(solution)/shard_map/dot_general | solution.py:103
  188.0 6.8 %multiply_convert_fusion.3 = (bf16[768,768]{0,1:T(8,128)(2,1)}, f32[768,768]{0,1:T(8,128)}) fusion(f32[768,768]{0,1:T(8,128)S(1)} %fusion.3, bf16[768,2048]{1,0:T(8,128)(2,1)} %bitcast.20, bf16[1,2,2048,768]{3,2,1,0:T(8,128)(2,1)S(1)} %copy-done.17), kind=kOutput, calls=%fused_computation.27 | convolution fusion | flops 2419458048 | bytes 12189696 | tf_op jit(solution)/shard_map/dot_general | solution.py:104
  194.8 6.3 %convolution_convert_fusion.1 = bf16[2048,768]{1,0:T(8,128)(2,1)} fusion(bf16[768,2048]{1,0:T(8,128)(2,1)S(1)} %bitcast.125, bf16[768,768]{0,1:T(8,128)(2,1)} %get-tuple-element.60), kind=kOutput, calls=%fused_computation.9 | convolution fusion | flops 2417491968 | bytes 7471104 | tf_op jit(solution)/shard_map/dot_general | solution.py:53
  202.5 2.9 collective-permute-start.4
  206.8 2.9 collective-permute-start.1
  209.8 4.3 collective-permute-done.4
  214.0 8.3 %collective-permute-done.5 = bf16[1,768,256]{1,2,0:T(8,128)(2,1)S(1)} collective-permute-done((bf16[1,768,256]{1,2,0:T(8,128)(2,1)}, bf16[1,768,256]{1,2,0:T(8,128)(2,1)S(1)}, u32[]{:S(2)}, u32[]{:S(2)}) %collective-permute-start.5) | collective-permute-done | bytes 393248 | tf_op jit(solution)/shard_map/ppermute | solution.py:17
  222.3 8.4 %collective-permute-done.1 = bf16[1,768,256]{1,2,0:T(8,128)(2,1)S(1)} collective-permute-done((bf16[1,768,256]{1,2,0:T(8,128)(2,1)S(1)}, bf16[1,768,256]{1,2,0:T(8,128)(2,1)S(1)}, u32[]{:S(2)}, u32[]{:S(2)}) %collective-permute-start.1) | collective-permute-done | bytes 393248 | tf_op jit(solution)/shard_map/ppermute | solution.py:17
  230.8 47.2 %reduce-scatter.5.cloned.1.call-done = bf16[256,768]{1,0:T(8,128)(2,1)} async-done(((bf16[2048,768]{1,0:T(8,128)(2,1)}), bf16[256,768]{1,0:T(8,128)(2,1)}) %reduce-scatter.5.cloned.1.call-update) | async-done | bytes 393232 | tf_op jit(solution)/shard_map/reduce_scatter | solution.py:149
  278.0 2.8 subtract_convert_fusion.1
  281.0 62.8 %all-gather.5.cloned.1.call-done = bf16[1,768,2048]{1,2,0:T(8,128)(2,1)} async-done(((bf16[1,768,256]{1,2,0:T(8,128)(2,1)}), bf16[1,768,2048]{1,2,0:T(8,128)(2,1)}) %all-gather.5.cloned.1.call-update) | async-done | bytes 3145744 | tf_op jit(solution)/shard_map/all_gather | solution.py:91
  343.9 7.6 %multiply_convert_fusion.2 = (bf16[768,768]{0,1:T(8,128)(2,1)S(1)}, bf16[768,768]{0,1:T(8,128)(2,1)S(1)}) fusion(f32[768,768]{0,1:T(8,128)} %copy-done.20, f32[768,768]{0,1:T(8,128)} %get-tuple-element.61, bf16[768,2048]{1,0:T(8,128)(2,1)} %bitcast.126, bf16[1,768,2048]{1,2,0:T(8,128)(2,1)} %all-gather.5.cloned.1.call-done), kind=kOutput, calls=%fused_computation.26 | convolution fusion | flops 2423586816 | bytes 13369344 | tf_op jit(solution)/shard_map/dot_general | solution.py:59
  352.9 9.6 %convolution_convert_fusion = bf16[2048,1536]{1,0:T(8,128)(2,1)} fusion(bf16[768,2048]{1,0:T(8,128)(2,1)} %bitcast.20, bf16[768,768]{0,1:T(8,128)(2,1)S(1)} %get-tuple-element.35, bf16[768,768]{0,1:T(8,128)(2,1)S(1)} %get-tuple-element.34), kind=kOutput, calls=%fused_computation.5 | convolution fusion | flops 4839702528 | bytes 11796480 | tf_op jit(solution)/shard_map/dot_general | solution.py:53
  364.5 5.4 %convolution_convert_fusion.2 = bf16[768,2048]{1,0:T(8,128)(2,1)} fusion(bf16[768,768]{0,1:T(8,128)(2,1)} %get-tuple-element.60, bf16[1,768,2048]{1,2,0:T(8,128)(2,1)S(1)} %copy-done.18), kind=kOutput, calls=%fused_computation.10 | convolution fusion | flops 2417491968 | bytes 7471104 | tf_op jit(solution)/shard_map/dot_general | solution.py:107
  369.9 5.8 %all-to-all-start.1 = ((bf16[16,48,2048]{2,1,0:T(8,128)(2,1)}), bf16[16,48,2048]{2,1,0:T(8,128)(2,1)S(1)}, u32[]{:S(2)}, u32[]{:S(2)}) async-start(bf16[16,48,2048]{2,1,0:T(8,128)(2,1)} %bitcast.128), calls=%async_computation.1 | async-start | bytes 6291456 | tf_op jit(solution)/shard_map/all_to_all | solution.py:110
  375.7 5.0 fusion.4
  380.7 6.1 %add_convert_fusion = bf16[768,2048]{1,0:T(8,128)(2,1)} fusion(f32[768,2048]{1,0:T(8,128)S(1)} %fusion.4, bf16[768,768]{0,1:T(8,128)(2,1)S(1)} %copy-done.22, bf16[1,2,2048,768]{3,2,1,0:T(8,128)(2,1)} %all-gather.3.cloned.1.call-done), kind=kOutput, calls=%fused_computation.6 | convolution fusion | flops 2419064832 | bytes 13762560 | tf_op jit(solution)/shard_map/dot_general | solution.py:59
  386.7 29.2 %all-to-all-done.1 = bf16[16,48,2048]{2,1,0:T(8,128)(2,1)S(1)} async-done(((bf16[16,48,2048]{2,1,0:T(8,128)(2,1)}), bf16[16,48,2048]{2,1,0:T(8,128)(2,1)S(1)}, u32[]{:S(2)}, u32[]{:S(2)}) %all-to-all-start.1) | async-done | bytes 3145760 | tf_op jit(solution)/shard_map/all_to_all | solution.py:110
  415.9 7.7 %all-to-all-start.3 = ((bf16[16,48,2048]{2,1,0:T(8,128)(2,1)}), bf16[16,48,2048]{2,1,0:T(8,128)(2,1)}, u32[]{:S(2)}, u32[]{:S(2)}) async-start(bf16[16,48,2048]{2,1,0:T(8,128)(2,1)} %bitcast.127), calls=%async_computation.3 | async-start | bytes 6291456 | tf_op jit(solution)/shard_map/all_to_all | solution.py:136
  423.6 2.5 convert_element_type.98
  426.1 2.9 collective-permute-start.2
  431.1 2.3 copy.45
  433.3 2.3 copy.46
  436.6 3.3 gather_fusion.2
  439.8 23.9 %all-to-all-done.3 = bf16[16,48,2048]{2,1,0:T(8,128)(2,1)} async-done(((bf16[16,48,2048]{2,1,0:T(8,128)(2,1)}), bf16[16,48,2048]{2,1,0:T(8,128)(2,1)}, u32[]{:S(2)}, u32[]{:S(2)}) %all-to-all-start.3) | async-done | bytes 3145760 | tf_op jit(solution)/shard_map/all_to_all | solution.py:136
  463.7 7.7 %gather_fusion.3 = bf16[512,2048]{1,0:T(8,128)(2,1)} fusion(bf16[768,2048]{1,0:T(8,128)(2,1)} %bitcast.29, s32[1024]{0:T(1024)S(1)} %pad_clamp_fusion.1), kind=kCustom, calls=%fused_computation.1.clone | custom fusion | bytes 4196352 | tf_op jit(solution)/shard_map/jit(_take)/gather | solution.py:143
  471.4 4.8 broadcast_select_fusion
  476.2 5.2 reshape.154
  481.4 3.0 reshape.152
  484.4 3.9 reduce_sum.45
  488.2 6.2 %multiply_reduce_fusion = bf16[128,2048]{1,0:T(8,128)(2,1)} fusion(f32[128,4,2048]{2,1,0:T(4,128)} %reshape.154, f32[128,4]{1,0:T(8,128)S(1)} %copy-done.10), kind=kLoop, calls=%fused_computation.8 | loop fusion | flops 1835008 | bytes 4720640 | tf_op jit(solution)/shard_map/reduce_sum | solution.py:120
  494.4 25.7 %reduce-scatter.3.cloned.1.call-done = bf16[256,1536]{1,0:T(8,128)(2,1)} async-done(((bf16[2048,1536]{1,0:T(8,128)(2,1)}), bf16[256,1536]{1,0:T(8,128)(2,1)}) %reduce-scatter.3.cloned.1.call-update) | async-done | bytes 786448 | tf_op jit(solution)/shard_map/reduce_scatter | solution.py:149
  521.5 4.3 subtract_convert_fusion
  (95 shorter events, 18.3 us)
Async XLA Ops:
  7.2 37.8 %copy-start = (bf16[128,2048]{1,0:T(8,128)(2,1)S(1)}, bf16[128,2048]{1,0:T(8,128)(2,1)}, u32[]{:S(2)}) copy-start(bf16[128,2048]{1,0:T(8,128)(2,1)} %param.13) | copy-start | bytes 1572868
  7.2 22.4 %copy-start.14 = (s32[16]{0:T(128)S(1)}, s32[16]{0:T(128)}, u32[]{:S(2)}) copy-start(s32[16]{0:T(128)} %param.16) | copy-start | bytes 196
  7.2 22.1 %copy-start.15 = (s32[128,4]{0,1:T(4,128)S(1)}, s32[128,4]{0,1:T(4,128)}, u32[]{:S(2)}) copy-start(s32[128,4]{0,1:T(4,128)} %param.14) | copy-start | bytes 6148
  7.2 173.5 %all-gather.3.cloned.1.call-start = ((), (), s32[]{:S(2)}) async-start(), calls=%async_computation.6 | async-start | bytes 7077888 | tf_op jit(solution)/shard_map/all_gather | solution.py:90
  7.2 21.0 %collective-permute-start = (bf16[1,2,256,768]{3,2,1,0:T(8,128)(2,1)}, bf16[1,2,256,768]{3,2,1,0:T(8,128)(2,1)S(1)}, u32[]{:S(2)}, u32[]{:S(2)}) collective-permute-start(bf16[1,2,256,768]{3,2,1,0:T(8,128)(2,1)} %param.17), channel_id=1, source_target_pairs={{64,0},{72,8},{80,16},{88,24},{96,32},{104,40},{112,48},{120,56},{... | collective-permute-start | bytes 2359304 | tf_op jit(solution)/shard_map/ppermute | solution.py:17
  40.6 8.7 %copy-start.11 = (s32[128,4]{1,0:T(8,128)}, s32[128,4]{1,0:T(8,128)S(1)}, u32[]{:S(2)}) copy-start(s32[128,4]{1,0:T(8,128)S(1)} %copy.31) | copy-start | bytes 6148
  52.6 7.5 %copy-start.16 = (f32[128,4]{0,1:T(4,128)S(1)}, f32[128,4]{0,1:T(4,128)}, u32[]{:S(2)}) copy-start(f32[128,4]{0,1:T(4,128)} %param.15) | copy-start | bytes 6148
  52.6 7.8 %copy-start.12 = (bf16[128,2048]{1,0:T(8,128)(2,1)S(1)}, bf16[128,2048]{1,0:T(8,128)(2,1)}, u32[]{:S(2)}) copy-start(bf16[128,2048]{1,0:T(8,128)(2,1)} %param.23) | copy-start | bytes 1572868
  52.6 47.6 %all-to-all-start = ((bf16[16,48,2048]{2,1,0:T(8,128)(2,1)}), bf16[16,48,2048]{2,1,0:T(8,128)(2,1)}, u32[]{:S(2)}, u32[]{:S(2)}) async-start(bf16[16,48,2048]{2,1,0:T(8,128)(2,1)} %select_select_fusion.1), calls=%async_computation | async-start | bytes 6291456 | tf_op jit(solution)/shard_map/all_to_all | solution.py:100
  60.3 3.1 copy-start.9
  100.2 94.5 %all-to-all-start.2 = ((bf16[16,48,2048]{2,1,0:T(8,128)(2,1)}), bf16[16,48,2048]{2,1,0:T(8,128)(2,1)S(1)}, u32[]{:S(2)}, u32[]{:S(2)}) async-start(bf16[16,48,2048]{2,1,0:T(8,128)(2,1)} %select_select_fusion), calls=%async_computation.2 | async-start | bytes 6291456 | tf_op jit(solution)/shard_map/all_to_all | solution.py:127
  108.3 169.7 %reduce-scatter.5.cloned.1.call-start = ((), (), s32[]{:S(2)}) async-start(), calls=%async_computation.9 | async-start | bytes 3538944 | tf_op jit(solution)/shard_map/reduce_scatter | solution.py:149
  180.7 7.3 %copy-start.17 = (bf16[1,2,2048,768]{3,2,1,0:T(8,128)(2,1)S(1)}, bf16[1,2,2048,768]{3,2,1,0:T(8,128)(2,1)}, u32[]{:S(2)}) copy-start(bf16[1,2,2048,768]{3,2,1,0:T(8,128)(2,1)} %all-gather.3.cloned.1.call-done) | copy-start | bytes 18874372
  186.5 1.5 copy-start.20
  194.8 6.3 %copy-start.6 = (bf16[16,48,2048]{2,1,0:T(8,128)(2,1)}, bf16[16,48,2048]{2,1,0:T(8,128)(2,1)S(1)}, u32[]{:S(2)}) copy-start(bf16[16,48,2048]{2,1,0:T(8,128)(2,1)S(1)} %all-to-all-done.2) | copy-start | bytes 9437188
  201.1 1.1 copy-start.7
  201.1 4.4 copy-start.8
  201.1 5.5 %copy-start.13 = (bf16[1,768,256]{2,1,0:T(8,128)(2,1)S(1)}, bf16[1,768,256]{2,1,0:T(8,128)(2,1)}, u32[]{:S(2)}) copy-start(bf16[1,768,256]{2,1,0:T(8,128)(2,1)} %param.18) | copy-start | bytes 1179652
  201.1 142.8 %all-gather.5.cloned.1.call-start = ((), (), s32[]{:S(2)}) async-start(), calls=%async_computation.7 | async-start | bytes 3538944 | tf_op jit(solution)/shard_map/all_gather | solution.py:91
  202.5 11.5 %collective-permute-start.4 = (bf16[1,768,256]{1,2,0:T(8,128)(2,1)S(1)}, bf16[1,768,256]{1,2,0:T(8,128)(2,1)S(1)}, u32[]{:S(2)}, u32[]{:S(2)}) collective-permute-start(bf16[1,768,256]{1,2,0:T(8,128)(2,1)S(1)} %convert_element_type.105), channel_id=1, source_target_pairs={{64,0},{72,8},{80,16},{88,24},{96,32},{104,40},{112,48},{120,56},{... | collective-permute-start | bytes 1179656 | tf_op jit(solution)/shard_map/ppermute | solution.py:17
  206.5 15.8 %collective-permute-start.5 = (bf16[1,768,256]{1,2,0:T(8,128)(2,1)}, bf16[1,768,256]{1,2,0:T(8,128)(2,1)S(1)}, u32[]{:S(2)}, u32[]{:S(2)}) collective-permute-start(bf16[1,768,256]{1,2,0:T(8,128)(2,1)} %convert_element_type.108), channel_id=1, source_target_pairs={{64,0},{72,8},{80,16},{88,24},{96,32},{104,40},{112,48},{120,56},{... | collective-permute-start | bytes 1179656 | tf_op jit(solution)/shard_map/ppermute | solution.py:17
  206.8 24.0 %collective-permute-start.1 = (bf16[1,768,256]{1,2,0:T(8,128)(2,1)S(1)}, bf16[1,768,256]{1,2,0:T(8,128)(2,1)S(1)}, u32[]{:S(2)}, u32[]{:S(2)}) collective-permute-start(bf16[1,768,256]{1,2,0:T(8,128)(2,1)S(1)} %copy.36), channel_id=1, source_target_pairs={{64,0},{72,8},{80,16},{88,24},{96,32},{104,40},{112,48},{120,56},{... | collective-permute-start | bytes 1179656 | tf_op jit(solution)/shard_map/ppermute | solution.py:17
  280.8 239.3 %reduce-scatter.3.cloned.1.call-start = ((), (), s32[]{:S(2)}) async-start(), calls=%async_computation.8 | async-start | bytes 7077888 | tf_op jit(solution)/shard_map/reduce_scatter | solution.py:149
  351.5 1.0 copy-start.19
  351.5 1.4 copy-start.21
  362.6 1.9 copy-start.18
  369.9 46.1 %all-to-all-start.1 = ((bf16[16,48,2048]{2,1,0:T(8,128)(2,1)}), bf16[16,48,2048]{2,1,0:T(8,128)(2,1)S(1)}, u32[]{:S(2)}, u32[]{:S(2)}) async-start(bf16[16,48,2048]{2,1,0:T(8,128)(2,1)} %bitcast.128), calls=%async_computation.1 | async-start | bytes 6291456 | tf_op jit(solution)/shard_map/all_to_all | solution.py:110
  375.6 5.0 copy-start.22
  415.9 47.8 %all-to-all-start.3 = ((bf16[16,48,2048]{2,1,0:T(8,128)(2,1)}), bf16[16,48,2048]{2,1,0:T(8,128)(2,1)}, u32[]{:S(2)}, u32[]{:S(2)}) async-start(bf16[16,48,2048]{2,1,0:T(8,128)(2,1)} %bitcast.127), calls=%async_computation.3 | async-start | bytes 6291456 | tf_op jit(solution)/shard_map/all_to_all | solution.py:136
  423.6 5.4 %copy-start.5 = (f32[1,2,256,768]{3,2,1,0:T(8,128)S(1)}, f32[1,2,256,768]{3,2,1,0:T(8,128)}, u32[]{:S(2)}) copy-start(f32[1,2,256,768]{3,2,1,0:T(8,128)} %param.20) | copy-start | bytes 4718596
  426.1 95.3 %collective-permute-start.2 = (bf16[1,2,256,768]{3,2,1,0:T(8,128)(2,1)}, bf16[1,2,256,768]{3,2,1,0:T(8,128)(2,1)}, u32[]{:S(2)}, u32[]{:S(2)}) collective-permute-start(bf16[1,2,256,768]{3,2,1,0:T(8,128)(2,1)} %convert_element_type.98), channel_id=1, source_target_pairs={{64,0},{72,8},{80,16},{88,24},{96,32},{104,40},{112,48},{120,56},{... | collective-permute-start | bytes 2359304 | tf_op jit(solution)/shard_map/ppermute | solution.py:17
  430.0 91.4 %collective-permute-start.3 = (bf16[1,2,256,768]{3,2,1,0:T(8,128)(2,1)}, bf16[1,2,256,768]{3,2,1,0:T(8,128)(2,1)}, u32[]{:S(2)}, u32[]{:S(2)}) collective-permute-start(bf16[1,2,256,768]{3,2,1,0:T(8,128)(2,1)} %convert_element_type.101), channel_id=1, source_target_pairs={{64,0},{72,8},{80,16},{88,24},{96,32},{104,40},{112,48},{120,56},{... | collective-permute-start | bytes 2359304 | tf_op jit(solution)/shard_map/ppermute | solution.py:17
  463.7 7.7 %copy-start.2 = (bf16[512,2048]{1,0:T(8,128)(2,1)S(1)}, bf16[512,2048]{1,0:T(8,128)(2,1)}, u32[]{:S(2)}) copy-start(bf16[512,2048]{1,0:T(8,128)(2,1)} %gather_fusion.2) | copy-start | bytes 6291460
  484.4 3.9 copy-start.10
  494.4 27.0 %copy-start.3 = (bf16[1,2,256,768]{3,2,1,0:T(8,128)(2,1)S(1)}, bf16[1,2,256,768]{3,2,1,0:T(8,128)(2,1)}, u32[]{:S(2)}) copy-start(bf16[1,2,256,768]{3,2,1,0:T(8,128)(2,1)} %broadcast_select_fusion.1) | copy-start | bytes 2359300
  494.4 27.0 %copy-start.4 = (f32[1,2,256,768]{3,2,1,0:T(8,128)S(1)}, f32[1,2,256,768]{3,2,1,0:T(8,128)}, u32[]{:S(2)}) copy-start(f32[1,2,256,768]{3,2,1,0:T(8,128)} %param.19) | copy-start | bytes 4718596
  521.5 4.3 copy-start.1
Sparse Core Ops, SparseCore 0:
  29.4 151.2 all-gather.2
  201.2 76.7 reduce-scatter.4
  281.1 62.6 all-gather.4
  362.7 157.3 reduce-scatter.2
